TPU v7x, 256 devices: a whole 4x4x8 slice. The times are simulated.
256 devices in a mesh: dp: 16 (over y, z_hi), mp: 16 (over x, z_lo, core).
Axes of the slice: x: 4, y: 4, z: 8 (z_hi: 4, z_lo: 2; z = z_hi * 2 + z_lo), core: 2. Of those that a mesh axis runs over, the one named last changes fastest.
Arguments:
- inputs: bfloat16 [16, 512, 4096], P('dp', None, 'mp'), may hold values from -6 to 6
- out_grads: bfloat16 [16, 512, 4096], P('dp', None, 'mp'), may hold values from -6 to 6
- gate_weight: bfloat16 [4096, 14336], P('dp', 'mp'), may hold values from -0.09375 to 0.09375
- down_weight: bfloat16 [14336, 4096], P('mp', 'dp'), may hold values from -0.046875 to 0.046875
- in_proj: bfloat16 [4096, 64], replicated, may hold values from -0.09375 to 0.09375
- out_proj: bfloat16 [14336, 64], P('mp'), may hold values from -0.046875 to 0.046875
- in_precond: float32 [64, 64], replicated, may hold values from -0.75 to 0.75
- out_precond: float32 [64, 64], replicated, may hold values from -0.75 to 0.75
- queries: bfloat16 [2048, 4096], P('dp', 'mp'), may hold values from -48 to 48
- languages: int32 [2048], P('dp'), may hold values from 0 to 31, as said below
Outputs:
- influence: float32 [16, 32], P('dp')
Inputs may be any that keep to these rules, and one draw needn't show every extreme that they name: Each of the 32 languages labels exactly 64 queries.
All inputs are finite; a program needn't handle non-finite values.
Results may differ from a plain program's by a relative error of at most 0.0042.
Values may be sent and summed in bfloat16 or wider, within the bound.
No kernel may reach another device: no remote copies, remote signals or barrier semaphores. Data moves between devices by JAX's collectives and lax.ppermute only.
A program may use at most 128 MiB of HBM per device.

v0:
```python
import jax
import jax.numpy as jnp
from jax import lax
from jax.sharding import PartitionSpec as P

LANGS = 32


def shards(
    inputs,
    out_grads,
    gate_weight,
    down_weight,
    in_proj,
    out_proj,
    in_precond,
    out_precond,
    queries,
    languages,
):
    examples = inputs.shape[0]
    seq_len = inputs.shape[1]
    rows_full, grads_full = (
        lax.all_gather(inputs, "mp", axis=2, tiled=True),
        lax.all_gather(out_grads, "mp", axis=2, tiled=True),
    )
    tok_rows = rows_full.reshape(examples * seq_len, rows_full.shape[2])
    tok_grads = grads_full.reshape(examples * seq_len, grads_full.shape[2])
    columns = tok_rows
    gate = jnp.dot(
        columns,
        lax.all_gather(gate_weight, "dp", axis=0, tiled=True),
        preferred_element_type=jnp.float32,
    )
    columns = tok_grads
    hidden_grad = lax.dot_general(
        columns,
        lax.all_gather(down_weight, "dp", axis=1, tiled=True),
        (((1,), (1,)), ((), ())),
        preferred_element_type=jnp.float32,
    )
    up_grad = (hidden_grad * jax.nn.silu(gate)).astype(jnp.bfloat16)
    rank = in_proj.shape[1]
    band = rank // lax.axis_size("mp")
    in_factor = jnp.dot(
        jnp.dot(tok_rows, in_proj, preferred_element_type=jnp.float32),
        in_precond.T,
        precision=lax.Precision.HIGHEST,
    )
    in_three = in_factor.reshape(examples, seq_len, rank)
    out_part = jnp.dot(up_grad, out_proj, preferred_element_type=jnp.float32)
    out_sum = lax.psum(out_part, "mp")
    out_factor = jnp.dot(out_sum, out_precond, precision=lax.Precision.HIGHEST)
    full = (
        jnp.einsum(
            "esi,esj->eij",
            in_three,
            out_factor.reshape(examples, seq_len, rank),
            precision=lax.Precision.HIGHEST,
        )
        / seq_len
    )
    own_block = lax.dynamic_slice_in_dim(full, lax.axis_index("mp") * band, band, 1)
    projected = own_block.reshape(examples, band * rank).astype(jnp.bfloat16)
    per_language = languages.shape[0] * lax.axis_size("dp") // LANGS
    lang_ids = jnp.arange(LANGS, dtype=jnp.int32)
    query_piece = lax.all_gather(queries, "dp", axis=0, tiled=True)
    label_piece = lax.all_gather(languages, "dp", axis=0, tiled=True)
    block_scores = lax.dot_general(
        projected, query_piece, (((1,), (1,)), ((), ())), preferred_element_type=jnp.float32
    )
    onehot = (label_piece[:, None] == lang_ids[None, :]).astype(jnp.float32)
    partial_sums = jnp.dot(block_scores, onehot, precision=lax.Precision.HIGHEST)
    totals = lax.psum(partial_sums, "mp")
    return totals / per_language


def solution(mesh):
    return jax.shard_map(
        shards,
        mesh=mesh,
        in_specs=(
            P("dp", None, "mp"),
            P("dp", None, "mp"),
            P("dp", "mp"),
            P("mp", "dp"),
            P(),
            P("mp", None),
            P(),
            P(),
            P("dp", "mp"),
            P("dp"),
        ),
        out_specs=P("dp", None),
        check_vma=False,
    )
```

profile of v0, /device:TPU:1, one launch (start us, length us, event | category | flops | bytes accessed | tf_op | source)
XLA Modules:
  0.0 558.4 jit_solution(12647882360686652842)
XLA Ops:
  6.5 0.0 copy-start
  6.5 0.0 all-gather.7.cloned.1.call-start
  6.5 0.7 all-gather.7.cloned.1.call-update
  7.3 0.0 all-gather.13.cloned.1.call-start
  7.3 0.7 all-gather.13.cloned.1.call-update
  8.0 0.0 all-gather.9.cloned.1.call-start
  8.1 0.7 all-gather.9.cloned.1.call-update
  8.7 0.0 all-gather.11.cloned.1.call-start
  8.8 0.5 all-gather.11.cloned.1.call-update
  9.3 0.0 copy-start.4
  9.3 0.0 all-reduce.2.cloned.1.call-start
  9.4 52.4 %all-gather.7.cloned.1.call-done = bf16[1,512,4096]{2,1,0:T(8,128)(2,1)} async-done(((bf16[1,512,256]{2,1,0:T(8,128)(2,1)}), bf16[1,512,4096]{2,1,0:T(8,128)(2,1)}) %all-gather.7.cloned.1.call-update) | async-done | bytes 4194320 | tf_op jit(solution)/shard_map/all_gather | solution.py:24
  61.8 96.9 %all-gather.13.cloned.1.call-done = bf16[4096,896]{1,0:T(8,128)(2,1)} async-done(((bf16[256,896]{1,0:T(8,128)(2,1)}), bf16[4096,896]{1,0:T(8,128)(2,1)}) %all-gather.13.cloned.1.call-update) | async-done | bytes 7340048 | tf_op jit(solution)/shard_map/all_gather | solution.py:32
  158.7 10.1 %fusion.2 = f32[512,896]{1,0:T(8,128)S(1)} fusion(bf16[4096,896]{1,0:T(8,128)(2,1)} %all-gather.13.cloned.1.call-done, bf16[1,512,4096]{2,1,0:T(8,128)(2,1)} %all-gather.7.cloned.1.call-done), kind=kOutput, calls=%fused_computation.2 | convolution fusion | flops 3758096384 | bytes 13369344 | tf_op jit(solution)/shard_map/dot_general | solution.py:30
  168.8 0.0 copy-start.3
  168.8 50.9 %all-gather.9.cloned.1.call-done = bf16[1,512,4096]{2,1,0:T(8,128)(2,1)} async-done(((bf16[1,512,256]{2,1,0:T(8,128)(2,1)}), bf16[1,512,4096]{2,1,0:T(8,128)(2,1)}) %all-gather.9.cloned.1.call-update) | async-done | bytes 4194320 | tf_op jit(solution)/shard_map/all_gather | solution.py:25
  219.7 115.6 %all-gather.11.cloned.1.call-done = bf16[896,4096]{1,0:T(8,128)(2,1)} async-done(((bf16[896,256]{1,0:T(8,128)(2,1)}), bf16[896,4096]{1,0:T(8,128)(2,1)}) %all-gather.11.cloned.1.call-update) | async-done | bytes 7340048 | tf_op jit(solution)/shard_map/all_gather | solution.py:38
  335.3 0.0 copy-done.4
  335.3 9.9 %fusion.9 = f32[512,64]{1,0:T(8,128)} fusion(bf16[896,64]{0,1:T(8,128)(2,1)S(1)} %copy-done.4, f32[512,896]{1,0:T(8,128)S(1)} %fusion.2, bf16[896,4096]{1,0:T(8,128)(2,1)} %all-gather.11.cloned.1.call-done, bf16[1,512,4096]{2,1,0:T(8,128)(2,1)} %all-gather.9.cloned.1.call-done), kind=kOutput, calls=%fused_computation.8 | convolution fusion | flops 3819569152 | bytes 13615104 | tf_op jit(solution)/shard_map/dot_general | solution.py:51
  345.2 0.0 copy-start.1
  345.2 0.0 copy-start.2
  345.2 0.0 all-reduce.2.cloned.1.call-update
  345.3 0.0 all-gather.15.cloned.1.call-start
  345.3 0.5 all-gather.15.cloned.1.call-update
  345.8 0.0 copy-done.3
  345.9 34.9 %all-gather = s32[16,1,128]{2,1,0:T(1,128)S(1)} all-gather(s32[1,1,128]{2,1,0:T(1,128)S(1)} %bitcast.32), channel_id=1, replica_groups=mesh['dp'=16,'mp'=16] {'dp'}, dimensions={0}, use_global_device_ids=true | all-gather | bytes 8704 | tf_op jit(solution)/shard_map/all_gather | solution.py:68
  380.7 0.0 copy-done
  380.7 3.4 fusion.4
  384.2 0.0 copy-done.1
  384.2 0.4 fusion.16
  384.5 80.6 %all-reduce.2.cloned.1.call-done = f32[512,64]{1,0:T(8,128)} async-done(((f32[512,64]{1,0:T(8,128)}), f32[512,64]{1,0:T(8,128)}) %all-reduce.2.cloned.1.call-update) | async-done | bytes 131088 | tf_op jit(solution)/shard_map/psum | solution.py:52
  465.1 0.0 copy-done.2
  465.1 1.3 fusion.17
  466.4 0.6 fusion.18
  467.1 0.1 reshape.32
  467.1 53.2 %all-gather.15.cloned.1.call-done = bf16[2048,256]{1,0:T(8,128)(2,1)} async-done(((bf16[128,256]{1,0:T(8,128)(2,1)}), bf16[2048,256]{1,0:T(8,128)(2,1)}) %all-gather.15.cloned.1.call-update) | async-done | bytes 1048592 | tf_op jit(solution)/shard_map/all_gather | solution.py:67
  520.4 1.6 convolution_bitcast_fusion
  522.0 0.6 fusion.11
  522.5 28.5 %psum.15 = f32[1,32]{1,0:T(1,128)S(1)} all-reduce(f32[1,32]{1,0:T(1,128)S(1)} %fusion.11), channel_id=1, replica_groups=mesh['dp'=16,'mp'=16] {'mp'}, use_global_device_ids=true, to_apply=%region_1.2 | all-reduce | flops 32 | bytes 256 | tf_op jit(solution)/shard_map/psum | solution.py:74
  551.0 0.5 broadcast_multiply_fusion
  (1 shorter events, 0.0 us)
Async XLA Ops:
  6.5 374.2 %copy-start = (bf16[4096,64]{0,1:T(8,128)(2,1)S(1)}, bf16[4096,64]{0,1:T(8,128)(2,1)}, u32[]{:S(2)}) copy-start(bf16[4096,64]{0,1:T(8,128)(2,1)} %param.14) | copy-start | bytes 1572868
  6.5 55.3 %all-gather.7.cloned.1.call-start = ((), (), s32[]{:S(2)}) async-start(), calls=%async_computation | async-start | bytes 4456448 | tf_op jit(solution)/shard_map/all_gather | solution.py:24
  7.3 151.4 %all-gather.13.cloned.1.call-start = ((), (), s32[]{:S(2)}) async-start(), calls=%async_computation.3 | async-start | bytes 7798784 | tf_op jit(solution)/shard_map/all_gather | solution.py:32
  8.0 211.7 %all-gather.9.cloned.1.call-start = ((), (), s32[]{:S(2)}) async-start(), calls=%async_computation.1 | async-start | bytes 4456448 | tf_op jit(solution)/shard_map/all_gather | solution.py:25
  8.7 326.6 %all-gather.11.cloned.1.call-start = ((), (), s32[]{:S(2)}) async-start(), calls=%async_computation.2 | async-start | bytes 7798784 | tf_op jit(solution)/shard_map/all_gather | solution.py:38
  9.3 326.0 %copy-start.4 = (bf16[896,64]{0,1:T(8,128)(2,1)S(1)}, bf16[896,64]{0,1:T(8,128)(2,1)}, u32[]{:S(2)}) copy-start(bf16[896,64]{0,1:T(8,128)(2,1)} %param.15) | copy-start | bytes 344068
  9.3 455.8 %all-reduce.2.cloned.1.call-start = ((), (), s32[]{:S(2)}) async-start(), calls=%async_computation.4 | async-start | bytes 524288 | tf_op jit(solution)/shard_map/psum | solution.py:52
  168.8 177.1 %copy-start.3 = (s32[128]{0:T(128)S(1)}, s32[128]{0:T(128)}, u32[]{:S(2)}) copy-start(s32[128]{0:T(128)} %param.19) | copy-start | bytes 1540
  345.2 38.9 %copy-start.1 = (f32[64,64]{1,0:T(8,128)S(1)}, f32[64,64]{1,0:T(8,128)}, u32[]{:S(2)}) copy-start(f32[64,64]{1,0:T(8,128)} %param.16) | copy-start | bytes 49156
  345.2 119.9 %copy-start.2 = (f32[64,64]{1,0:T(8,128)S(1)}, f32[64,64]{1,0:T(8,128)}, u32[]{:S(2)}) copy-start(f32[64,64]{1,0:T(8,128)} %param.17) | copy-start | bytes 49156
  345.3 175.1 %all-gather.15.cloned.1.call-start = ((), (), s32[]{:S(2)}) async-start(), calls=%async_computation.5 | async-start | bytes 1114112 | tf_op jit(solution)/shard_map/all_gather | solution.py:67
Sparse Core Ops, SparseCore 0:
  9.1 52.6 all-gather.6
  64.3 94.3 all-gather.12
  160.5 59.2 all-gather.8
  222.0 113.2 all-gather.10
  345.4 119.6 all-reduce.1
  467.7 52.6 all-gather.14
where the time goes:
time: 559 us; the launch traced here: 558 us
  waiting for transfers between devices  453 us (81%)
  blocking collectives  63.3 us (11%)
  matrix products  27.9 us (5%)
  between operations  13.6 us (2%)
    all_gather x1, waiting for transfers between devices, shards(): lax.all_gather(down_weight, 'dp', axis=1, tiled=True)  116 us
    all_gather x1, waiting for transfers between devices, shards(): lax.all_gather(gate_weight, 'dp', axis=0, tiled=True)  96.9 us
    psum x1, waiting for transfers between devices, shards(): out_sum = lax.psum(out_part, 'mp')  80.6 us
    all_gather x1, waiting for transfers between devices, shards(): query_piece = lax.all_gather(queries, 'dp', axis=0, tiled=True)  53.2 us
    all_gather x1, waiting for transfers between devices, shards(): lax.all_gather(inputs, 'mp', axis=2, tiled=True)  52.4 us
    all_gather x1, waiting for transfers between devices, shards(): lax.all_gather(out_grads, 'mp', axis=2, tiled=True)  50.9 us
    all_gather x1, blocking collectives, shards(): label_piece = lax.all_gather(languages, 'dp', axis=0, tiled=True)  34.9 us
    psum x1, blocking collectives, shards(): totals = lax.psum(partial_sums, 'mp')  28.5 us
  transfers between devices with their start and end apart: 6, of which 6 were waited for; matrix products, arithmetic and copies ran while one was open for 3% of the time, Pallas kernels for 0%

commit v1 on v0

v1 whole, which is shorter than its diff:
```python
import jax
import jax.numpy as jnp
from jax import lax
from jax.experimental import pallas as pl
from jax.experimental.pallas import tpu as pltpu
from jax.sharding import PartitionSpec as P

LANGS = 32
AXES = ("dp", "mp")
HIGH = lax.Precision.HIGHEST
F32 = jnp.float32


def flat(x, y, z, c):
    x, y, z = x % 4, y % 4, z % 8
    return (y * 4 + (z >> 1)) * 16 + x * 4 + (z & 1) * 2 + c


def perm_of(move):
    pairs = []
    for d in range(16):
        for m in range(16):
            place = (m >> 2, d >> 2, ((d & 3) << 1) | ((m >> 1) & 1), m & 1)
            there = move(*place)
            if there is not None:
                pairs.append((flat(*place), flat(*there)))
    return pairs


def send(v, move):
    return lax.ppermute(v, AXES, perm_of(move))


def ring(v, axis, ready=()):
    plus = (lambda x, y, z, c: (x + 1, y, z, c)) if axis == "x" else (lambda x, y, z, c: (x, y + 1, z, c))
    minus = (lambda x, y, z, c: (x - 1, y, z, c)) if axis == "x" else (lambda x, y, z, c: (x, y - 1, z, c))
    v, *ready = lax.optimization_barrier((v, *ready))
    half = v.shape[0] // 2
    before = send(v, plus)
    after = send(v, minus)
    low = send(before[:half], plus)
    high = send(after[half:], minus)
    return [v, before, after, low, high], ready


def weight_a(x, y, z, c):
    return (x, y, z + 4, c) if c == (z >> 1) & 1 else (x, y, z + 2, 1 - c)


def weight_b(x, y, z, c):
    return (x, y, z, c) if c == (z >> 1) & 1 else (x, y, z - 2, 1 - c)


def coords():
    d, m = lax.axis_index("dp"), lax.axis_index("mp")
    y, zhh, zhl = d // 4, (d // 2) % 2, d % 2
    x, zl, c = m // 4, (m // 2) % 2, m % 2
    return x, y, zhh, zhl, zl, c


def source_bit(zhh, zhl, c):
    same = (c + zhl + 1) % 2
    stays = (1 - same) * zhl
    return (zhh + 1 - stays) % 2


def matmul_kernel(gate, *refs):
    own, near, far, ws = refs[:5], refs[5:10], refs[10:15], refs[15:20]
    refs = refs[20:]
    if gate:
        _, proj, out, pout, xv, wv, xsem, wsem = refs
    else:
        out, xv, wv, xsem, wsem = refs
    x, y, zhh, zhl, zl, c = coords()
    bit = source_bit(zhh, zhl, c)
    base = 0 if gate else 512
    copies = []
    for s in range(4):
        row = ((s // 2 + c) % 2) * 512
        low = (zl + s % 2) % 2
        for n, step in enumerate((0, 3, 1, 2)):
            col = (((x + step) % 4) * 2 + low) * 256
            dst = xv.at[pl.ds(pl.multiple_of(row, 512), 512), pl.ds(pl.multiple_of(col, 256), 256)]
            if s < 2:
                group = (own, near)[s]
                src = group[3 + (0 if gate else 1)] if step == 2 else group[n].at[pl.ds(base, 512), :]
            elif step == 2:
                src = far[3 + s - 2].at[0, pl.ds(base, 512), :]
            else:
                src = far[n].at[s - 2, pl.ds(base, 512), :]
            copies.append(pltpu.make_async_copy(src, dst, xsem.at[s * 4 + n]))
    for r in range(2):
        h = bit if r == 0 else 1 - bit
        for n, step in enumerate((0, 3, 1, 2)):
            at = pl.ds(pl.multiple_of((((y + step) % 4) * 2 + h) * 256, 256), 256)
            dst = wv.at[at, :] if gate else wv.at[:, at]
            src = ws[3 + r].at[0] if step == 2 else ws[n].at[r]
            copies.append(pltpu.make_async_copy(src, dst, wsem.at[r * 4 + n]))
    for copy in copies:
        copy.start()
    for copy in copies:
        copy.wait()

    @pl.loop(0, 4)
    def _(i):
        at = pl.ds(pl.multiple_of(i * 256, 256), 256)
        rows = xv[at, :]
        if gate:
            out[at, :] = jnp.dot(rows, wv[...], preferred_element_type=F32)
            pout[at, :] = jnp.dot(rows, proj[...], preferred_element_type=F32)
        else:
            out[at, :] = lax.dot_general(rows, wv[...], (((1,), (1,)), ((), ())), preferred_element_type=F32)


def matmul(gate, blocks, *more):
    hbm = pl.BlockSpec(memory_space=pl.ANY)
    vmem = pl.BlockSpec(memory_space=pltpu.VMEM)
    shapes = [jax.ShapeDtypeStruct((1024, 896), F32)]
    if gate:
        shapes += [jax.ShapeDtypeStruct((1024, 64), F32)]
    wshape = (2048, 896) if gate else (896, 2048)
    return pl.pallas_call(
        lambda *refs: matmul_kernel(gate, *refs),
        out_shape=shapes,
        in_specs=[hbm] * 20 + ([hbm, vmem] if gate else []),
        out_specs=[vmem] * len(shapes),
        scratch_shapes=[
            pltpu.VMEM((1024, 2048), jnp.bfloat16),
            pltpu.VMEM(wshape, jnp.bfloat16),
            pltpu.SemaphoreType.DMA((16,)),
            pltpu.SemaphoreType.DMA((8,)),
        ],
        compiler_params=pltpu.CompilerParams(vmem_limit_bytes=48 << 20),
        cost_estimate=pl.CostEstimate(flops=2 * 1024 * 2048 * 960, bytes_accessed=12 << 20, transcendentals=0),
    )(*blocks, *more)


def everyone(v, axis):
    return lax.all_to_all(jnp.broadcast_to(v[None], (16,) + v.shape), axis, 0, 0, tiled=True)


def shards(inputs, out_grads, gate_weight, down_weight, in_proj, out_proj, in_precond, out_precond, queries, languages):
    x, y, zhh, zhl, zl, c = coords()
    swap = lambda x, y, z, c: (x, y, z, 1 - c)

    with jax.named_scope("language_sums"):
        onehot = (languages[None, :] == jnp.arange(LANGS, dtype=jnp.int32)[:, None]).astype(jnp.bfloat16)
        mine = jnp.dot(onehot, queries, preferred_element_type=F32)
        feature_block = jnp.sum(everyone(mine, "dp").reshape(16, LANGS, 256), axis=0)
        by_language = everyone(feature_block, "mp").reshape(16, LANGS, 256)

    with jax.named_scope("along_z"):
        both = jnp.concatenate([inputs[0], out_grads[0]], axis=0)
        turn = lambda v, k: send(v, lambda x, y, z, c: (x, y, z ^ k, c))
        ga = send(gate_weight, weight_a)
        gb = send(gate_weight, weight_b)
        both1, ga = lax.optimization_barrier((both, ga))
        near = turn(both1, 1)
        both2, gb = lax.optimization_barrier((both, gb))
        far2 = turn(both2, 2)
        both3, near = lax.optimization_barrier((both, near))
        far3 = turn(both3, 3)
        down2, far2 = lax.optimization_barrier((down_weight, far2))
        da = send(down2, weight_a)
        down3, far3 = lax.optimization_barrier((down_weight, far3))
        db = send(down3, weight_b)
    with jax.named_scope("along_x"):
        own_ring, _ = ring(both, "x")
        near_ring, own_ring[1:3] = ring(near, "x", own_ring[1:3])
        far_ring, near_ring[1:3] = ring(jnp.stack([far2, far3]), "x", near_ring[1:3])
    with jax.named_scope("along_y"):
        gate_ring, _ = ring(jnp.stack([ga, gb]), "y")
        down_ring, gate_ring[1:3] = ring(jnp.stack([da, db]), "y", gate_ring[1:3])
    tokens = own_ring + near_ring + far_ring

    proj_half = lax.dynamic_index_in_dim(in_proj.reshape(8, 2, 256, 64), c, 1, keepdims=False).reshape(2048, 64)
    out_mine = jnp.where(c == zhl, out_proj, send(out_proj, swap))

    gate, in_sum = matmul(True, tokens + gate_ring, by_language, proj_half)
    gate = gate[:512] + send(gate[512:], swap)
    in_sum = in_sum[:512] + send(in_sum[512:], swap)
    (hidden_grad,) = matmul(False, tokens + down_ring)
    hidden_grad = hidden_grad[:512] + send(hidden_grad[512:], swap)

    with jax.named_scope("finish"):
        up_grad = (hidden_grad * jax.nn.silu(gate)).astype(jnp.bfloat16)
        out_part = jnp.dot(up_grad, out_mine, preferred_element_type=F32)
        outer = lax.dot_general(in_sum, out_part, (((0,), (0,)), ((), ())), precision=HIGH)
        outer = send(outer, lambda x, y, z, c: (x, y, z ^ 2, c) if c else (x, y, z, c))
        total = jnp.sum(everyone(outer, "mp").reshape(16, 64, 64), axis=0)
        full = jnp.dot(jnp.dot(in_precond, total, precision=HIGH), out_precond, precision=HIGH) / 512
        projected = full.astype(jnp.bfloat16).astype(F32)
        by_language = by_language.transpose(1, 0, 2).reshape(LANGS, 64, 64)
        scores = jnp.sum(projected[None] * by_language, axis=(1, 2))
    return (scores / 64).reshape(1, LANGS)


def solution(mesh):
    return jax.shard_map(
        shards,
        mesh=mesh,
        in_specs=(
            P("dp", None, "mp"),
            P("dp", None, "mp"),
            P("dp", "mp"),
            P("mp", "dp"),
            P(),
            P("mp", None),
            P(),
            P(),
            P("dp", "mp"),
            P("dp"),
        ),
        out_specs=P("dp", None),
        check_vma=False,
    )
```

time: 559 us -> 239 us (0.43)
  waiting for transfers between devices: 453 us -> 74.2 us
  starting transfers between devices: 0.2 us -> 86.4 us
  blocking collectives: 63.3 us -> 10.3 us
  local copies, waits for them, and re-layouts: 0.11 us -> 29.2 us
  matrix products: 27.9 us -> 4.99 us
  Pallas kernels: 0 us -> 21.9 us
  between operations: 13.6 us -> 0.33 us
  other arithmetic: 0.53 us -> 10.5 us
    all_gather x5 -> x0, waiting for transfers between devices: 369 us -> none  [the longest x1 116 us: shards(): lax.all_gather(down_weight, 'dp', axis=1, tiled=True)]
    psum x1 -> x0, waiting for transfers between devices: 80.6 us -> none  [shards(): out_sum = lax.psum(out_part, 'mp')]
    ppermute x0 -> x32, waiting for transfers between devices: none -> 74.2 us  [send(): return lax.ppermute(v, AXES, perm_of(move))]
    ppermute x0 -> x32, starting transfers between devices: none -> 67.6 us  [send(): return lax.ppermute(v, AXES, perm_of(move))]
    all_gather x1 -> x0, blocking collectives: 34.9 us -> none  [shards(): label_piece = lax.all_gather(languages, 'dp', axis=0, tiled=True)]
    psum x1 -> x0, blocking collectives: 28.5 us -> none  [shards(): totals = lax.psum(partial_sums, 'mp')]
    dot_general x8 -> x5, matrix products: 27.9 us -> 4.99 us  [the longest x1 3.81 us: shards(): out_part = jnp.dot(up_grad, out_mine, preferred_element_type=F32)]
    pallas_call x0 -> x2, Pallas kernels: none -> 21.9 us  [matmul(): pl.pallas_call(lambda *refs: matmul_kernel(gate, *refs), out_shape=shapes...]
  transfers between devices with their start and end apart: 6 -> 34, of which waited for: 6 -> 10; matrix products, arithmetic and copies ran while one was open for 3% -> 15% of each run, Pallas kernels for 0% -> 9%
where the time goes in v1:
time: 239 us; the launch traced here: 238 us
  starting transfers between devices  86.4 us (36%)
  waiting for transfers between devices  74.2 us (31%)
  local copies, waits for them, and re-layouts  29.2 us (12%)
  Pallas kernels  21.9 us (9%)
  other arithmetic  10.5 us (4%)
  blocking collectives  10.3 us (4%)
  matrix products  4.99 us (2%)
    ppermute x32, waiting for transfers between devices, send(): return lax.ppermute(v, AXES, perm_of(move))  74.2 us
    ppermute x32, starting transfers between devices, send(): return lax.ppermute(v, AXES, perm_of(move))  67.6 us
    pallas_call x2, Pallas kernels, matmul(): pl.pallas_call(lambda *refs: matmul_kernel(gate, *refs), out_shape=shapes...  21.9 us
    all_to_all x2, starting transfers between devices, everyone(): lax.all_to_all(jnp.broadcast_to(v[None], (16,) + v.shape), axis, 0, 0, ti...  18.8 us
    all_to_all x1, blocking collectives, everyone(): lax.all_to_all(jnp.broadcast_to(v[None], (16,) + v.shape), axis, 0, 0, ti...  10.3 us
    slice x5, local copies, waits for them, and re-layouts, ring(): low = send(before[:half], plus)  6.29 us
    slice x5, local copies, waits for them, and re-layouts, ring(): high = send(after[half:], minus)  6.29 us
    unnamed x31, local copies, waits for them, and re-layouts  5.91 us
  transfers between devices with their start and end apart: 34, of which 10 were waited for; matrix products, arithmetic and copies ran while one was open for 15% of the time, Pallas kernels for 9%

profile of v1, /device:TPU:1, one launch (start us, length us, event | category | flops | bytes accessed | tf_op | source)
XLA Modules:
  0.0 237.7 jit_solution(15628667219489984214)
XLA Ops:
  0.0 4.4 %collective-permute-start = (bf16[256,896]{1,0:T(8,128)(2,1)}, bf16[256,896]{1,0:T(8,128)(2,1)S(1)}, u32[]{:S(2)}, u32[]{:S(2)}) collective-permute-start(bf16[256,896]{1,0:T(8,128)(2,1)} %param.12), channel_id=1, source_target_pairs={{0,32},{1,16},{2,34},{3,18},{4,36},{5,20},{6,38},{7,22},{8,40},{9,... | collective-permute-start | bytes 1376264 | tf_op jit(solution)/shard_map/along_z/ppermute | solution.py:31
  4.4 5.1 %collective-permute-start.6 = (bf16[256,896]{1,0:T(8,128)(2,1)}, bf16[256,896]{1,0:T(8,128)(2,1)S(1)}, u32[]{:S(2)}, u32[]{:S(2)}) collective-permute-start(bf16[256,896]{1,0:T(8,128)(2,1)} %param.12), channel_id=1, source_target_pairs={{0,0},{1,48},{2,2},{3,50},{4,4},{5,52},{6,6},{7,54},{8,8},{9,56},{... | collective-permute-start | bytes 1376264 | tf_op jit(solution)/shard_map/along_z/ppermute | solution.py:31
  9.5 1.1 pad_maximum_fusion.3.refs_0_
  10.5 14.4 %collective-permute-done = bf16[256,896]{1,0:T(8,128)(2,1)S(1)} collective-permute-done((bf16[256,896]{1,0:T(8,128)(2,1)}, bf16[256,896]{1,0:T(8,128)(2,1)S(1)}, u32[]{:S(2)}, u32[]{:S(2)}) %collective-permute-start) | collective-permute-done | bytes 458784 | tf_op jit(solution)/shard_map/along_z/ppermute | solution.py:31
  24.9 4.2 %collective-permute-start.1 = (bf16[1024,256]{1,0:T(8,128)(2,1)S(1)}, bf16[1024,256]{1,0:T(8,128)(2,1)S(1)}, u32[]{:S(2)}, u32[]{:S(2)}) collective-permute-start(bf16[1024,256]{1,0:T(8,128)(2,1)S(1)} %pad_maximum_fusion.3.refs_0_), channel_id=1, source_target_pairs={{0,2},{1,3},{2,0},{3,1},{4,6},{5,7},{6,4},{7,5},{8,10},{9,11},{10,... | collective-permute-start | bytes 1572872 | tf_op jit(solution)/shard_map/along_z/ppermute | solution.py:31
  29.1 2.4 %collective-permute-start.3 = (bf16[1024,256]{1,0:T(8,128)(2,1)S(1)}, bf16[1024,256]{1,0:T(8,128)(2,1)S(1)}, u32[]{:S(2)}, u32[]{:S(2)}) collective-permute-start(bf16[1024,256]{1,0:T(8,128)(2,1)S(1)} %pad_maximum_fusion.3.refs_0_), channel_id=1, source_target_pairs={{0,12},{1,13},{2,14},{3,15},{4,0},{5,1},{6,2},{7,3},{8,4},{9,5},{1... | collective-permute-start | bytes 1572872 | tf_op jit(solution)/shard_map/along_x/ppermute | solution.py:31
  31.6 19.2 %collective-permute-done.1.refs_5_ = bf16[1024,256]{1,0:T(8,128)(2,1)S(1)} collective-permute-done((bf16[1024,256]{1,0:T(8,128)(2,1)S(1)}, bf16[1024,256]{1,0:T(8,128)(2,1)S(1)}, u32[]{:S(2)}, u32[]{:S(2)}) %collective-permute-start.1) | collective-permute-done | bytes 524320 | tf_op jit(solution)/shard_map/along_z/ppermute | solution.py:31
  50.8 2.1 collective-permute-start.10
  53.9 2.7 %collective-permute-start.20 = (bf16[2,256,896]{2,1,0:T(8,128)(2,1)}, bf16[2,256,896]{2,1,0:T(8,128)(2,1)}, u32[]{:S(2)}, u32[]{:S(2)}) collective-permute-start(bf16[2,256,896]{2,1,0:T(8,128)(2,1)} %pad_maximum_fusion.1.refs_15_), channel_id=1, source_target_pairs={{0,192},{1,193},{2,194},{3,195},{4,196},{5,197},{6,198},{7,199},{8... | collective-permute-start | bytes 2752520 | tf_op jit(solution)/shard_map/along_y/ppermute | solution.py:31
  56.7 12.3 %collective-permute-done.7 = bf16[1024,256]{1,0:T(8,128)(2,1)S(1)} collective-permute-done((bf16[1024,256]{1,0:T(8,128)(2,1)S(1)}, bf16[1024,256]{1,0:T(8,128)(2,1)S(1)}, u32[]{:S(2)}, u32[]{:S(2)}) %collective-permute-start.7) | collective-permute-done | bytes 524320 | tf_op jit(solution)/shard_map/along_z/ppermute | solution.py:31
  69.9 10.8 %collective-permute-start.17 = (bf16[896,256]{1,0:T(8,128)(2,1)}, bf16[896,256]{1,0:T(8,128)(2,1)}, u32[]{:S(2)}, u32[]{:S(2)}) collective-permute-start(bf16[896,256]{1,0:T(8,128)(2,1)} %param.13), channel_id=1, source_target_pairs={{0,32},{1,16},{2,34},{3,18},{4,36},{5,20},{6,38},{7,22},{8,40},{9,... | collective-permute-start | bytes 1376264 | tf_op jit(solution)/shard_map/along_z/ppermute | solution.py:31
  81.7 14.7 %all-to-all-start = ((f32[16,32,256]{2,1,0:T(8,128)}), f32[16,32,256]{2,1,0:T(8,128)}, u32[]{:S(2)}, u32[]{:S(2)}) async-start(f32[16,32,256]{2,1,0:T(8,128)} %broadcast_in_dim.6), calls=%async_computation | async-start | bytes 1048576 | tf_op jit(solution)/shard_map/language_sums/all_to_all | solution.py:139
  96.4 4.6 %collective-permute-start.18 = (bf16[896,256]{1,0:T(8,128)(2,1)}, bf16[896,256]{1,0:T(8,128)(2,1)S(1)}, u32[]{:S(2)}, u32[]{:S(2)}) collective-permute-start(bf16[896,256]{1,0:T(8,128)(2,1)} %param.13), channel_id=1, source_target_pairs={{0,0},{1,48},{2,2},{3,50},{4,4},{5,52},{6,6},{7,54},{8,8},{9,56},{... | collective-permute-start | bytes 1376264 | tf_op jit(solution)/shard_map/along_z/ppermute | solution.py:31
  101.0 2.3 pad_maximum_fusion.refs_10_
  103.3 2.7 %collective-permute-start.14 = (bf16[2,1024,256]{2,1,0:T(8,128)(2,1)}, bf16[2,1024,256]{2,1,0:T(8,128)(2,1)}, u32[]{:S(2)}, u32[]{:S(2)}) collective-permute-start(bf16[2,1024,256]{2,1,0:T(8,128)(2,1)} %pad_maximum_fusion.refs_10_), channel_id=1, source_target_pairs={{0,12},{1,13},{2,14},{3,15},{4,0},{5,1},{6,2},{7,3},{8,4},{9,5},{1... | collective-permute-start | bytes 3145736 | tf_op jit(solution)/shard_map/along_x/ppermute | solution.py:31
  106.6 12.7 %collective-permute-done.18 = bf16[896,256]{1,0:T(8,128)(2,1)S(1)} collective-permute-done((bf16[896,256]{1,0:T(8,128)(2,1)}, bf16[896,256]{1,0:T(8,128)(2,1)S(1)}, u32[]{:S(2)}, u32[]{:S(2)}) %collective-permute-start.18) | collective-permute-done | bytes 458784 | tf_op jit(solution)/shard_map/along_z/ppermute | solution.py:31
  119.3 2.0 pad_maximum_fusion.2.refs_15_
  121.3 2.5 %collective-permute-start.25 = (bf16[2,896,256]{2,1,0:T(8,128)(2,1)}, bf16[2,896,256]{2,1,0:T(8,128)(2,1)}, u32[]{:S(2)}, u32[]{:S(2)}) collective-permute-start(bf16[2,896,256]{2,1,0:T(8,128)(2,1)} %pad_maximum_fusion.2.refs_15_), channel_id=1, source_target_pairs={{0,192},{1,193},{2,194},{3,195},{4,196},{5,197},{6,198},{7,199},{8... | collective-permute-start | bytes 2752520 | tf_op jit(solution)/shard_map/along_y/ppermute | solution.py:31
  124.5 2.5 %collective-permute-start.5 = (bf16[512,256]{1,0:T(8,128)(2,1)}, bf16[512,256]{1,0:T(8,128)(2,1)S(1)}, u32[]{:S(2)}, u32[]{:S(2)}) collective-permute-start(bf16[512,256]{1,0:T(8,128)(2,1)} %slice.65), channel_id=1, source_target_pairs={{0,12},{1,13},{2,14},{3,15},{4,0},{5,1},{6,2},{7,3},{8,4},{9,5},{1... | collective-permute-start | bytes 786440 | tf_op jit(solution)/shard_map/along_x/ppermute | solution.py:31
  127.0 1.1 reduce_sum.27
  128.9 4.1 %all-to-all-start.1 = ((f32[16,32,256]{2,1,0:T(8,128)}), f32[16,32,256]{2,1,0:T(8,128)}, u32[]{:S(2)}, u32[]{:S(2)}) async-start(f32[16,32,256]{2,1,0:T(8,128)} %broadcast_in_dim.7), calls=%async_computation.1 | async-start | bytes 1048576 | tf_op jit(solution)/shard_map/language_sums/all_to_all | solution.py:139
  133.2 2.7 %collective-permute-start.12 = (bf16[512,256]{1,0:T(8,128)(2,1)S(1)}, bf16[512,256]{1,0:T(8,128)(2,1)S(1)}, u32[]{:S(2)}, u32[]{:S(2)}) collective-permute-start(bf16[512,256]{1,0:T(8,128)(2,1)S(1)} %slice.67), channel_id=1, source_target_pairs={{0,12},{1,13},{2,14},{3,15},{4,0},{5,1},{6,2},{7,3},{8,4},{9,5},{1... | collective-permute-start | bytes 786440 | tf_op jit(solution)/shard_map/along_x/ppermute | solution.py:31
  135.9 1.8 slice.71
  137.7 2.7 %collective-permute-start.22 = (bf16[1,256,896]{2,1,0:T(8,128)(2,1)}, bf16[1,256,896]{2,1,0:T(8,128)(2,1)}, u32[]{:S(2)}, u32[]{:S(2)}) collective-permute-start(bf16[1,256,896]{2,1,0:T(8,128)(2,1)} %slice.71), channel_id=1, source_target_pairs={{0,192},{1,193},{2,194},{3,195},{4,196},{5,197},{6,198},{7,199},{8... | collective-permute-start | bytes 1376264 | tf_op jit(solution)/shard_map/along_y/ppermute | solution.py:31
  140.4 1.9 slice.69
  142.2 1.9 slice.68
  144.1 1.7 collective-permute-done.4.refs_3_
  147.5 1.2 collective-permute-start.15
  148.7 1.8 slice.70
  150.6 1.5 collective-permute-start.21
  152.9 2.2 reshape.26
  155.1 1.9 slice.73
  156.9 1.8 slice.72
  158.8 8.1 %collective-permute-done.11.refs_8_ = bf16[512,256]{1,0:T(8,128)(2,1)} collective-permute-done((bf16[512,256]{1,0:T(8,128)(2,1)}, bf16[512,256]{1,0:T(8,128)(2,1)}, u32[]{:S(2)}, u32[]{:S(2)}) %collective-permute-start.11) | collective-permute-done | bytes 262176 | tf_op jit(solution)/shard_map/along_x/ppermute | solution.py:31
  166.9 5.7 %collective-permute-start.27 = (bf16[1,896,256]{2,1,0:T(8,128)(2,1)}, bf16[1,896,256]{2,1,0:T(8,128)(2,1)}, u32[]{:S(2)}, u32[]{:S(2)}) collective-permute-start(bf16[1,896,256]{2,1,0:T(8,128)(2,1)} %slice.73), channel_id=1, source_target_pairs={{0,192},{1,193},{2,194},{3,195},{4,196},{5,197},{6,198},{7,199},{8... | collective-permute-start | bytes 1376264 | tf_op jit(solution)/shard_map/along_y/ppermute | solution.py:31
  172.6 1.3 constant_dynamic-slice_fusion
  173.9 2.0 copy.13
  177.9 11.8 %shard_map.100 = (f32[1024,896]{1,0:T(8,128)}, f32[1024,64]{1,0:T(8,128)S(1)}) custom-call(bf16[1024,256]{1,0:T(8,128)(2,1)S(1)} %pad_maximum_fusion.3.refs_0_, bf16[1024,256]{1,0:T(8,128)(2,1)S(1)} %collective-permute-done.2.refs_1_, bf16[1024,256]{1,0:T(8,128)(2,1)S(1)} %collective-permute-done.3.refs_2_, bf16[512,256]{1,0:T(8,128)(2,1)S(1)} %copy-done.4, ...), custom_call_target="tpu_custom_call" | custom-call | flops 4026531840 | bytes 12582912 | tf_op jit(solution)/shard_map/pallas_call | solution.py:122
  189.7 3.0 %slice.63 = f32[512,896]{1,0:T(8,128)} slice(f32[1024,896]{1,0:T(8,128)} %get-tuple-element.46), slice={[512:1024], [0:896]} | slice | bytes 3670016 | tf_op jit(solution)/shard_map/slice | solution.py:180
  193.5 10.0 %shard_map.101 = f32[1024,896]{1,0:T(8,128)} custom-call(bf16[1024,256]{1,0:T(8,128)(2,1)S(1)} %pad_maximum_fusion.3.refs_0_, bf16[1024,256]{1,0:T(8,128)(2,1)S(1)} %collective-permute-done.2.refs_1_, bf16[1024,256]{1,0:T(8,128)(2,1)S(1)} %collective-permute-done.3.refs_2_, bf16[512,256]{1,0:T(8,128)(2,1)S(1)} %copy-done.4, ...), custom_call_target="tpu_custom_call" | custom-call | flops 4026531840 | bytes 12582912 | tf_op jit(solution)/shard_map/pallas_call | solution.py:122
  203.5 1.7 slice.75
  206.1 2.9 %collective-permute-done.30 = bf16[896,64]{0,1:T(8,128)(2,1)S(1)} collective-permute-done((bf16[896,64]{0,1:T(8,128)(2,1)S(1)}, bf16[896,64]{0,1:T(8,128)(2,1)S(1)}, u32[]{:S(2)}, u32[]{:S(2)}) %collective-permute-start.30) | collective-permute-done | bytes 114720 | tf_op jit(solution)/shard_map/ppermute | solution.py:31
  209.8 3.8 %fusion.4 = f32[512,64]{1,0:T(8,128)S(1)} fusion(f32[512,896]{1,0:T(8,128)} %collective-permute-done.28, f32[1024,896]{1,0:T(8,128)} %shard_map.101, f32[512,896]{1,0:T(8,128)} %collective-permute-done.29, f32[1024,896]{1,0:T(8,128)} %get-tuple-element.46, bf16[896,64]{0,1:T(8,128)(2,1)S(1)} %copy-done.13, bf16[896,64]{0,1:T(8,128)(2,1)S(1)} %collective-permute-done.30, ...), kind=kOutput, calls=%fused_computation.9 | convolution fusion | flops 62447616 | bytes 7700481 | tf_op jit(solution)/shard_map/finish/dot_general | solution.py:187
  214.2 7.2 %collective-permute-start.31 = (f32[64,64]{1,0:T(8,128)S(1)}, f32[64,64]{1,0:T(8,128)S(1)}, u32[]{:S(2)}, u32[]{:S(2)}) collective-permute-start(f32[64,64]{1,0:T(8,128)S(1)} %fusion.6), channel_id=1, source_target_pairs={{0,0},{1,17},{2,2},{3,19},{4,4},{5,21},{6,6},{7,23},{8,8},{9,25},{... | collective-permute-start | bytes 49160 | tf_op jit(solution)/shard_map/finish/ppermute | solution.py:31
  221.5 1.3 collective-permute-done.31
  223.1 10.3 %all_to_all.15 = f32[16,1,4096]{2,1,0:T(1,128)S(1)} all-to-all(f32[16,1,4096]{2,1,0:T(1,128)S(1)} %reshape.29), channel_id=1, replica_groups=mesh['dp'=16,'mp'=16] {'mp'}, dimensions={0} | all-to-all | bytes 524288 | tf_op jit(solution)/shard_map/finish/all_to_all | solution.py:139
  233.9 1.3 reduce.2
  236.0 1.2 multiply_reduce_fusion
  (88 shorter events, 14.6 us)
Async XLA Ops:
  0.0 80.7 %copy-start = (bf16[128,256]{1,0:T(8,128)(2,1)S(1)}, bf16[128,256]{1,0:T(8,128)(2,1)}, u32[]{:S(2)}) copy-start(bf16[128,256]{1,0:T(8,128)(2,1)} %param.18) | copy-start | bytes 196612
  0.0 80.7 %copy-start.12 = (s32[128]{0:T(128)S(1)}, s32[128]{0:T(128)}, u32[]{:S(2)}) copy-start(s32[128]{0:T(128)} %param.19) | copy-start | bytes 1540
  0.0 24.9 %collective-permute-start = (bf16[256,896]{1,0:T(8,128)(2,1)}, bf16[256,896]{1,0:T(8,128)(2,1)S(1)}, u32[]{:S(2)}, u32[]{:S(2)}) collective-permute-start(bf16[256,896]{1,0:T(8,128)(2,1)} %param.12), channel_id=1, source_target_pairs={{0,32},{1,16},{2,34},{3,18},{4,36},{5,20},{6,38},{7,22},{8,40},{9,... | collective-permute-start | bytes 1376264 | tf_op jit(solution)/shard_map/along_z/ppermute | solution.py:31
  4.4 27.2 %collective-permute-start.6 = (bf16[256,896]{1,0:T(8,128)(2,1)}, bf16[256,896]{1,0:T(8,128)(2,1)S(1)}, u32[]{:S(2)}, u32[]{:S(2)}) collective-permute-start(bf16[256,896]{1,0:T(8,128)(2,1)} %param.12), channel_id=1, source_target_pairs={{0,0},{1,48},{2,2},{3,50},{4,4},{5,52},{6,6},{7,54},{8,8},{9,56},{... | collective-permute-start | bytes 1376264 | tf_op jit(solution)/shard_map/along_z/ppermute | solution.py:31
  24.9 25.8 %collective-permute-start.1 = (bf16[1024,256]{1,0:T(8,128)(2,1)S(1)}, bf16[1024,256]{1,0:T(8,128)(2,1)S(1)}, u32[]{:S(2)}, u32[]{:S(2)}) collective-permute-start(bf16[1024,256]{1,0:T(8,128)(2,1)S(1)} %pad_maximum_fusion.3.refs_0_), channel_id=1, source_target_pairs={{0,2},{1,3},{2,0},{3,1},{4,6},{5,7},{6,4},{7,5},{8,10},{9,11},{10,... | collective-permute-start | bytes 1572872 | tf_op jit(solution)/shard_map/along_z/ppermute | solution.py:31
  29.1 21.7 %collective-permute-start.3 = (bf16[1024,256]{1,0:T(8,128)(2,1)S(1)}, bf16[1024,256]{1,0:T(8,128)(2,1)S(1)}, u32[]{:S(2)}, u32[]{:S(2)}) collective-permute-start(bf16[1024,256]{1,0:T(8,128)(2,1)S(1)} %pad_maximum_fusion.3.refs_0_), channel_id=1, source_target_pairs={{0,12},{1,13},{2,14},{3,15},{4,0},{5,1},{6,2},{7,3},{8,4},{9,5},{1... | collective-permute-start | bytes 1572872 | tf_op jit(solution)/shard_map/along_x/ppermute | solution.py:31
  31.6 19.2 %collective-permute-start.2 = (bf16[1024,256]{1,0:T(8,128)(2,1)S(1)}, bf16[1024,256]{1,0:T(8,128)(2,1)S(1)}, u32[]{:S(2)}, u32[]{:S(2)}) collective-permute-start(bf16[1024,256]{1,0:T(8,128)(2,1)S(1)} %pad_maximum_fusion.3.refs_0_), channel_id=1, source_target_pairs={{0,4},{1,5},{2,6},{3,7},{4,8},{5,9},{6,10},{7,11},{8,12},{9,13},{1... | collective-permute-start | bytes 1572872 | tf_op jit(solution)/shard_map/along_x/ppermute | solution.py:31
  31.6 37.5 %collective-permute-start.7 = (bf16[1024,256]{1,0:T(8,128)(2,1)S(1)}, bf16[1024,256]{1,0:T(8,128)(2,1)S(1)}, u32[]{:S(2)}, u32[]{:S(2)}) collective-permute-start(bf16[1024,256]{1,0:T(8,128)(2,1)S(1)} %pad_maximum_fusion.3.refs_0_), channel_id=1, source_target_pairs={{0,16},{1,17},{2,18},{3,19},{4,20},{5,21},{6,22},{7,23},{8,24},{9,... | collective-permute-start | bytes 1572872 | tf_op jit(solution)/shard_map/along_z/ppermute | solution.py:31
  50.8 19.1 %collective-permute-start.8 = (bf16[1024,256]{1,0:T(8,128)(2,1)S(1)}, bf16[1024,256]{1,0:T(8,128)(2,1)S(1)}, u32[]{:S(2)}, u32[]{:S(2)}) collective-permute-start(bf16[1024,256]{1,0:T(8,128)(2,1)S(1)} %pad_maximum_fusion.3.refs_0_), channel_id=1, source_target_pairs={{0,18},{1,19},{2,16},{3,17},{4,22},{5,23},{6,20},{7,21},{8,26},{9,... | collective-permute-start | bytes 1572872 | tf_op jit(solution)/shard_map/along_z/ppermute | solution.py:31
  50.8 45.6 %collective-permute-start.10 = (bf16[1024,256]{1,0:T(8,128)(2,1)S(1)}, bf16[1024,256]{1,0:T(8,128)(2,1)S(1)}, u32[]{:S(2)}, u32[]{:S(2)}) collective-permute-start(bf16[1024,256]{1,0:T(8,128)(2,1)S(1)} %collective-permute-done.1.refs_5_), channel_id=1, source_target_pairs={{0,12},{1,13},{2,14},{3,15},{4,0},{5,1},{6,2},{7,3},{8,4},{9,5},{1... | collective-permute-start | bytes 1572872 | tf_op jit(solution)/shard_map/along_x/ppermute | solution.py:31
  52.9 50.4 %collective-permute-start.9 = (bf16[1024,256]{1,0:T(8,128)(2,1)S(1)}, bf16[1024,256]{1,0:T(8,128)(2,1)S(1)}, u32[]{:S(2)}, u32[]{:S(2)}) collective-permute-start(bf16[1024,256]{1,0:T(8,128)(2,1)S(1)} %collective-permute-done.1.refs_5_), channel_id=1, source_target_pairs={{0,4},{1,5},{2,6},{3,7},{4,8},{5,9},{6,10},{7,11},{8,12},{9,13},{1... | collective-permute-start | bytes 1572872 | tf_op jit(solution)/shard_map/along_x/ppermute | solution.py:31
  53.9 67.4 %collective-permute-start.20 = (bf16[2,256,896]{2,1,0:T(8,128)(2,1)}, bf16[2,256,896]{2,1,0:T(8,128)(2,1)}, u32[]{:S(2)}, u32[]{:S(2)}) collective-permute-start(bf16[2,256,896]{2,1,0:T(8,128)(2,1)} %pad_maximum_fusion.1.refs_15_), channel_id=1, source_target_pairs={{0,192},{1,193},{2,194},{3,195},{4,196},{5,197},{6,198},{7,199},{8... | collective-permute-start | bytes 2752520 | tf_op jit(solution)/shard_map/along_y/ppermute | solution.py:31
  69.0 0.9 copy-start.8
  69.0 52.3 %collective-permute-start.19 = (bf16[2,256,896]{2,1,0:T(8,128)(2,1)}, bf16[2,256,896]{2,1,0:T(8,128)(2,1)}, u32[]{:S(2)}, u32[]{:S(2)}) collective-permute-start(bf16[2,256,896]{2,1,0:T(8,128)(2,1)} %pad_maximum_fusion.1.refs_15_), channel_id=1, source_target_pairs={{0,64},{1,65},{2,66},{3,67},{4,68},{5,69},{6,70},{7,71},{8,72},{9,... | collective-permute-start | bytes 2752520 | tf_op jit(solution)/shard_map/along_y/ppermute | solution.py:31
  69.9 10.8 %copy-start.9 = (bf16[1024,256]{1,0:T(8,128)(2,1)}, bf16[1024,256]{1,0:T(8,128)(2,1)S(1)}, u32[]{:S(2)}) copy-start(bf16[1024,256]{1,0:T(8,128)(2,1)S(1)} %collective-permute-done.8) | copy-start | bytes 1572868
  69.9 36.6 %collective-permute-start.17 = (bf16[896,256]{1,0:T(8,128)(2,1)}, bf16[896,256]{1,0:T(8,128)(2,1)}, u32[]{:S(2)}, u32[]{:S(2)}) collective-permute-start(bf16[896,256]{1,0:T(8,128)(2,1)} %param.13), channel_id=1, source_target_pairs={{0,32},{1,16},{2,34},{3,18},{4,36},{5,20},{6,38},{7,22},{8,40},{9,... | collective-permute-start | bytes 1376264 | tf_op jit(solution)/shard_map/along_z/ppermute | solution.py:31
  81.7 45.3 %all-to-all-start = ((f32[16,32,256]{2,1,0:T(8,128)}), f32[16,32,256]{2,1,0:T(8,128)}, u32[]{:S(2)}, u32[]{:S(2)}) async-start(f32[16,32,256]{2,1,0:T(8,128)} %broadcast_in_dim.6), calls=%async_computation | async-start | bytes 1048576 | tf_op jit(solution)/shard_map/language_sums/all_to_all | solution.py:139
  96.4 22.9 %collective-permute-start.18 = (bf16[896,256]{1,0:T(8,128)(2,1)}, bf16[896,256]{1,0:T(8,128)(2,1)S(1)}, u32[]{:S(2)}, u32[]{:S(2)}) collective-permute-start(bf16[896,256]{1,0:T(8,128)(2,1)} %param.13), channel_id=1, source_target_pairs={{0,0},{1,48},{2,2},{3,50},{4,4},{5,52},{6,6},{7,54},{8,8},{9,56},{... | collective-permute-start | bytes 1376264 | tf_op jit(solution)/shard_map/along_z/ppermute | solution.py:31
  103.3 29.9 %collective-permute-start.14 = (bf16[2,1024,256]{2,1,0:T(8,128)(2,1)}, bf16[2,1024,256]{2,1,0:T(8,128)(2,1)}, u32[]{:S(2)}, u32[]{:S(2)}) collective-permute-start(bf16[2,1024,256]{2,1,0:T(8,128)(2,1)} %pad_maximum_fusion.refs_10_), channel_id=1, source_target_pairs={{0,12},{1,13},{2,14},{3,15},{4,0},{5,1},{6,2},{7,3},{8,4},{9,5},{1... | collective-permute-start | bytes 3145736 | tf_op jit(solution)/shard_map/along_x/ppermute | solution.py:31
  106.6 31.1 %collective-permute-start.13 = (bf16[2,1024,256]{2,1,0:T(8,128)(2,1)}, bf16[2,1024,256]{2,1,0:T(8,128)(2,1)}, u32[]{:S(2)}, u32[]{:S(2)}) collective-permute-start(bf16[2,1024,256]{2,1,0:T(8,128)(2,1)} %pad_maximum_fusion.refs_10_), channel_id=1, source_target_pairs={{0,4},{1,5},{2,6},{3,7},{4,8},{5,9},{6,10},{7,11},{8,12},{9,13},{1... | collective-permute-start | bytes 3145736 | tf_op jit(solution)/shard_map/along_x/ppermute | solution.py:31
  121.3 29.2 %collective-permute-start.25 = (bf16[2,896,256]{2,1,0:T(8,128)(2,1)}, bf16[2,896,256]{2,1,0:T(8,128)(2,1)}, u32[]{:S(2)}, u32[]{:S(2)}) collective-permute-start(bf16[2,896,256]{2,1,0:T(8,128)(2,1)} %pad_maximum_fusion.2.refs_15_), channel_id=1, source_target_pairs={{0,192},{1,193},{2,194},{3,195},{4,196},{5,197},{6,198},{7,199},{8... | collective-permute-start | bytes 2752520 | tf_op jit(solution)/shard_map/along_y/ppermute | solution.py:31
  123.8 29.1 %collective-permute-start.24 = (bf16[2,896,256]{2,1,0:T(8,128)(2,1)}, bf16[2,896,256]{2,1,0:T(8,128)(2,1)}, u32[]{:S(2)}, u32[]{:S(2)}) collective-permute-start(bf16[2,896,256]{2,1,0:T(8,128)(2,1)} %pad_maximum_fusion.2.refs_15_), channel_id=1, source_target_pairs={{0,64},{1,65},{2,66},{3,67},{4,68},{5,69},{6,70},{7,71},{8,72},{9,... | collective-permute-start | bytes 2752520 | tf_op jit(solution)/shard_map/along_y/ppermute | solution.py:31
  124.5 8.6 %collective-permute-start.5 = (bf16[512,256]{1,0:T(8,128)(2,1)}, bf16[512,256]{1,0:T(8,128)(2,1)S(1)}, u32[]{:S(2)}, u32[]{:S(2)}) collective-permute-start(bf16[512,256]{1,0:T(8,128)(2,1)} %slice.65), channel_id=1, source_target_pairs={{0,12},{1,13},{2,14},{3,15},{4,0},{5,1},{6,2},{7,3},{8,4},{9,5},{1... | collective-permute-start | bytes 786440 | tf_op jit(solution)/shard_map/along_x/ppermute | solution.py:31
  128.9 47.1 %all-to-all-start.1 = ((f32[16,32,256]{2,1,0:T(8,128)}), f32[16,32,256]{2,1,0:T(8,128)}, u32[]{:S(2)}, u32[]{:S(2)}) async-start(f32[16,32,256]{2,1,0:T(8,128)} %broadcast_in_dim.7), calls=%async_computation.1 | async-start | bytes 1048576 | tf_op jit(solution)/shard_map/language_sums/all_to_all | solution.py:139
  133.1 12.8 %collective-permute-start.4 = (bf16[512,256]{1,0:T(8,128)(2,1)S(1)}, bf16[512,256]{1,0:T(8,128)(2,1)S(1)}, u32[]{:S(2)}, u32[]{:S(2)}) collective-permute-start(bf16[512,256]{1,0:T(8,128)(2,1)S(1)} %slice.64), channel_id=1, source_target_pairs={{0,4},{1,5},{2,6},{3,7},{4,8},{5,9},{6,10},{7,11},{8,12},{9,13},{1... | collective-permute-start | bytes 786440 | tf_op jit(solution)/shard_map/along_x/ppermute | solution.py:31
  133.2 13.6 %collective-permute-start.12 = (bf16[512,256]{1,0:T(8,128)(2,1)S(1)}, bf16[512,256]{1,0:T(8,128)(2,1)S(1)}, u32[]{:S(2)}, u32[]{:S(2)}) collective-permute-start(bf16[512,256]{1,0:T(8,128)(2,1)S(1)} %slice.67), channel_id=1, source_target_pairs={{0,12},{1,13},{2,14},{3,15},{4,0},{5,1},{6,2},{7,3},{8,4},{9,5},{1... | collective-permute-start | bytes 786440 | tf_op jit(solution)/shard_map/along_x/ppermute | solution.py:31
  137.7 34.9 %collective-permute-start.22 = (bf16[1,256,896]{2,1,0:T(8,128)(2,1)}, bf16[1,256,896]{2,1,0:T(8,128)(2,1)}, u32[]{:S(2)}, u32[]{:S(2)}) collective-permute-start(bf16[1,256,896]{2,1,0:T(8,128)(2,1)} %slice.71), channel_id=1, source_target_pairs={{0,192},{1,193},{2,194},{3,195},{4,196},{5,197},{6,198},{7,199},{8... | collective-permute-start | bytes 1376264 | tf_op jit(solution)/shard_map/along_y/ppermute | solution.py:31
  145.9 0.7 copy-start.3
  146.5 29.4 %collective-permute-start.16 = (bf16[1,1024,256]{2,1,0:T(8,128)(2,1)}, bf16[1,1024,256]{2,1,0:T(8,128)(2,1)}, u32[]{:S(2)}, u32[]{:S(2)}) collective-permute-start(bf16[1,1024,256]{2,1,0:T(8,128)(2,1)} %slice.69), channel_id=1, source_target_pairs={{0,12},{1,13},{2,14},{3,15},{4,0},{5,1},{6,2},{7,3},{8,4},{9,5},{1... | collective-permute-start | bytes 1572872 | tf_op jit(solution)/shard_map/along_x/ppermute | solution.py:31
  146.8 0.7 copy-start.5
  147.5 28.5 %collective-permute-start.15 = (bf16[1,1024,256]{2,1,0:T(8,128)(2,1)}, bf16[1,1024,256]{2,1,0:T(8,128)(2,1)}, u32[]{:S(2)}, u32[]{:S(2)}) collective-permute-start(bf16[1,1024,256]{2,1,0:T(8,128)(2,1)} %slice.68), channel_id=1, source_target_pairs={{0,4},{1,5},{2,6},{3,7},{4,8},{5,9},{6,10},{7,11},{8,12},{9,13},{1... | collective-permute-start | bytes 1572872 | tf_op jit(solution)/shard_map/along_x/ppermute | solution.py:31
  150.6 25.4 %collective-permute-start.21 = (bf16[1,256,896]{2,1,0:T(8,128)(2,1)}, bf16[1,256,896]{2,1,0:T(8,128)(2,1)}, u32[]{:S(2)}, u32[]{:S(2)}) collective-permute-start(bf16[1,256,896]{2,1,0:T(8,128)(2,1)} %slice.70), channel_id=1, source_target_pairs={{0,64},{1,65},{2,66},{3,67},{4,68},{5,69},{6,70},{7,71},{8,72},{9,... | collective-permute-start | bytes 1376264 | tf_op jit(solution)/shard_map/along_y/ppermute | solution.py:31
  152.8 14.0 %collective-permute-start.11 = (bf16[512,256]{1,0:T(8,128)(2,1)}, bf16[512,256]{1,0:T(8,128)(2,1)}, u32[]{:S(2)}, u32[]{:S(2)}) collective-permute-start(bf16[512,256]{1,0:T(8,128)(2,1)} %slice.66), channel_id=1, source_target_pairs={{0,4},{1,5},{2,6},{3,7},{4,8},{5,9},{6,10},{7,11},{8,12},{9,13},{1... | collective-permute-start | bytes 786440 | tf_op jit(solution)/shard_map/along_x/ppermute | solution.py:31
  155.1 17.5 %copy-start.7 = (bf16[8,2,256,64]{2,1,0,3:T(2,128)(2,1)S(1)}, bf16[8,2,256,64]{2,1,0,3:T(2,128)(2,1)}, u32[]{:S(2)}) copy-start(bf16[8,2,256,64]{2,1,0,3:T(2,128)(2,1)} %reshape.26) | copy-start | bytes 1572868
  166.9 26.6 %collective-permute-start.27 = (bf16[1,896,256]{2,1,0:T(8,128)(2,1)}, bf16[1,896,256]{2,1,0:T(8,128)(2,1)}, u32[]{:S(2)}, u32[]{:S(2)}) collective-permute-start(bf16[1,896,256]{2,1,0:T(8,128)(2,1)} %slice.73), channel_id=1, source_target_pairs={{0,192},{1,193},{2,194},{3,195},{4,196},{5,197},{6,198},{7,199},{8... | collective-permute-start | bytes 1376264 | tf_op jit(solution)/shard_map/along_y/ppermute | solution.py:31
  172.6 20.9 %collective-permute-start.26 = (bf16[1,896,256]{2,1,0:T(8,128)(2,1)}, bf16[1,896,256]{2,1,0:T(8,128)(2,1)}, u32[]{:S(2)}, u32[]{:S(2)}) collective-permute-start(bf16[1,896,256]{2,1,0:T(8,128)(2,1)} %slice.72), channel_id=1, source_target_pairs={{0,64},{1,65},{2,66},{3,67},{4,68},{5,69},{6,70},{7,71},{8,72},{9,... | collective-permute-start | bytes 1376264 | tf_op jit(solution)/shard_map/along_y/ppermute | solution.py:31
  176.0 1.0 copy-start.4
  176.9 0.9 copy-start.6
  189.7 3.1 %copy-start.1 = (f32[1024,64]{1,0:T(8,128)}, f32[1024,64]{1,0:T(8,128)S(1)}, u32[]{:S(2)}) copy-start(f32[1024,64]{1,0:T(8,128)S(1)} %get-tuple-element.44) | copy-start | bytes 786436
  192.8 16.2 %collective-permute-start.29 = (f32[512,896]{1,0:T(8,128)}, f32[512,896]{1,0:T(8,128)}, u32[]{:S(2)}, u32[]{:S(2)}) collective-permute-start(f32[512,896]{1,0:T(8,128)} %slice.63), channel_id=1, source_target_pairs={{0,1},{1,0},{2,3},{3,2},{4,5},{5,4},{6,7},{7,6},{8,9},{9,8},{10,11... | collective-permute-start | bytes 5505032 | tf_op jit(solution)/shard_map/ppermute | solution.py:31
  203.5 1.9 copy-start.13
  203.5 2.3 copy-start.2
  205.2 4.5 %collective-permute-start.28 = (f32[512,896]{1,0:T(8,128)S(1)}, f32[512,896]{1,0:T(8,128)}, u32[]{:S(2)}, u32[]{:S(2)}) collective-permute-start(f32[512,896]{1,0:T(8,128)S(1)} %slice.75), channel_id=1, source_target_pairs={{0,1},{1,0},{2,3},{3,2},{4,5},{5,4},{6,7},{7,6},{8,9},{9,8},{10,11... | collective-permute-start | bytes 5505032 | tf_op jit(solution)/shard_map/ppermute | solution.py:31
  205.4 3.6 %collective-permute-start.30 = (bf16[896,64]{0,1:T(8,128)(2,1)S(1)}, bf16[896,64]{0,1:T(8,128)(2,1)S(1)}, u32[]{:S(2)}, u32[]{:S(2)}) collective-permute-start(bf16[896,64]{0,1:T(8,128)(2,1)S(1)} %copy-done.13), channel_id=1, source_target_pairs={{0,1},{1,0},{2,3},{3,2},{4,5},{5,4},{6,7},{7,6},{8,9},{9,8},{10,11... | collective-permute-start | bytes 344072 | tf_op jit(solution)/shard_map/ppermute | solution.py:31
  205.9 7.7 %collective-permute-start.23 = (f32[512,64]{1,0:T(8,128)S(1)}, f32[512,64]{1,0:T(8,128)S(1)}, u32[]{:S(2)}, u32[]{:S(2)}) collective-permute-start(f32[512,64]{1,0:T(8,128)S(1)} %slice.57), channel_id=1, source_target_pairs={{0,1},{1,0},{2,3},{3,2},{4,5},{5,4},{6,7},{7,6},{8,9},{9,8},{10,11... | collective-permute-start | bytes 393224 | tf_op jit(solution)/shard_map/ppermute | solution.py:31
  214.2 21.3 %copy-start.10 = (f32[64,64]{1,0:T(8,128)S(1)}, f32[64,64]{1,0:T(8,128)}, u32[]{:S(2)}) copy-start(f32[64,64]{1,0:T(8,128)} %param.16) | copy-start | bytes 49156
  214.2 21.5 %copy-start.11 = (f32[64,64]{1,0:T(8,128)S(1)}, f32[64,64]{1,0:T(8,128)}, u32[]{:S(2)}) copy-start(f32[64,64]{1,0:T(8,128)} %param.17) | copy-start | bytes 49156
  214.2 8.5 %collective-permute-start.31 = (f32[64,64]{1,0:T(8,128)S(1)}, f32[64,64]{1,0:T(8,128)S(1)}, u32[]{:S(2)}, u32[]{:S(2)}) collective-permute-start(f32[64,64]{1,0:T(8,128)S(1)} %fusion.6), channel_id=1, source_target_pairs={{0,0},{1,17},{2,2},{3,19},{4,4},{5,21},{6,6},{7,23},{8,8},{9,25},{... | collective-permute-start | bytes 49160 | tf_op jit(solution)/shard_map/finish/ppermute | solution.py:31

commit v2 on v1

v2 whole, which is shorter than its diff:
```python
import jax
import jax.numpy as jnp
from jax import lax
from jax.experimental import pallas as pl
from jax.experimental.pallas import tpu as pltpu
from jax.sharding import PartitionSpec as P

LANGS = 32
AXES = ("dp", "mp")
HIGH = lax.Precision.HIGHEST
F32 = jnp.float32


def flat(x, y, z, c):
    x, y, z = x % 4, y % 4, z % 8
    return (y * 4 + (z >> 1)) * 16 + x * 4 + (z & 1) * 2 + c


def perm_of(move):
    pairs = []
    for d in range(16):
        for m in range(16):
            place = (m >> 2, d >> 2, ((d & 3) << 1) | ((m >> 1) & 1), m & 1)
            there = move(*place)
            if there is not None:
                pairs.append((flat(*place), flat(*there)))
    return pairs


def send(v, move):
    return lax.ppermute(v, AXES, perm_of(move))


def first(v, *ready):
    return lax.optimization_barrier((v, *ready))


def ring_moves(axis):
    if axis == "x":
        return (lambda x, y, z, c: (x + 1, y, z, c)), (lambda x, y, z, c: (x - 1, y, z, c))
    return (lambda x, y, z, c: (x, y + 1, z, c)), (lambda x, y, z, c: (x, y - 1, z, c))


def ring_near(v, axis):
    plus, minus = ring_moves(axis)
    return send(v, plus), send(v, minus)


def ring_far(before, after, axis):
    plus, minus = ring_moves(axis)
    half = before.shape[0] // 2
    return send(before[:half], plus), send(after[half:], minus)


def weight_a(x, y, z, c):
    return (x, y, z + 4, c) if c == (z >> 1) & 1 else (x, y, z + 2, 1 - c)


def weight_b(x, y, z, c):
    return (x, y, z, c) if c == (z >> 1) & 1 else (x, y, z - 2, 1 - c)


def coords():
    d, m = lax.axis_index("dp"), lax.axis_index("mp")
    y, zhh, zhl = d // 4, (d // 2) % 2, d % 2
    x, zl, c = m // 4, (m // 2) % 2, m % 2
    return x, y, zhh, zhl, zl, c


def source_bit(zhh, zhl, c):
    same = (c + zhl + 1) % 2
    stays = (1 - same) * zhl
    return (zhh + 1 - stays) % 2


def token_copies(which, late, refs, xv, sem, x, zhh, zhl, zl, c):
    copies = []
    for s in range(2):
        low = (zl + s + (zl + zhl) % 2) % 2 if late else (zl + s) % 2
        for n, step in enumerate((0, 3, 1, 2)):
            col = pl.multiple_of((((x + step) % 4) * 2 + low) * 256, 256)
            for t in range(2):
                row = pl.multiple_of(((t + c) % 2) * 256, 256)
                if step == 2:
                    src = refs[s * 5 + 3 + which].at[pl.ds(t * 256, 256), :]
                else:
                    src = refs[s * 5 + n].at[pl.ds(which * 512 + t * 256, 256), :]
                dst = xv.at[pl.ds(row, 256), pl.ds(col, 256)]
                copies.append(pltpu.make_async_copy(src, dst, sem.at[(s * 4 + n) * 2 + t]))
    return copies


def gate_copies(ref, proj, wv, sem, bit, c):
    copies = []
    for n in range(8):
        src = proj.at[pl.ds(pl.multiple_of((n * 2 + c) * 256, 256), 256), :]
        copies.append(pltpu.make_async_copy(src, wv.at[pl.ds(n * 256, 256), pl.ds(896, 128)], sem.at[8 + n]))
    for r in range(2):
        h = bit if r == 0 else 1 - bit
        for n in range(4):
            row = pl.multiple_of((n * 2 + h) * 256, 256)
            copies.append(pltpu.make_async_copy(ref.at[n, r], wv.at[pl.ds(row, 256), pl.ds(0, 896)], sem.at[r * 4 + n]))
    return copies


def down_copies(ref, wv, sem, bit):
    copies = []
    for r in range(2):
        h = bit if r == 0 else 1 - bit
        for n in range(4):
            col = pl.multiple_of((n * 2 + h) * 256, 256)
            src = ref.at[n, r, pl.ds(0, 896), :]
            copies.append(pltpu.make_async_copy(src, wv.at[:, pl.ds(col, 256)], sem.at[r * 4 + n]))
    return copies


def matmul_kernel(gate, hidden, late, *refs):
    refs = list(refs)
    take = lambda n: [refs.pop(0) for _ in range(n)]
    blocks = take(10)
    gw, proj = take(2) if gate else (None, None)
    dw = take(1)[0] if hidden else None
    take(1)
    gouts = take(2) if gate else []
    houts = take(2) if hidden else []
    gscr = take(4) if gate else []
    hscr = take(4) if hidden else []
    x, y, zhh, zhl, zl, c = coords()
    bit = source_bit(zhh, zhl, c)
    gcopies = hcopies = []
    if gate:
        gcopies = gate_copies(gw, proj, gscr[1], gscr[3], bit, c)
        gcopies = gcopies + token_copies(0, late, blocks, gscr[0], gscr[2], x, zhh, zhl, zl, c)
    if hidden:
        hcopies = down_copies(dw, hscr[1], hscr[3], bit)
        hcopies = hcopies + token_copies(1, late, blocks, hscr[0], hscr[2], x, zhh, zhl, zl, c)
    for copy in gcopies + hcopies:
        copy.start()

    def products(copies, scr, outs, contract):
        for copy in copies:
            copy.wait()

        @pl.loop(0, 2)
        def _(i):
            rows = scr[0][pl.ds(pl.multiple_of(i * 256, 256), 256), :]
            product = lax.dot_general(rows, scr[1][...], (((1,), (contract,)), ((), ())), preferred_element_type=F32)
            for part in range(2):
                @pl.when(i == part)
                def _():
                    outs[part][...] = product

    if gate:
        products(gcopies, gscr, gouts, 0)
    if hidden:
        products(hcopies, hscr, houts, 1)


def matmul(late, blocks, after, gate=None, proj=None, down=None):
    hbm = pl.BlockSpec(memory_space=pltpu.MemorySpace.HBM)
    vmem = pl.BlockSpec(memory_space=pltpu.VMEM)
    shapes, scratch = [], []
    args = list(blocks)
    for there, wshape in ((gate is not None, (2048, 1024)), (down is not None, (896, 2048))):
        if there:
            width = wshape[1] if wshape[0] == 2048 else 896
            shapes += [jax.ShapeDtypeStruct((256, width), F32)] * 2
            scratch += [
                pltpu.VMEM((512, 2048), jnp.bfloat16),
                pltpu.VMEM(wshape, jnp.bfloat16),
                pltpu.SemaphoreType.DMA((16,)),
                pltpu.SemaphoreType.DMA((16,)),
            ]
    if gate is not None:
        args += [gate, proj]
    if down is not None:
        args += [down]
    args += [after]
    flops = 2 * 512 * 2048 * 960 * ((gate is not None) + (down is not None))
    return pl.pallas_call(
        lambda *refs: matmul_kernel(gate is not None, down is not None, late, *refs),
        out_shape=shapes,
        in_specs=[hbm] * len(args),
        out_specs=[vmem] * len(shapes),
        scratch_shapes=scratch,
        compiler_params=pltpu.CompilerParams(vmem_limit_bytes=60 << 20),
        cost_estimate=pl.CostEstimate(flops=flops, bytes_accessed=10 << 20, transcendentals=0),
    )(*args)


def everyone(v, axis):
    return lax.all_to_all(jnp.broadcast_to(v[None], (16,) + v.shape), axis, 0, 0, tiled=True)


def shards(inputs, out_grads, gate_weight, down_weight, in_proj, out_proj, in_precond, out_precond, queries, languages):
    x, y, zhh, zhl, zl, c = coords()
    swap = lambda x, y, z, c: (x, y, z, 1 - c)
    rings = [[y * 4 + h for y in range(4)] for h in range(4)]

    hold = lax.optimization_barrier
    in_proj = jnp.pad(in_proj, ((0, 0), (0, 64)))
    with jax.named_scope("language_sums"):
        onehot = (languages[None, :] == jnp.arange(LANGS, dtype=jnp.int32)[:, None]).astype(jnp.bfloat16)
        mine = jnp.dot(onehot, queries, preferred_element_type=F32)
        high = lax.reduce_precision(mine, 8, 7)
        halves = [high.astype(jnp.bfloat16), (mine - high).astype(jnp.bfloat16)]
        down_weight = jnp.concatenate([down_weight, *halves], axis=0)
    inward = lambda x, y, z, c: (x, y, z ^ 3, c) if z % 4 in (1, 2) else None
    outward = lambda x, y, z, c: (x, y, z ^ 1, c) if z % 4 in (1, 2) else None
    with jax.named_scope("first_moves"):
        ga = send(gate_weight, weight_a)
        gb = send(gate_weight, weight_b)
        both = jnp.concatenate([inputs[0], out_grads[0]], axis=0)
        near = send(both, lambda x, y, z, c: (x, y, z ^ 1, c))
        inner_a = send(both, inward)
        own1, own2 = ring_near(both, "x")
        gates = lax.all_gather(jnp.stack([ga, gb]), "dp", axis_index_groups=rings)
        out_mine = jnp.where(c == zhl, out_proj, send(out_proj, swap))
        near, inner_a, own1, own2, down_weight, out_mine, in_proj, ga = hold(
            (near, inner_a, own1, own2, down_weight, out_mine, in_proj, ga)
        )
    with jax.named_scope("second_moves"):
        da = send(down_weight, weight_a)
        db = send(down_weight, weight_b)
        inner_b = send(near, inward)
        outer_a = send(inner_a, outward)
        near1, near2 = ring_near(near, "x")
        inner_b, outer_a, da, db, near1, near2 = hold((inner_b, outer_a, da, db, near1, near2))
    with jax.named_scope("third_moves"):
        downs = lax.all_gather(jnp.stack([da, db]), "dp", axis_index_groups=rings)
        far_a = jnp.where(zl == zhl, outer_a, inner_a)
        outer_b = send(inner_b, outward)
        fa1, fa2 = ring_near(far_a, "x")
        near3, near4 = ring_far(near1, near2, "x")
        outer_b, fa1, fa2, near3, near4, own1, own2 = hold((outer_b, fa1, fa2, near3, near4, own1, own2))
    with jax.named_scope("fourth_moves"):
        far_b = jnp.where(zl == zhl, outer_b, inner_b)
        fb1, fb2 = ring_near(far_b, "x")
        fa3, fa4 = ring_far(fa1, fa2, "x")
        own3, own4 = ring_far(own1, own2, "x")
        fb1, fb2, fa3, fa4, own3, own4 = hold((fb1, fb2, fa3, fa4, own3, own4))
    early = [both, own1, own2, own3, own4, near, near1, near2, near3, near4]
    with jax.named_scope("fifth_moves"):
        fb3, fb4 = ring_far(fb1, fb2, "x")
        gate0 = matmul(False, early, fb1, gate=gates, proj=in_proj)
        hidden0 = matmul(False, early, gate0[1], down=downs)
    late = [far_a, fa1, fa2, fa3, fa4, far_b, fb1, fb2, fb3, fb4]

    def finish(gate, gate_other, hidden, hidden_other):
        gate = gate + send(gate_other, swap)
        hidden_grad = hidden + send(hidden_other, swap)
        up_grad = (hidden_grad * jax.nn.silu(gate[:, :896])).astype(jnp.bfloat16)
        out_part = jnp.dot(up_grad, out_mine, preferred_element_type=F32)
        return lax.dot_general(gate[:, 896:960], out_part, (((0,), (0,)), ((), ())), precision=HIGH)

    with jax.named_scope("second_half"):
        both1 = matmul(True, late, hidden0[1], gate=gates, proj=in_proj, down=downs)
        outer1 = finish(*both1)
    with jax.named_scope("first_half"):
        outer0 = finish(*gate0, *hidden0)

    with jax.named_scope("language_sums"):
        sums = jnp.sum(downs[:, :, 896:].astype(F32).reshape(16, LANGS, 256), axis=0)
        sums = sums + send(sums, swap)
        by_language = jnp.where(c == zhl, sums, send(sums, lambda x, y, z, c: (x, y, z ^ 2, c)))

    with jax.named_scope("finish"):
        outers = outer0 + send(outer1, lambda x, y, z, c: (x, y, z ^ 2, c))
        part = jnp.dot(jnp.dot(in_precond, outers, precision=HIGH), out_precond, precision=HIGH) / 512
        bands = lax.all_to_all(part.reshape(16, 256), "mp", 0, 0, tiled=True)
        projected = lax.reduce_precision(jnp.sum(bands, axis=0), 8, 7)
        scores = jnp.sum(projected[None, :] * by_language, axis=1)
        scores = jnp.sum(everyone(scores, "mp").reshape(16, LANGS), axis=0)
    return (scores / 64).reshape(1, LANGS)


def solution(mesh):
    return jax.shard_map(
        shards,
        mesh=mesh,
        in_specs=(
            P("dp", None, "mp"),
            P("dp", None, "mp"),
            P("dp", "mp"),
            P("mp", "dp"),
            P(),
            P("mp", None),
            P(),
            P(),
            P("dp", "mp"),
            P("dp"),
        ),
        out_specs=P("dp", None),
        check_vma=False,
    )
```

time: 239 us -> 211 us (0.88)
  starting transfers between devices: 86.4 us -> 49 us
  local copies, waits for them, and re-layouts: 29.2 us -> 7.07 us
  between operations: 0.33 us -> 14.1 us
  waiting for transfers between devices: 74.2 us -> 86.9 us
  blocking collectives: 10.3 us -> 18.1 us
  Pallas kernels: 21.9 us -> 26.3 us
  other arithmetic: 10.5 us -> 7.23 us
  matrix products: 4.99 us -> 2.13 us
    all_to_all x2 -> x0, starting transfers between devices: 18.8 us -> none  [everyone(): lax.all_to_all(jnp.broadcast_to(v[None], (16,) + v.shape), axis, 0, 0, ti...]
    ppermute x32 -> x33, starting transfers between devices: 67.6 us -> 49 us  [send(): return lax.ppermute(v, AXES, perm_of(move))]
    slice x13 -> x9, local copies, waits for them, and re-layouts: 17.3 us -> 1.12 us  [the longest x1 0.97 us: shards(): downs[:, :, 896:].astype(F32).reshape(16, LANGS, 256)]
    ppermute x32 -> x33, waiting for transfers between devices: 74.2 us -> 86.9 us  [send(): return lax.ppermute(v, AXES, perm_of(move))]
    all_to_all x0 -> x1, blocking collectives: none -> 9.78 us  [shards(): bands = lax.all_to_all(part.reshape(16, 256), 'mp', 0, 0, tiled=True)]
    pallas_call x2 -> x3, Pallas kernels: 21.9 us -> 26.3 us  [matmul(): pl.pallas_call(lambda *refs: matmul_kernel(gate is not None, down is not...]
    another operation x3 -> x2, other arithmetic: 5.37 us -> 2.21 us  [the longest x1 1.19 us: shards(): downs = lax.all_gather(jnp.stack([da, db]), 'dp', axis_index_groups=rings)]
    dot_general x4 -> x6, matrix products: 4.87 us -> 2 us  [the longest x2 0.78 us: finish(): out_part = jnp.dot(up_grad, out_mine, preferred_element_type=F32)]
  transfers between devices with their start and end apart: 34 -> 35, of which waited for: 10 -> 13; matrix products, arithmetic and copies ran while one was open for 15% -> 6% of each run, Pallas kernels for 9% -> 12%
where the time goes in v2:
time: 211 us
  waiting for transfers between devices  86.9 us (41%)
  starting transfers between devices  49 us (23%)
  Pallas kernels  26.3 us (12%)
  blocking collectives  18.1 us (9%)
  between operations  14.1 us (7%)
  other arithmetic  7.23 us (3%)
  local copies, waits for them, and re-layouts  7.07 us (3%)
  matrix products  2.13 us (1%)
    ppermute x33, waiting for transfers between devices, send(): return lax.ppermute(v, AXES, perm_of(move))  86.9 us
    ppermute x33, starting transfers between devices, send(): return lax.ppermute(v, AXES, perm_of(move))  49 us
    pallas_call x3, Pallas kernels, matmul(): pl.pallas_call(lambda *refs: matmul_kernel(gate is not None, down is not...  26.3 us
    all_to_all x1, blocking collectives, shards(): bands = lax.all_to_all(part.reshape(16, 256), 'mp', 0, 0, tiled=True)  9.78 us
    all_to_all x1, blocking collectives, everyone(): lax.all_to_all(jnp.broadcast_to(v[None], (16,) + v.shape), axis, 0, 0, ti...  8.32 us
    unnamed x61, local copies, waits for them, and re-layouts  4.58 us
  transfers between devices with their start and end apart: 35, of which 13 were waited for; matrix products, arithmetic and copies ran while one was open for 6% of the time, Pallas kernels for 12%

profile of v2, /device:TPU:1, one launch (start us, length us, event | category | flops | bytes accessed | tf_op | source)
XLA Modules:
  0.0 210.9 jit_solution(351233354813385442)
XLA Ops:
  6.5 4.4 %collective-permute-start.5 = (bf16[256,896]{1,0:T(8,128)(2,1)}, bf16[256,896]{1,0:T(8,128)(2,1)S(1)}, u32[]{:S(2)}, u32[]{:S(2)}) collective-permute-start(bf16[256,896]{1,0:T(8,128)(2,1)} %param.12), channel_id=1, source_target_pairs={{0,32},{1,16},{2,34},{3,18},{4,36},{5,20},{6,38},{7,22},{8,40},{9,... | collective-permute-start | bytes 1376264 | tf_op jit(solution)/shard_map/first_moves/ppermute | solution.py:31
  10.9 5.1 %collective-permute-start.23 = (bf16[256,896]{1,0:T(8,128)(2,1)}, bf16[256,896]{1,0:T(8,128)(2,1)S(1)}, u32[]{:S(2)}, u32[]{:S(2)}) collective-permute-start(bf16[256,896]{1,0:T(8,128)(2,1)} %param.12), channel_id=1, source_target_pairs={{0,0},{1,48},{2,2},{3,50},{4,4},{5,52},{6,6},{7,54},{8,8},{9,56},{... | collective-permute-start | bytes 1376264 | tf_op jit(solution)/shard_map/first_moves/ppermute | solution.py:31
  16.0 15.5 %collective-permute-done.5 = bf16[256,896]{1,0:T(8,128)(2,1)S(1)} collective-permute-done((bf16[256,896]{1,0:T(8,128)(2,1)}, bf16[256,896]{1,0:T(8,128)(2,1)S(1)}, u32[]{:S(2)}, u32[]{:S(2)}) %collective-permute-start.5) | collective-permute-done | bytes 458784 | tf_op jit(solution)/shard_map/first_moves/ppermute | solution.py:31
  31.5 4.9 %collective-permute-done.23 = bf16[256,896]{1,0:T(8,128)(2,1)S(1)} collective-permute-done((bf16[256,896]{1,0:T(8,128)(2,1)}, bf16[256,896]{1,0:T(8,128)(2,1)S(1)}, u32[]{:S(2)}, u32[]{:S(2)}) %collective-permute-start.23) | collective-permute-done | bytes 458784 | tf_op jit(solution)/shard_map/first_moves/ppermute | solution.py:31
  36.4 1.0 pad_maximum_fusion.1
  37.5 1.1 pad_maximum_fusion.2.refs_0_
  39.0 1.4 collective-permute-start.1
  40.4 1.5 collective-permute-start.2
  42.0 1.3 collective-permute-start.3
  43.3 1.5 copy.16
  44.8 1.3 pad.4.refs_11_
  46.2 1.1 pad_maximum_fusion.3
  47.3 0.7 broadcast_select_fusion.2
  48.0 0.6 collective-permute-done.refs_5_
  48.5 3.6 %collective-permute-done.2.refs_1_ = bf16[1024,256]{1,0:T(8,128)(2,1)S(1)} collective-permute-done((bf16[1024,256]{1,0:T(8,128)(2,1)S(1)}, bf16[1024,256]{1,0:T(8,128)(2,1)S(1)}, u32[]{:S(2)}, u32[]{:S(2)}) %collective-permute-start.2) | collective-permute-done | bytes 524320 | tf_op jit(solution)/shard_map/first_moves/ppermute | solution.py:31
  52.4 4.6 %collective-permute-start.8 = (bf16[960,256]{1,0:T(8,128)(2,1)S(1)}, bf16[960,256]{1,0:T(8,128)(2,1)S(1)}, u32[]{:S(2)}, u32[]{:S(2)}) collective-permute-start(bf16[960,256]{1,0:T(8,128)(2,1)S(1)} %pad_maximum_fusion.3), channel_id=1, source_target_pairs={{0,32},{1,16},{2,34},{3,18},{4,36},{5,20},{6,38},{7,22},{8,40},{9,... | collective-permute-start | bytes 1474568 | tf_op jit(solution)/shard_map/second_moves/ppermute | solution.py:31
  57.0 1.2 collective-permute-start.10
  58.2 1.5 collective-permute-start.11
  59.7 1.5 collective-permute-start.6
  61.2 1.3 collective-permute-start.7
  62.4 16.2 %collective-permute-done.8 = bf16[960,256]{1,0:T(8,128)(2,1)S(1)} collective-permute-done((bf16[960,256]{1,0:T(8,128)(2,1)S(1)}, bf16[960,256]{1,0:T(8,128)(2,1)S(1)}, u32[]{:S(2)}, u32[]{:S(2)}) %collective-permute-start.8) | collective-permute-done | bytes 491552 | tf_op jit(solution)/shard_map/second_moves/ppermute | solution.py:31
  78.7 2.2 %collective-permute-start.9 = (bf16[960,256]{1,0:T(8,128)(2,1)S(1)}, bf16[960,256]{1,0:T(8,128)(2,1)S(1)}, u32[]{:S(2)}, u32[]{:S(2)}) collective-permute-start(bf16[960,256]{1,0:T(8,128)(2,1)S(1)} %pad_maximum_fusion.3), channel_id=1, source_target_pairs={{0,0},{1,48},{2,2},{3,50},{4,4},{5,52},{6,6},{7,54},{8,8},{9,56},{... | collective-permute-start | bytes 1474568 | tf_op jit(solution)/shard_map/second_moves/ppermute | solution.py:31
  80.9 14.3 %collective-permute-done.9 = bf16[960,256]{1,0:T(8,128)(2,1)S(1)} collective-permute-done((bf16[960,256]{1,0:T(8,128)(2,1)S(1)}, bf16[960,256]{1,0:T(8,128)(2,1)S(1)}, u32[]{:S(2)}, u32[]{:S(2)}) %collective-permute-start.9) | collective-permute-done | bytes 491552 | tf_op jit(solution)/shard_map/second_moves/ppermute | solution.py:31
  95.3 1.2 pad_maximum_fusion
  96.6 1.1 broadcast_select_fusion.1.refs_0_
  97.8 2.7 %collective-permute-start.14 = (bf16[1024,256]{1,0:T(8,128)(2,1)S(1)}, bf16[1024,256]{1,0:T(8,128)(2,1)S(1)}, u32[]{:S(2)}, u32[]{:S(2)}) collective-permute-start(bf16[1024,256]{1,0:T(8,128)(2,1)S(1)} %broadcast_select_fusion.1.refs_0_), channel_id=1, source_target_pairs={{0,12},{1,13},{2,14},{3,15},{4,0},{5,1},{6,2},{7,3},{8,4},{9,5},{1... | collective-permute-start | bytes 1572872 | tf_op jit(solution)/shard_map/third_moves/ppermute | solution.py:31
  100.5 1.3 collective-permute-start.12
  101.9 2.7 %collective-permute-start.16 = (bf16[512,256]{1,0:T(8,128)(2,1)S(1)}, bf16[512,256]{1,0:T(8,128)(2,1)}, u32[]{:S(2)}, u32[]{:S(2)}) collective-permute-start(bf16[512,256]{1,0:T(8,128)(2,1)S(1)} %slice.40), channel_id=1, source_target_pairs={{0,12},{1,13},{2,14},{3,15},{4,0},{5,1},{6,2},{7,3},{8,4},{9,5},{1... | collective-permute-start | bytes 786440 | tf_op jit(solution)/shard_map/third_moves/ppermute | solution.py:31
  104.6 8.7 %collective-permute-done.15.refs_8_ = bf16[512,256]{1,0:T(8,128)(2,1)S(1)} collective-permute-done((bf16[512,256]{1,0:T(8,128)(2,1)S(1)}, bf16[512,256]{1,0:T(8,128)(2,1)S(1)}, u32[]{:S(2)}, u32[]{:S(2)}) %collective-permute-start.15) | collective-permute-done | bytes 262176 | tf_op jit(solution)/shard_map/third_moves/ppermute | solution.py:31
  113.5 0.8 copy-done.15
  114.6 2.8 %collective-permute-start.18 = (bf16[1024,256]{1,0:T(8,128)(2,1)S(1)}, bf16[1024,256]{1,0:T(8,128)(2,1)S(1)}, u32[]{:S(2)}, u32[]{:S(2)}) collective-permute-start(bf16[1024,256]{1,0:T(8,128)(2,1)S(1)} %broadcast_select_fusion.refs_5_), channel_id=1, source_target_pairs={{0,12},{1,13},{2,14},{3,15},{4,0},{5,1},{6,2},{7,3},{8,4},{9,5},{1... | collective-permute-start | bytes 1572872 | tf_op jit(solution)/shard_map/fourth_moves/ppermute | solution.py:31
  117.4 1.5 collective-permute-start.20
  119.1 4.9 %collective-permute-done.19.refs_3_ = bf16[512,256]{1,0:T(8,128)(2,1)S(1)} collective-permute-done((bf16[512,256]{1,0:T(8,128)(2,1)S(1)}, bf16[512,256]{1,0:T(8,128)(2,1)S(1)}, u32[]{:S(2)}, u32[]{:S(2)}) %collective-permute-start.19) | collective-permute-done | bytes 262176 | tf_op jit(solution)/shard_map/fourth_moves/ppermute | solution.py:31
  124.0 5.1 %collective-permute-done.20.refs_4_ = bf16[512,256]{1,0:T(8,128)(2,1)S(1)} collective-permute-done((bf16[512,256]{1,0:T(8,128)(2,1)S(1)}, bf16[512,256]{1,0:T(8,128)(2,1)S(1)}, u32[]{:S(2)}, u32[]{:S(2)}) %collective-permute-start.20) | collective-permute-done | bytes 262176 | tf_op jit(solution)/shard_map/fourth_moves/ppermute | solution.py:31
  129.1 6.5 %collective-permute-done.21.refs_3_ = bf16[512,256]{1,0:T(8,128)(2,1)S(1)} collective-permute-done((bf16[512,256]{1,0:T(8,128)(2,1)S(1)}, bf16[512,256]{1,0:T(8,128)(2,1)S(1)}, u32[]{:S(2)}, u32[]{:S(2)}) %collective-permute-start.21) | collective-permute-done | bytes 262176 | tf_op jit(solution)/shard_map/fourth_moves/ppermute | solution.py:31
  135.8 0.7 copy-done.17
  136.5 2.5 %collective-permute-start.27 = (bf16[512,256]{1,0:T(8,128)(2,1)S(1)}, bf16[512,256]{1,0:T(8,128)(2,1)S(1)}, u32[]{:S(2)}, u32[]{:S(2)}) collective-permute-start(bf16[512,256]{1,0:T(8,128)(2,1)S(1)} %slice.48), channel_id=1, source_target_pairs={{0,12},{1,13},{2,14},{3,15},{4,0},{5,1},{6,2},{7,3},{8,4},{9,5},{1... | collective-permute-start | bytes 786440 | tf_op jit(solution)/shard_map/fifth_moves/ppermute | solution.py:31
  139.0 7.2 %fifth_moves.2 = (f32[256,1024]{1,0:T(8,128)}, f32[256,1024]{1,0:T(8,128)}) custom-call(bf16[1024,256]{1,0:T(8,128)(2,1)} %copy-done.1, bf16[1024,256]{1,0:T(8,128)(2,1)} %copy-done.2, bf16[1024,256]{1,0:T(8,128)(2,1)} %copy-done.3, bf16[512,256]{1,0:T(8,128)(2,1)} %copy-done.11, bf16[512,256]{1,0:T(8,128)(2,1)} %copy-done.12, bf16[1024,256]{1,0:T(8,128)(2,1)} %copy-done.6, ...), custom_call_target="tpu_custom_call" | custom-call | flops 2013265920 | bytes 10485760 | tf_op jit(solution)/shard_map/fifth_moves/pallas_call | solution.py:180
  146.3 6.9 %fifth_moves.3 = (f32[256,896]{1,0:T(8,128)}, f32[256,896]{1,0:T(8,128)}) custom-call(bf16[1024,256]{1,0:T(8,128)(2,1)} %copy-done.1, bf16[1024,256]{1,0:T(8,128)(2,1)} %copy-done.2, bf16[1024,256]{1,0:T(8,128)(2,1)} %copy-done.3, bf16[512,256]{1,0:T(8,128)(2,1)} %copy-done.11, bf16[512,256]{1,0:T(8,128)(2,1)} %copy-done.12, bf16[1024,256]{1,0:T(8,128)(2,1)} %copy-done.6, ...), custom_call_target="tpu_custom_call" | custom-call | flops 2013265920 | bytes 10485760 | tf_op jit(solution)/shard_map/fifth_moves/pallas_call | solution.py:180
  153.3 0.7 copy-done.27
  153.9 0.7 copy-done.28
  154.6 12.2 %second_half.1 = (f32[256,1024]{1,0:T(8,128)}, f32[256,1024]{1,0:T(8,128)}, f32[256,896]{1,0:T(8,128)}, f32[256,896]{1,0:T(8,128)}) custom-call(bf16[1024,256]{1,0:T(8,128)(2,1)} %copy-done.13, bf16[1024,256]{1,0:T(8,128)(2,1)} %copy-done.15, bf16[1024,256]{1,0:T(8,128)(2,1)} %copy-done.16, bf16[512,256]{1,0:T(8,128)(2,1)} %copy-done.25, ...), custom_call_target="tpu_custom_call" | custom-call | flops 4026531840 | bytes 10485760 | tf_op jit(solution)/shard_map/second_half/pallas_call | solution.py:180
  167.9 1.0 slice.56
  169.3 3.0 %collective-permute-done.31 = f32[32,256]{1,0:T(8,128)S(1)} collective-permute-done((f32[32,256]{1,0:T(8,128)S(1)}, f32[32,256]{1,0:T(8,128)S(1)}, u32[]{:S(2)}, u32[]{:S(2)}) %collective-permute-start.31) | collective-permute-done | bytes 32800 | tf_op jit(solution)/shard_map/language_sums/ppermute | solution.py:31
  172.4 6.9 %collective-permute-start.32 = (f32[32,256]{1,0:T(8,128)S(1)}, f32[32,256]{1,0:T(8,128)S(1)}, u32[]{:S(2)}, u32[]{:S(2)}) collective-permute-start(f32[32,256]{1,0:T(8,128)S(1)} %add.48), channel_id=1, source_target_pairs={{0,16},{1,17},{2,18},{3,19},{4,20},{5,21},{6,22},{7,23},{8,24},{9,... | collective-permute-start | bytes 98312 | tf_op jit(solution)/shard_map/language_sums/ppermute | solution.py:31
  181.0 3.2 %collective-permute-done.30 = f32[64,64]{1,0:T(8,128)S(1)} collective-permute-done((f32[64,64]{1,0:T(8,128)S(1)}, f32[64,64]{1,0:T(8,128)S(1)}, u32[]{:S(2)}, u32[]{:S(2)}) %collective-permute-start.30) | collective-permute-done | bytes 16416 | tf_op jit(solution)/shard_map/finish/ppermute | solution.py:31
  185.2 9.8 %all_to_all.16 = f32[16,1,256]{2,1,0:T(1,128)S(1)} all-to-all(f32[16,1,256]{2,1,0:T(1,128)S(1)} %all_to_all.13), channel_id=1, replica_groups=mesh['dp'=16,'mp'=16] {'mp'}, dimensions={0} | all-to-all | bytes 32768 | tf_op jit(solution)/shard_map/finish/all_to_all | solution.py:270
  195.2 8.3 %all_to_all.17 = f32[16,1,32]{2,1,0:T(1,128)S(1)} all-to-all(f32[16,1,32]{2,1,0:T(1,128)S(1)} %broadcast_in_dim.2), channel_id=1, replica_groups=mesh['dp'=16,'mp'=16] {'mp'}, dimensions={0} | all-to-all | bytes 4096 | tf_op jit(solution)/shard_map/finish/all_to_all | solution.py:192
  (125 shorter events, 6.8 us)
Async XLA Ops:
  6.5 39.6 %copy-start = (bf16[128,256]{1,0:T(8,128)(2,1)S(1)}, bf16[128,256]{1,0:T(8,128)(2,1)}, u32[]{:S(2)}) copy-start(bf16[128,256]{1,0:T(8,128)(2,1)} %param.18) | copy-start | bytes 196612
  6.5 39.6 %copy-start.22 = (s32[128]{0:T(128)S(1)}, s32[128]{0:T(128)}, u32[]{:S(2)}) copy-start(s32[128]{0:T(128)} %param.19) | copy-start | bytes 1540
  6.5 132.5 %all-gather.5.cloned.1.call-start = ((), (), s32[]{:S(2)}) async-start(), calls=%async_computation.2 | async-start | bytes 4587520 | tf_op jit(solution)/shard_map/first_moves/all_gather | solution.py:217
  6.5 24.9 %collective-permute-start.5 = (bf16[256,896]{1,0:T(8,128)(2,1)}, bf16[256,896]{1,0:T(8,128)(2,1)S(1)}, u32[]{:S(2)}, u32[]{:S(2)}) collective-permute-start(bf16[256,896]{1,0:T(8,128)(2,1)} %param.12), channel_id=1, source_target_pairs={{0,32},{1,16},{2,34},{3,18},{4,36},{5,20},{6,38},{7,22},{8,40},{9,... | collective-permute-start | bytes 1376264 | tf_op jit(solution)/shard_map/first_moves/ppermute | solution.py:31
  10.9 25.5 %collective-permute-start.23 = (bf16[256,896]{1,0:T(8,128)(2,1)}, bf16[256,896]{1,0:T(8,128)(2,1)S(1)}, u32[]{:S(2)}, u32[]{:S(2)}) collective-permute-start(bf16[256,896]{1,0:T(8,128)(2,1)} %param.12), channel_id=1, source_target_pairs={{0,0},{1,48},{2,2},{3,50},{4,4},{5,52},{6,6},{7,54},{8,8},{9,56},{... | collective-permute-start | bytes 1376264 | tf_op jit(solution)/shard_map/first_moves/ppermute | solution.py:31
  37.4 108.9 %all-gather.7.cloned.1.call-start = ((), (), s32[]{:S(2)}) async-start(), calls=%async_computation.3 | async-start | bytes 4915200 | tf_op jit(solution)/shard_map/third_moves/all_gather | solution.py:230
  38.5 58.0 %copy-start.1 = (bf16[1024,256]{1,0:T(8,128)(2,1)}, bf16[1024,256]{1,0:T(8,128)(2,1)S(1)}, u32[]{:S(2)}) copy-start(bf16[1024,256]{1,0:T(8,128)(2,1)S(1)} %pad_maximum_fusion.2.refs_0_) | copy-start | bytes 1572868
  38.5 10.0 %collective-permute-start = (bf16[1024,256]{1,0:T(8,128)(2,1)S(1)}, bf16[1024,256]{1,0:T(8,128)(2,1)S(1)}, u32[]{:S(2)}, u32[]{:S(2)}) collective-permute-start(bf16[1024,256]{1,0:T(8,128)(2,1)S(1)} %pad_maximum_fusion.2.refs_0_), channel_id=1, source_target_pairs={{0,2},{1,3},{2,0},{3,1},{4,6},{5,7},{6,4},{7,5},{8,10},{9,11},{10,... | collective-permute-start | bytes 1572872 | tf_op jit(solution)/shard_map/first_moves/ppermute | solution.py:31
  39.0 9.5 %collective-permute-start.1 = (bf16[1024,256]{1,0:T(8,128)(2,1)S(1)}, bf16[1024,256]{1,0:T(8,128)(2,1)}, u32[]{:S(2)}, u32[]{:S(2)}) collective-permute-start(bf16[1024,256]{1,0:T(8,128)(2,1)S(1)} %pad_maximum_fusion.2.refs_0_), channel_id=1, source_target_pairs={{2,16},{3,17},{6,20},{7,21},{10,24},{11,25},{14,28},{15,29},{16,2}... | collective-permute-start | bytes 1572872 | tf_op jit(solution)/shard_map/first_moves/ppermute | solution.py:31
  40.4 11.7 %collective-permute-start.2 = (bf16[1024,256]{1,0:T(8,128)(2,1)S(1)}, bf16[1024,256]{1,0:T(8,128)(2,1)S(1)}, u32[]{:S(2)}, u32[]{:S(2)}) collective-permute-start(bf16[1024,256]{1,0:T(8,128)(2,1)S(1)} %pad_maximum_fusion.2.refs_0_), channel_id=1, source_target_pairs={{0,4},{1,5},{2,6},{3,7},{4,8},{5,9},{6,10},{7,11},{8,12},{9,13},{1... | collective-permute-start | bytes 1572872 | tf_op jit(solution)/shard_map/first_moves/ppermute | solution.py:31
  42.0 10.4 %collective-permute-start.3 = (bf16[1024,256]{1,0:T(8,128)(2,1)S(1)}, bf16[1024,256]{1,0:T(8,128)(2,1)S(1)}, u32[]{:S(2)}, u32[]{:S(2)}) collective-permute-start(bf16[1024,256]{1,0:T(8,128)(2,1)S(1)} %pad_maximum_fusion.2.refs_0_), channel_id=1, source_target_pairs={{0,12},{1,13},{2,14},{3,15},{4,0},{5,1},{6,2},{7,3},{8,4},{9,5},{1... | collective-permute-start | bytes 1572872 | tf_op jit(solution)/shard_map/first_moves/ppermute | solution.py:31
  43.3 4.0 %collective-permute-start.4 = (bf16[896,64]{0,1:T(8,128)(2,1)}, bf16[896,64]{0,1:T(8,128)(2,1)S(1)}, u32[]{:S(2)}, u32[]{:S(2)}) collective-permute-start(bf16[896,64]{0,1:T(8,128)(2,1)} %param.15), channel_id=1, source_target_pairs={{0,1},{1,0},{2,3},{3,2},{4,5},{5,4},{6,7},{7,6},{8,9},{9,8},{10,11... | collective-permute-start | bytes 344072 | tf_op jit(solution)/shard_map/first_moves/ppermute | solution.py:31
  48.5 68.9 %copy-start.6 = (bf16[1024,256]{1,0:T(8,128)(2,1)}, bf16[1024,256]{1,0:T(8,128)(2,1)S(1)}, u32[]{:S(2)}) copy-start(bf16[1024,256]{1,0:T(8,128)(2,1)S(1)} %collective-permute-done.refs_5_) | copy-start | bytes 1572868
  52.1 66.7 %copy-start.2 = (bf16[1024,256]{1,0:T(8,128)(2,1)}, bf16[1024,256]{1,0:T(8,128)(2,1)S(1)}, u32[]{:S(2)}) copy-start(bf16[1024,256]{1,0:T(8,128)(2,1)S(1)} %collective-permute-done.2.refs_1_) | copy-start | bytes 1572868
  52.4 66.6 %copy-start.3 = (bf16[1024,256]{1,0:T(8,128)(2,1)}, bf16[1024,256]{1,0:T(8,128)(2,1)S(1)}, u32[]{:S(2)}) copy-start(bf16[1024,256]{1,0:T(8,128)(2,1)S(1)} %collective-permute-done.3.refs_2_) | copy-start | bytes 1572868
  52.4 26.3 %collective-permute-start.8 = (bf16[960,256]{1,0:T(8,128)(2,1)S(1)}, bf16[960,256]{1,0:T(8,128)(2,1)S(1)}, u32[]{:S(2)}, u32[]{:S(2)}) collective-permute-start(bf16[960,256]{1,0:T(8,128)(2,1)S(1)} %pad_maximum_fusion.3), channel_id=1, source_target_pairs={{0,32},{1,16},{2,34},{3,18},{4,36},{5,20},{6,38},{7,22},{8,40},{9,... | collective-permute-start | bytes 1474568 | tf_op jit(solution)/shard_map/second_moves/ppermute | solution.py:31
  57.0 38.3 %collective-permute-start.10 = (bf16[1024,256]{1,0:T(8,128)(2,1)S(1)}, bf16[1024,256]{1,0:T(8,128)(2,1)S(1)}, u32[]{:S(2)}, u32[]{:S(2)}) collective-permute-start(bf16[1024,256]{1,0:T(8,128)(2,1)S(1)} %collective-permute-done.refs_5_), channel_id=1, source_target_pairs={{0,4},{1,5},{2,6},{3,7},{4,8},{5,9},{6,10},{7,11},{8,12},{9,13},{1... | collective-permute-start | bytes 1572872 | tf_op jit(solution)/shard_map/second_moves/ppermute | solution.py:31
  58.2 37.1 %collective-permute-start.11 = (bf16[1024,256]{1,0:T(8,128)(2,1)S(1)}, bf16[1024,256]{1,0:T(8,128)(2,1)S(1)}, u32[]{:S(2)}, u32[]{:S(2)}) collective-permute-start(bf16[1024,256]{1,0:T(8,128)(2,1)S(1)} %collective-permute-done.refs_5_), channel_id=1, source_target_pairs={{0,12},{1,13},{2,14},{3,15},{4,0},{5,1},{6,2},{7,3},{8,4},{9,5},{1... | collective-permute-start | bytes 1572872 | tf_op jit(solution)/shard_map/second_moves/ppermute | solution.py:31
  59.7 35.6 %collective-permute-start.6 = (bf16[1024,256]{1,0:T(8,128)(2,1)S(1)}, bf16[1024,256]{1,0:T(8,128)(2,1)}, u32[]{:S(2)}, u32[]{:S(2)}) collective-permute-start(bf16[1024,256]{1,0:T(8,128)(2,1)S(1)} %collective-permute-done.refs_5_), channel_id=1, source_target_pairs={{2,16},{3,17},{6,20},{7,21},{10,24},{11,25},{14,28},{15,29},{16,2}... | collective-permute-start | bytes 1572872 | tf_op jit(solution)/shard_map/second_moves/ppermute | solution.py:31
  61.2 34.2 %collective-permute-start.7 = (bf16[1024,256]{1,0:T(8,128)(2,1)}, bf16[1024,256]{1,0:T(8,128)(2,1)}, u32[]{:S(2)}, u32[]{:S(2)}) collective-permute-start(bf16[1024,256]{1,0:T(8,128)(2,1)} %collective-permute-done.1), channel_id=1, source_target_pairs={{2,0},{3,1},{6,4},{7,5},{10,8},{11,9},{14,12},{15,13},{16,18},{17,... | collective-permute-start | bytes 1572872 | tf_op jit(solution)/shard_map/second_moves/ppermute | solution.py:31
  78.7 16.6 %collective-permute-start.9 = (bf16[960,256]{1,0:T(8,128)(2,1)S(1)}, bf16[960,256]{1,0:T(8,128)(2,1)S(1)}, u32[]{:S(2)}, u32[]{:S(2)}) collective-permute-start(bf16[960,256]{1,0:T(8,128)(2,1)S(1)} %pad_maximum_fusion.3), channel_id=1, source_target_pairs={{0,0},{1,48},{2,2},{3,50},{4,4},{5,52},{6,6},{7,54},{8,8},{9,56},{... | collective-permute-start | bytes 1474568 | tf_op jit(solution)/shard_map/second_moves/ppermute | solution.py:31
  95.3 22.1 %copy-start.4 = (bf16[1024,256]{1,0:T(8,128)(2,1)}, bf16[1024,256]{1,0:T(8,128)(2,1)S(1)}, u32[]{:S(2)}) copy-start(bf16[1024,256]{1,0:T(8,128)(2,1)S(1)} %collective-permute-done.10.refs_6_) | copy-start | bytes 1572868
  95.3 22.1 %copy-start.5 = (bf16[1024,256]{1,0:T(8,128)(2,1)}, bf16[1024,256]{1,0:T(8,128)(2,1)S(1)}, u32[]{:S(2)}) copy-start(bf16[1024,256]{1,0:T(8,128)(2,1)S(1)} %collective-permute-done.11.refs_7_) | copy-start | bytes 1572868
  97.7 37.8 %copy-start.13 = (bf16[1024,256]{1,0:T(8,128)(2,1)}, bf16[1024,256]{1,0:T(8,128)(2,1)S(1)}, u32[]{:S(2)}) copy-start(bf16[1024,256]{1,0:T(8,128)(2,1)S(1)} %broadcast_select_fusion.1.refs_0_) | copy-start | bytes 1572868
  97.7 15.7 %collective-permute-start.13 = (bf16[1024,256]{1,0:T(8,128)(2,1)S(1)}, bf16[1024,256]{1,0:T(8,128)(2,1)S(1)}, u32[]{:S(2)}, u32[]{:S(2)}) collective-permute-start(bf16[1024,256]{1,0:T(8,128)(2,1)S(1)} %broadcast_select_fusion.1.refs_0_), channel_id=1, source_target_pairs={{0,4},{1,5},{2,6},{3,7},{4,8},{5,9},{6,10},{7,11},{8,12},{9,13},{1... | collective-permute-start | bytes 1572872 | tf_op jit(solution)/shard_map/third_moves/ppermute | solution.py:31
  97.8 15.6 %collective-permute-start.14 = (bf16[1024,256]{1,0:T(8,128)(2,1)S(1)}, bf16[1024,256]{1,0:T(8,128)(2,1)S(1)}, u32[]{:S(2)}, u32[]{:S(2)}) collective-permute-start(bf16[1024,256]{1,0:T(8,128)(2,1)S(1)} %broadcast_select_fusion.1.refs_0_), channel_id=1, source_target_pairs={{0,12},{1,13},{2,14},{3,15},{4,0},{5,1},{6,2},{7,3},{8,4},{9,5},{1... | collective-permute-start | bytes 1572872 | tf_op jit(solution)/shard_map/third_moves/ppermute | solution.py:31
  100.5 13.0 %collective-permute-start.12 = (bf16[1024,256]{1,0:T(8,128)(2,1)}, bf16[1024,256]{1,0:T(8,128)(2,1)S(1)}, u32[]{:S(2)}, u32[]{:S(2)}) collective-permute-start(bf16[1024,256]{1,0:T(8,128)(2,1)} %collective-permute-done.6), channel_id=1, source_target_pairs={{2,0},{3,1},{6,4},{7,5},{10,8},{11,9},{14,12},{15,13},{16,18},{17,... | collective-permute-start | bytes 1572872 | tf_op jit(solution)/shard_map/third_moves/ppermute | solution.py:31
  101.8 11.6 %collective-permute-start.15 = (bf16[512,256]{1,0:T(8,128)(2,1)S(1)}, bf16[512,256]{1,0:T(8,128)(2,1)S(1)}, u32[]{:S(2)}, u32[]{:S(2)}) collective-permute-start(bf16[512,256]{1,0:T(8,128)(2,1)S(1)} %slice.39), channel_id=1, source_target_pairs={{0,4},{1,5},{2,6},{3,7},{4,8},{5,9},{6,10},{7,11},{8,12},{9,13},{1... | collective-permute-start | bytes 786440 | tf_op jit(solution)/shard_map/third_moves/ppermute | solution.py:31
  101.9 11.5 %collective-permute-start.16 = (bf16[512,256]{1,0:T(8,128)(2,1)S(1)}, bf16[512,256]{1,0:T(8,128)(2,1)}, u32[]{:S(2)}, u32[]{:S(2)}) collective-permute-start(bf16[512,256]{1,0:T(8,128)(2,1)S(1)} %slice.40), channel_id=1, source_target_pairs={{0,12},{1,13},{2,14},{3,15},{4,0},{5,1},{6,2},{7,3},{8,4},{9,5},{1... | collective-permute-start | bytes 786440 | tf_op jit(solution)/shard_map/third_moves/ppermute | solution.py:31
  113.4 25.6 %copy-start.10 = (bf16[512,256]{1,0:T(8,128)(2,1)}, bf16[512,256]{1,0:T(8,128)(2,1)S(1)}, u32[]{:S(2)}) copy-start(bf16[512,256]{1,0:T(8,128)(2,1)S(1)} %collective-permute-done.15.refs_8_) | copy-start | bytes 786436
  113.4 22.3 %copy-start.16 = (bf16[1024,256]{1,0:T(8,128)(2,1)}, bf16[1024,256]{1,0:T(8,128)(2,1)S(1)}, u32[]{:S(2)}) copy-start(bf16[1024,256]{1,0:T(8,128)(2,1)S(1)} %collective-permute-done.14.refs_2_) | copy-start | bytes 1572868
  114.3 9.7 %collective-permute-start.19 = (bf16[512,256]{1,0:T(8,128)(2,1)S(1)}, bf16[512,256]{1,0:T(8,128)(2,1)S(1)}, u32[]{:S(2)}, u32[]{:S(2)}) collective-permute-start(bf16[512,256]{1,0:T(8,128)(2,1)S(1)} %slice.41), channel_id=1, source_target_pairs={{0,4},{1,5},{2,6},{3,7},{4,8},{5,9},{6,10},{7,11},{8,12},{9,13},{1... | collective-permute-start | bytes 786440 | tf_op jit(solution)/shard_map/fourth_moves/ppermute | solution.py:31
  114.3 21.2 %copy-start.14 = (bf16[1024,256]{1,0:T(8,128)(2,1)}, bf16[1024,256]{1,0:T(8,128)(2,1)S(1)}, u32[]{:S(2)}) copy-start(bf16[1024,256]{1,0:T(8,128)(2,1)S(1)} %broadcast_select_fusion.refs_5_) | copy-start | bytes 1572868
  114.3 21.2 %collective-permute-start.17 = (bf16[1024,256]{1,0:T(8,128)(2,1)S(1)}, bf16[1024,256]{1,0:T(8,128)(2,1)S(1)}, u32[]{:S(2)}, u32[]{:S(2)}) collective-permute-start(bf16[1024,256]{1,0:T(8,128)(2,1)S(1)} %broadcast_select_fusion.refs_5_), channel_id=1, source_target_pairs={{0,4},{1,5},{2,6},{3,7},{4,8},{5,9},{6,10},{7,11},{8,12},{9,13},{1... | collective-permute-start | bytes 1572872 | tf_op jit(solution)/shard_map/fourth_moves/ppermute | solution.py:31
  114.6 20.9 %collective-permute-start.18 = (bf16[1024,256]{1,0:T(8,128)(2,1)S(1)}, bf16[1024,256]{1,0:T(8,128)(2,1)S(1)}, u32[]{:S(2)}, u32[]{:S(2)}) collective-permute-start(bf16[1024,256]{1,0:T(8,128)(2,1)S(1)} %broadcast_select_fusion.refs_5_), channel_id=1, source_target_pairs={{0,12},{1,13},{2,14},{3,15},{4,0},{5,1},{6,2},{7,3},{8,4},{9,5},{1... | collective-permute-start | bytes 1572872 | tf_op jit(solution)/shard_map/fourth_moves/ppermute | solution.py:31
  117.4 11.6 %collective-permute-start.20 = (bf16[512,256]{1,0:T(8,128)(2,1)S(1)}, bf16[512,256]{1,0:T(8,128)(2,1)S(1)}, u32[]{:S(2)}, u32[]{:S(2)}) collective-permute-start(bf16[512,256]{1,0:T(8,128)(2,1)S(1)} %slice.42), channel_id=1, source_target_pairs={{0,12},{1,13},{2,14},{3,15},{4,0},{5,1},{6,2},{7,3},{8,4},{9,5},{1... | collective-permute-start | bytes 786440 | tf_op jit(solution)/shard_map/fourth_moves/ppermute | solution.py:31
  118.9 16.6 %collective-permute-start.21 = (bf16[512,256]{1,0:T(8,128)(2,1)S(1)}, bf16[512,256]{1,0:T(8,128)(2,1)S(1)}, u32[]{:S(2)}, u32[]{:S(2)}) collective-permute-start(bf16[512,256]{1,0:T(8,128)(2,1)S(1)} %slice.43), channel_id=1, source_target_pairs={{0,4},{1,5},{2,6},{3,7},{4,8},{5,9},{6,10},{7,11},{8,12},{9,13},{1... | collective-permute-start | bytes 786440 | tf_op jit(solution)/shard_map/fourth_moves/ppermute | solution.py:31
  124.0 11.5 %collective-permute-start.22 = (bf16[512,256]{1,0:T(8,128)(2,1)S(1)}, bf16[512,256]{1,0:T(8,128)(2,1)S(1)}, u32[]{:S(2)}, u32[]{:S(2)}) collective-permute-start(bf16[512,256]{1,0:T(8,128)(2,1)S(1)} %slice.44), channel_id=1, source_target_pairs={{0,12},{1,13},{2,14},{3,15},{4,0},{5,1},{6,2},{7,3},{8,4},{9,5},{1... | collective-permute-start | bytes 786440 | tf_op jit(solution)/shard_map/fourth_moves/ppermute | solution.py:31
  135.6 17.6 %collective-permute-start.26 = (bf16[512,256]{1,0:T(8,128)(2,1)S(1)}, bf16[512,256]{1,0:T(8,128)(2,1)S(1)}, u32[]{:S(2)}, u32[]{:S(2)}) collective-permute-start(bf16[512,256]{1,0:T(8,128)(2,1)S(1)} %slice.47), channel_id=1, source_target_pairs={{0,4},{1,5},{2,6},{3,7},{4,8},{5,9},{6,10},{7,11},{8,12},{9,13},{1... | collective-permute-start | bytes 786440 | tf_op jit(solution)/shard_map/fifth_moves/ppermute | solution.py:31
  136.5 16.8 %collective-permute-start.27 = (bf16[512,256]{1,0:T(8,128)(2,1)S(1)}, bf16[512,256]{1,0:T(8,128)(2,1)S(1)}, u32[]{:S(2)}, u32[]{:S(2)}) collective-permute-start(bf16[512,256]{1,0:T(8,128)(2,1)S(1)} %slice.48), channel_id=1, source_target_pairs={{0,12},{1,13},{2,14},{3,15},{4,0},{5,1},{6,2},{7,3},{8,4},{9,5},{1... | collective-permute-start | bytes 786440 | tf_op jit(solution)/shard_map/fifth_moves/ppermute | solution.py:31
  146.2 33.1 %collective-permute-start.24 = (f32[256,1024]{1,0:T(8,128)}, f32[256,1024]{1,0:T(8,128)S(1)}, u32[]{:S(2)}, u32[]{:S(2)}) collective-permute-start(f32[256,1024]{1,0:T(8,128)} %get-tuple-element.60.refs_11_), channel_id=1, source_target_pairs={{0,1},{1,0},{2,3},{3,2},{4,5},{5,4},{6,7},{7,6},{8,9},{9,8},{10,11... | collective-permute-start | bytes 3145736 | tf_op jit(solution)/shard_map/first_half/ppermute | solution.py:31
  154.6 24.6 %copy-start.8 = (f32[256,1024]{1,0:T(8,128)S(1)}, f32[256,1024]{1,0:T(8,128)}, u32[]{:S(2)}) copy-start(f32[256,1024]{1,0:T(8,128)} %get-tuple-element.59) | copy-start | bytes 3145732
  166.9 12.5 %collective-permute-start.28 = (f32[256,1024]{1,0:T(8,128)}, f32[256,1024]{1,0:T(8,128)S(1)}, u32[]{:S(2)}, u32[]{:S(2)}) collective-permute-start(f32[256,1024]{1,0:T(8,128)} %get-tuple-element.70), channel_id=1, source_target_pairs={{0,1},{1,0},{2,3},{3,2},{4,5},{5,4},{6,7},{7,6},{8,9},{9,8},{10,11... | collective-permute-start | bytes 3145736 | tf_op jit(solution)/shard_map/second_half/ppermute | solution.py:31
  167.4 12.2 %collective-permute-start.29 = (f32[256,896]{1,0:T(8,128)}, f32[256,896]{1,0:T(8,128)S(1)}, u32[]{:S(2)}, u32[]{:S(2)}) collective-permute-start(f32[256,896]{1,0:T(8,128)} %get-tuple-element.72), channel_id=1, source_target_pairs={{0,1},{1,0},{2,3},{3,2},{4,5},{5,4},{6,7},{7,6},{8,9},{9,8},{10,11... | collective-permute-start | bytes 2752520 | tf_op jit(solution)/shard_map/second_half/ppermute | solution.py:31
  167.5 13.0 %collective-permute-start.25 = (f32[256,896]{1,0:T(8,128)S(1)}, f32[256,896]{1,0:T(8,128)S(1)}, u32[]{:S(2)}, u32[]{:S(2)}) collective-permute-start(f32[256,896]{1,0:T(8,128)S(1)} %copy-done.24), channel_id=1, source_target_pairs={{0,1},{1,0},{2,3},{3,2},{4,5},{5,4},{6,7},{7,6},{8,9},{9,8},{10,11... | collective-permute-start | bytes 2752520 | tf_op jit(solution)/shard_map/first_half/ppermute | solution.py:31
  168.9 3.4 %collective-permute-start.31 = (f32[32,256]{1,0:T(8,128)S(1)}, f32[32,256]{1,0:T(8,128)S(1)}, u32[]{:S(2)}, u32[]{:S(2)}) collective-permute-start(f32[32,256]{1,0:T(8,128)S(1)} %convert_reduce_fusion), channel_id=1, source_target_pairs={{0,1},{1,0},{2,3},{3,2},{4,5},{5,4},{6,7},{7,6},{8,9},{9,8},{10,11... | collective-permute-start | bytes 98312 | tf_op jit(solution)/shard_map/language_sums/ppermute | solution.py:31
  172.4 22.7 %collective-permute-start.32 = (f32[32,256]{1,0:T(8,128)S(1)}, f32[32,256]{1,0:T(8,128)S(1)}, u32[]{:S(2)}, u32[]{:S(2)}) collective-permute-start(f32[32,256]{1,0:T(8,128)S(1)} %add.48), channel_id=1, source_target_pairs={{0,16},{1,17},{2,18},{3,19},{4,20},{5,21},{6,22},{7,23},{8,24},{9,... | collective-permute-start | bytes 98312 | tf_op jit(solution)/shard_map/language_sums/ppermute | solution.py:31
  180.4 3.8 %collective-permute-start.30 = (f32[64,64]{1,0:T(8,128)S(1)}, f32[64,64]{1,0:T(8,128)S(1)}, u32[]{:S(2)}, u32[]{:S(2)}) collective-permute-start(f32[64,64]{1,0:T(8,128)S(1)} %fusion.2), channel_id=1, source_target_pairs={{0,16},{1,17},{2,18},{3,19},{4,20},{5,21},{6,22},{7,23},{8,24},{9,... | collective-permute-start | bytes 49160 | tf_op jit(solution)/shard_map/finish/ppermute | solution.py:31
  (17 other events, 105.2 us)
Sparse Core Ops, SparseCore 0:
  37.5 46.8 all-gather.4
  96.7 48.8 all-gather.6

commit v3 on v2

--- a/solution.py
+++ b/solution.py
@@ -114,78 +114,84 @@
     return copies
 
 
-def matmul_kernel(gate, hidden, late, *refs):
-    refs = list(refs)
-    take = lambda n: [refs.pop(0) for _ in range(n)]
-    blocks = take(10)
-    gw, proj = take(2) if gate else (None, None)
-    dw = take(1)[0] if hidden else None
-    take(1)
-    gouts = take(2) if gate else []
-    houts = take(2) if hidden else []
-    gscr = take(4) if gate else []
-    hscr = take(4) if hidden else []
+def gate_kernel(late, *refs):
+    blocks, (weights, proj, _, keep, other, xv, wv, xsem, wsem) = refs[:10], refs[10:]
     x, y, zhh, zhl, zl, c = coords()
-    bit = source_bit(zhh, zhl, c)
-    gcopies = hcopies = []
-    if gate:
-        gcopies = gate_copies(gw, proj, gscr[1], gscr[3], bit, c)
-        gcopies = gcopies + token_copies(0, late, blocks, gscr[0], gscr[2], x, zhh, zhl, zl, c)
-    if hidden:
-        hcopies = down_copies(dw, hscr[1], hscr[3], bit)
-        hcopies = hcopies + token_copies(1, late, blocks, hscr[0], hscr[2], x, zhh, zhl, zl, c)
-    for copy in gcopies + hcopies:
+    copies = gate_copies(weights, proj, wv, wsem, source_bit(zhh, zhl, c), c)
+    copies = copies + token_copies(0, late, blocks, xv, xsem, x, zhh, zhl, zl, c)
+    for copy in copies:
         copy.start()
-
-    def products(copies, scr, outs, contract):
-        for copy in copies:
-            copy.wait()
-
-        @pl.loop(0, 2)
-        def _(i):
-            rows = scr[0][pl.ds(pl.multiple_of(i * 256, 256), 256), :]
-            product = lax.dot_general(rows, scr[1][...], (((1,), (contract,)), ((), ())), preferred_element_type=F32)
-            for part in range(2):
-                @pl.when(i == part)
-                def _():
-                    outs[part][...] = product
-
-    if gate:
-        products(gcopies, gscr, gouts, 0)
-    if hidden:
-        products(hcopies, hscr, houts, 1)
-
-
-def matmul(late, blocks, after, gate=None, proj=None, down=None):
-    hbm = pl.BlockSpec(memory_space=pltpu.MemorySpace.HBM)
-    vmem = pl.BlockSpec(memory_space=pltpu.VMEM)
-    shapes, scratch = [], []
-    args = list(blocks)
-    for there, wshape in ((gate is not None, (2048, 1024)), (down is not None, (896, 2048))):
-        if there:
-            width = wshape[1] if wshape[0] == 2048 else 896
-            shapes += [jax.ShapeDtypeStruct((256, width), F32)] * 2
-            scratch += [
-                pltpu.VMEM((512, 2048), jnp.bfloat16),
-                pltpu.VMEM(wshape, jnp.bfloat16),
-                pltpu.SemaphoreType.DMA((16,)),
-                pltpu.SemaphoreType.DMA((16,)),
-            ]
-    if gate is not None:
-        args += [gate, proj]
-    if down is not None:
-        args += [down]
-    args += [after]
-    flops = 2 * 512 * 2048 * 960 * ((gate is not None) + (down is not None))
+    for copy in copies:
+        copy.wait()
+
+    @pl.loop(0, 2)
+    def _(i):
+        rows = xv[pl.ds(pl.multiple_of(i * 256, 256), 256), :]
+        product = jnp.dot(rows, wv[...], preferred_element_type=F32)
+        for part, target in enumerate((keep, other)):
+            @pl.when(i == part)
+            def _():
+                target[...] = product
+
+
+def hidden_kernel(*refs):
+    early, late, (weights, _, keep, other, xv, wv, xsem0, xsem1, wsem) = refs[:10], refs[10:20], refs[20:]
+    x, y, zhh, zhl, zl, c = coords()
+    first = down_copies(weights, wv, wsem, source_bit(zhh, zhl, c))
+    first = first + token_copies(1, False, early, xv.at[pl.ds(0, 512), :], xsem0, x, zhh, zhl, zl, c)
+    second = token_copies(1, True, late, xv.at[pl.ds(512, 512), :], xsem1, x, zhh, zhl, zl, c)
+    for copy in first + second:
+        copy.start()
+
+    @pl.loop(0, 4)
+    def _(i):
+        for at, copies in ((0, first), (2, second)):
+            @pl.when(i == at)
+            def _():
+                for copy in copies:
+                    copy.wait()
+
+        rows = xv[pl.ds(pl.multiple_of(i * 256, 256), 256), :]
+        product = lax.dot_general(rows, wv[...], (((1,), (1,)), ((), ())), preferred_element_type=F32)
+        place = pl.ds(pl.multiple_of((i // 2) * 256, 256), 256)
+        for part, target in enumerate((keep, other)):
+            @pl.when(i % 2 == part)
+            def _():
+                target[place, :] = product
+
+
+def call(kernel, args, shape, scratch, flops):
     return pl.pallas_call(
-        lambda *refs: matmul_kernel(gate is not None, down is not None, late, *refs),
-        out_shape=shapes,
-        in_specs=[hbm] * len(args),
-        out_specs=[vmem] * len(shapes),
+        kernel,
+        out_shape=[jax.ShapeDtypeStruct(shape, F32)] * 2,
+        in_specs=[pl.BlockSpec(memory_space=pltpu.MemorySpace.HBM)] * len(args),
+        out_specs=[pl.BlockSpec(memory_space=pltpu.VMEM)] * 2,
         scratch_shapes=scratch,
         compiler_params=pltpu.CompilerParams(vmem_limit_bytes=60 << 20),
-        cost_estimate=pl.CostEstimate(flops=flops, bytes_accessed=10 << 20, transcendentals=0),
+        cost_estimate=pl.CostEstimate(flops=flops, bytes_accessed=8 << 20, transcendentals=0),
     )(*args)
+
+
+def gate_matmul(late, blocks, weights, proj, after):
+    scratch = [
+        pltpu.VMEM((512, 2048), jnp.bfloat16),
+        pltpu.VMEM((2048, 1024), jnp.bfloat16),
+        pltpu.SemaphoreType.DMA((16,)),
+        pltpu.SemaphoreType.DMA((16,)),
+    ]
+    kernel = lambda *refs: gate_kernel(late, *refs)
+    return call(kernel, [*blocks, weights, proj, after], (256, 1024), scratch, 2 * 512 * 2048 * 1024)
+
+
+def hidden_matmul(early, late, weights, after):
+    scratch = [
+        pltpu.VMEM((1024, 2048), jnp.bfloat16),
+        pltpu.VMEM((896, 2048), jnp.bfloat16),
+        pltpu.SemaphoreType.DMA((16,)),
+        pltpu.SemaphoreType.DMA((16,)),
+        pltpu.SemaphoreType.DMA((8,)),
+    ]
+    return call(hidden_kernel, [*early, *late, weights, after], (512, 896), scratch, 2 * 1024 * 2048 * 896)
 
 
 def everyone(v, axis):
@@ -232,40 +238,43 @@
         outer_b = send(inner_b, outward)
         fa1, fa2 = ring_near(far_a, "x")
         near3, near4 = ring_far(near1, near2, "x")
-        outer_b, fa1, fa2, near3, near4, own1, own2 = hold((outer_b, fa1, fa2, near3, near4, own1, own2))
+        own3, own4 = ring_far(own1, own2, "x")
+        outer_b, fa1, fa2, near3, near4, own3, own4 = hold((outer_b, fa1, fa2, near3, near4, own3, own4))
+    early = [both, own1, own2, own3, own4, near, near1, near2, near3, near4]
     with jax.named_scope("fourth_moves"):
         far_b = jnp.where(zl == zhl, outer_b, inner_b)
         fb1, fb2 = ring_near(far_b, "x")
         fa3, fa4 = ring_far(fa1, fa2, "x")
-        own3, own4 = ring_far(own1, own2, "x")
-        fb1, fb2, fa3, fa4, own3, own4 = hold((fb1, fb2, fa3, fa4, own3, own4))
-    early = [both, own1, own2, own3, own4, near, near1, near2, near3, near4]
+        gate0 = gate_matmul(False, early, gates, in_proj, fa1)
+        fb1, fb2, fa3, fa4, *gate0 = hold((fb1, fb2, fa3, fa4, *gate0))
     with jax.named_scope("fifth_moves"):
         fb3, fb4 = ring_far(fb1, fb2, "x")
-        gate0 = matmul(False, early, fb1, gate=gates, proj=in_proj)
-        hidden0 = matmul(False, early, gate0[1], down=downs)
-    late = [far_a, fa1, fa2, fa3, fa4, far_b, fb1, fb2, fb3, fb4]
-
-    def finish(gate, gate_other, hidden, hidden_other):
-        gate = gate + send(gate_other, swap)
-        hidden_grad = hidden + send(hidden_other, swap)
+        late = [far_a, fa1, fa2, fa3, fa4, far_b, fb1, fb2, fb3, fb4]
+        gate1 = gate_matmul(True, late, gates, in_proj, gate0[1])
+        downs, other = hold((downs, gate1[1]))
+        gate1 = [gate1[0], other]
+        gate_both = [keep + send(other, swap) for keep, other in (gate0, gate1)]
+    with jax.named_scope("hidden"):
+        sums = jnp.sum(downs[:, :, 896:].astype(F32).reshape(16, LANGS, 256), axis=0)
+        hidden, other = hidden_matmul(early, late, downs, sums)
+        hidden = hidden + send(other, swap)
+        sums = sums + send(sums, swap)
+
+    def finish(gate, hidden_grad):
         up_grad = (hidden_grad * jax.nn.silu(gate[:, :896])).astype(jnp.bfloat16)
         out_part = jnp.dot(up_grad, out_mine, preferred_element_type=F32)
         return lax.dot_general(gate[:, 896:960], out_part, (((0,), (0,)), ((), ())), precision=HIGH)
 
     with jax.named_scope("second_half"):
-        both1 = matmul(True, late, hidden0[1], gate=gates, proj=in_proj, down=downs)
-        outer1 = finish(*both1)
+        outer1 = finish(gate_both[1], hidden[256:])
     with jax.named_scope("first_half"):
-        outer0 = finish(*gate0, *hidden0)
-
-    with jax.named_scope("language_sums"):
-        sums = jnp.sum(downs[:, :, 896:].astype(F32).reshape(16, LANGS, 256), axis=0)
-        sums = sums + send(sums, swap)
-        by_language = jnp.where(c == zhl, sums, send(sums, lambda x, y, z, c: (x, y, z ^ 2, c)))
+        outer0 = finish(gate_both[0], hidden[:256])
 
     with jax.named_scope("finish"):
-        outers = outer0 + send(outer1, lambda x, y, z, c: (x, y, z ^ 2, c))
+        moved = jnp.concatenate([jnp.pad(outer1, ((0, 0), (0, 192))), sums], axis=0)
+        moved = send(moved, lambda x, y, z, c: (x, y, z ^ 2, c))
+        outers = outer0 + moved[:64, :64]
+        by_language = jnp.where(c == zhl, sums, moved[64:])
         part = jnp.dot(jnp.dot(in_precond, outers, precision=HIGH), out_precond, precision=HIGH) / 512
         bands = lax.all_to_all(part.reshape(16, 256), "mp", 0, 0, tiled=True)
         projected = lax.reduce_precision(jnp.sum(bands, axis=0), 8, 7)

time: 211 us -> 210 us (level)
  waiting for transfers between devices: 86.9 us -> 80.4 us
  starting transfers between devices: 49 us -> 55.4 us
  other arithmetic: 7.23 us -> 4.93 us
    ppermute x33 -> x31, waiting for transfers between devices: 86.9 us -> 80.4 us  [send(): return lax.ppermute(v, AXES, perm_of(move))]
    ppermute x33 -> x31, starting transfers between devices: 49 us -> 55.3 us  [send(): return lax.ppermute(v, AXES, perm_of(move))]
    unnamed x61 -> x71, local copies, waits for them, and re-layouts: 4.58 us -> 4.74 us
  transfers between devices with their start and end apart: 35 -> 33, of which waited for: 13 -> 12; matrix products, arithmetic and copies ran while one was open for 6% -> 3% of each run, Pallas kernels for 12% -> 7%
where the time goes in v3:
time: 210 us
  waiting for transfers between devices  80.4 us (38%)
  starting transfers between devices  55.4 us (26%)
  Pallas kernels  25.5 us (12%)
  blocking collectives  18.9 us (9%)
  between operations  14.1 us (7%)
  local copies, waits for them, and re-layouts  8.55 us (4%)
  other arithmetic  4.93 us (2%)
  matrix products  2.13 us (1%)
    ppermute x31, waiting for transfers between devices, send(): return lax.ppermute(v, AXES, perm_of(move))  80.4 us
    ppermute x31, starting transfers between devices, send(): return lax.ppermute(v, AXES, perm_of(move))  55.3 us
    pallas_call x3, Pallas kernels, call(): pl.pallas_call(kernel, out_shape=[jax.ShapeDtypeStruct(shape, F32)] * 2,...  25.5 us
    all_to_all x1, blocking collectives, shards(): bands = lax.all_to_all(part.reshape(16, 256), 'mp', 0, 0, tiled=True)  10.6 us
    all_to_all x1, blocking collectives, everyone(): lax.all_to_all(jnp.broadcast_to(v[None], (16,) + v.shape), axis, 0, 0, ti...  8.32 us
    unnamed x71, local copies, waits for them, and re-layouts  4.74 us
  transfers between devices with their start and end apart: 33, of which 12 were waited for; matrix products, arithmetic and copies ran while one was open for 3% of the time, Pallas kernels for 7%

profile of v3, /device:TPU:1, one launch (start us, length us, event | category | flops | bytes accessed | tf_op | source)
XLA Modules:
  0.0 210.0 jit_solution(327299793328765020)
XLA Ops:
  6.5 4.5 %collective-permute-start.5 = (bf16[256,896]{1,0:T(8,128)(2,1)}, bf16[256,896]{1,0:T(8,128)(2,1)S(1)}, u32[]{:S(2)}, u32[]{:S(2)}) collective-permute-start(bf16[256,896]{1,0:T(8,128)(2,1)} %param.12), channel_id=1, source_target_pairs={{0,32},{1,16},{2,34},{3,18},{4,36},{5,20},{6,38},{7,22},{8,40},{9,... | collective-permute-start | bytes 1376264 | tf_op jit(solution)/shard_map/first_moves/ppermute | solution.py:31
  11.0 5.1 %collective-permute-start.23 = (bf16[256,896]{1,0:T(8,128)(2,1)}, bf16[256,896]{1,0:T(8,128)(2,1)S(1)}, u32[]{:S(2)}, u32[]{:S(2)}) collective-permute-start(bf16[256,896]{1,0:T(8,128)(2,1)} %param.12), channel_id=1, source_target_pairs={{0,0},{1,48},{2,2},{3,50},{4,4},{5,52},{6,6},{7,54},{8,8},{9,56},{... | collective-permute-start | bytes 1376264 | tf_op jit(solution)/shard_map/first_moves/ppermute | solution.py:31
  16.1 15.4 %collective-permute-done.5 = bf16[256,896]{1,0:T(8,128)(2,1)S(1)} collective-permute-done((bf16[256,896]{1,0:T(8,128)(2,1)}, bf16[256,896]{1,0:T(8,128)(2,1)S(1)}, u32[]{:S(2)}, u32[]{:S(2)}) %collective-permute-start.5) | collective-permute-done | bytes 458784 | tf_op jit(solution)/shard_map/first_moves/ppermute | solution.py:31
  31.5 4.9 %collective-permute-done.23 = bf16[256,896]{1,0:T(8,128)(2,1)S(1)} collective-permute-done((bf16[256,896]{1,0:T(8,128)(2,1)}, bf16[256,896]{1,0:T(8,128)(2,1)S(1)}, u32[]{:S(2)}, u32[]{:S(2)}) %collective-permute-start.23) | collective-permute-done | bytes 458784 | tf_op jit(solution)/shard_map/first_moves/ppermute | solution.py:31
  36.5 1.1 pad_maximum_fusion.1
  37.7 0.8 collective-permute-start
  38.5 1.5 collective-permute-start.1
  40.0 1.2 collective-permute-start.2
  41.2 1.5 collective-permute-start.3
  43.2 1.2 pad.8.refs_11_
  45.2 3.3 %collective-permute-done.refs_5_ = bf16[1024,256]{1,0:T(8,128)(2,1)} collective-permute-done((bf16[1024,256]{1,0:T(8,128)(2,1)S(1)}, bf16[1024,256]{1,0:T(8,128)(2,1)}, u32[]{:S(2)}, u32[]{:S(2)}) %collective-permute-start) | collective-permute-done | bytes 524320 | tf_op jit(solution)/shard_map/first_moves/ppermute | solution.py:31
  48.6 2.7 %collective-permute-done.2.refs_1_ = bf16[1024,256]{1,0:T(8,128)(2,1)S(1)} collective-permute-done((bf16[1024,256]{1,0:T(8,128)(2,1)S(1)}, bf16[1024,256]{1,0:T(8,128)(2,1)S(1)}, u32[]{:S(2)}, u32[]{:S(2)}) %collective-permute-start.2) | collective-permute-done | bytes 524320 | tf_op jit(solution)/shard_map/first_moves/ppermute | solution.py:31
  51.6 4.6 %collective-permute-start.8 = (bf16[960,256]{1,0:T(8,128)(2,1)S(1)}, bf16[960,256]{1,0:T(8,128)(2,1)S(1)}, u32[]{:S(2)}, u32[]{:S(2)}) collective-permute-start(bf16[960,256]{1,0:T(8,128)(2,1)S(1)} %pad_maximum_fusion.3), channel_id=1, source_target_pairs={{0,32},{1,16},{2,34},{3,18},{4,36},{5,20},{6,38},{7,22},{8,40},{9,... | collective-permute-start | bytes 1474568 | tf_op jit(solution)/shard_map/second_moves/ppermute | solution.py:31
  56.2 1.2 collective-permute-start.10
  57.4 1.5 collective-permute-start.11
  58.9 0.7 collective-permute-start.6
  59.6 1.3 collective-permute-start.7
  60.9 16.9 %collective-permute-done.8 = bf16[960,256]{1,0:T(8,128)(2,1)S(1)} collective-permute-done((bf16[960,256]{1,0:T(8,128)(2,1)S(1)}, bf16[960,256]{1,0:T(8,128)(2,1)S(1)}, u32[]{:S(2)}, u32[]{:S(2)}) %collective-permute-start.8) | collective-permute-done | bytes 491552 | tf_op jit(solution)/shard_map/second_moves/ppermute | solution.py:31
  77.7 2.9 %collective-permute-start.9 = (bf16[960,256]{1,0:T(8,128)(2,1)S(1)}, bf16[960,256]{1,0:T(8,128)(2,1)S(1)}, u32[]{:S(2)}, u32[]{:S(2)}) collective-permute-start(bf16[960,256]{1,0:T(8,128)(2,1)S(1)} %pad_maximum_fusion.3), channel_id=1, source_target_pairs={{0,0},{1,48},{2,2},{3,50},{4,4},{5,52},{6,6},{7,54},{8,8},{9,56},{... | collective-permute-start | bytes 1474568 | tf_op jit(solution)/shard_map/second_moves/ppermute | solution.py:31
  80.6 13.7 %collective-permute-done.9 = bf16[960,256]{1,0:T(8,128)(2,1)S(1)} collective-permute-done((bf16[960,256]{1,0:T(8,128)(2,1)S(1)}, bf16[960,256]{1,0:T(8,128)(2,1)S(1)}, u32[]{:S(2)}, u32[]{:S(2)}) %collective-permute-start.9) | collective-permute-done | bytes 491552 | tf_op jit(solution)/shard_map/second_moves/ppermute | solution.py:31
  94.4 1.1 pad_maximum_fusion
  95.7 2.7 %collective-permute-start.18 = (bf16[512,256]{1,0:T(8,128)(2,1)S(1)}, bf16[512,256]{1,0:T(8,128)(2,1)S(1)}, u32[]{:S(2)}, u32[]{:S(2)}) collective-permute-start(bf16[512,256]{1,0:T(8,128)(2,1)S(1)} %slice.54), channel_id=1, source_target_pairs={{0,12},{1,13},{2,14},{3,15},{4,0},{5,1},{6,2},{7,3},{8,4},{9,5},{1... | collective-permute-start | bytes 786440 | tf_op jit(solution)/shard_map/third_moves/ppermute | solution.py:31
  98.6 2.7 %collective-permute-start.14 = (bf16[1024,256]{1,0:T(8,128)(2,1)S(1)}, bf16[1024,256]{1,0:T(8,128)(2,1)S(1)}, u32[]{:S(2)}, u32[]{:S(2)}) collective-permute-start(bf16[1024,256]{1,0:T(8,128)(2,1)S(1)} %broadcast_select_fusion.1.refs_0_.refs_10_), channel_id=1, source_target_pairs={{0,12},{1,13},{2,14},{3,15},{4,0},{5,1},{6,2},{7,3},{8,4},{9,5},{1... | collective-permute-start | bytes 1572872 | tf_op jit(solution)/shard_map/third_moves/ppermute | solution.py:31
  101.3 1.3 collective-permute-start.12
  102.8 2.6 %collective-permute-start.16 = (bf16[512,256]{1,0:T(8,128)(2,1)S(1)}, bf16[512,256]{1,0:T(8,128)(2,1)S(1)}, u32[]{:S(2)}, u32[]{:S(2)}) collective-permute-start(bf16[512,256]{1,0:T(8,128)(2,1)S(1)} %slice.52), channel_id=1, source_target_pairs={{0,12},{1,13},{2,14},{3,15},{4,0},{5,1},{6,2},{7,3},{8,4},{9,5},{1... | collective-permute-start | bytes 786440 | tf_op jit(solution)/shard_map/third_moves/ppermute | solution.py:31
  105.4 6.7 %collective-permute-done.15.refs_8_ = bf16[512,256]{1,0:T(8,128)(2,1)S(1)} collective-permute-done((bf16[512,256]{1,0:T(8,128)(2,1)S(1)}, bf16[512,256]{1,0:T(8,128)(2,1)S(1)}, u32[]{:S(2)}, u32[]{:S(2)}) %collective-permute-start.15) | collective-permute-done | bytes 262176 | tf_op jit(solution)/shard_map/third_moves/ppermute | solution.py:31
  112.2 0.7 copy-done.20
  113.0 0.9 collective-permute-start.19
  114.0 1.8 collective-permute-start.20
  115.8 0.7 slice.55
  116.5 0.7 slice.56
  117.2 2.7 %collective-permute-start.22 = (bf16[512,256]{1,0:T(8,128)(2,1)}, bf16[512,256]{1,0:T(8,128)(2,1)S(1)}, u32[]{:S(2)}, u32[]{:S(2)}) collective-permute-start(bf16[512,256]{1,0:T(8,128)(2,1)} %slice.56), channel_id=1, source_target_pairs={{0,12},{1,13},{2,14},{3,15},{4,0},{5,1},{6,2},{7,3},{8,4},{9,5},{1... | collective-permute-start | bytes 786440 | tf_op jit(solution)/shard_map/fourth_moves/ppermute | solution.py:31
  119.9 7.2 %fourth_moves.1 = (f32[256,1024]{1,0:T(8,128)}, f32[256,1024]{1,0:T(8,128)}) custom-call(bf16[1024,256]{1,0:T(8,128)(2,1)} %copy-done.2, bf16[1024,256]{1,0:T(8,128)(2,1)} %copy-done.6, bf16[1024,256]{1,0:T(8,128)(2,1)} %copy-done.7, bf16[512,256]{1,0:T(8,128)(2,1)} %copy-done.18, bf16[512,256]{1,0:T(8,128)(2,1)} %copy-done.19, ...), custom_call_target="tpu_custom_call" | custom-call | flops 2147483648 | bytes 8388608 | tf_op jit(solution)/shard_map/fourth_moves/pallas_call | solution.py:164
  127.2 1.9 collective-permute-done.21.refs_3_.refs_13_
  129.2 2.7 %collective-permute-start.26 = (bf16[512,256]{1,0:T(8,128)(2,1)S(1)}, bf16[512,256]{1,0:T(8,128)(2,1)S(1)}, u32[]{:S(2)}, u32[]{:S(2)}) collective-permute-start(bf16[512,256]{1,0:T(8,128)(2,1)S(1)} %slice.59), channel_id=1, source_target_pairs={{0,12},{1,13},{2,14},{3,15},{4,0},{5,1},{6,2},{7,3},{8,4},{9,5},{1... | collective-permute-start | bytes 786440 | tf_op jit(solution)/shard_map/fifth_moves/ppermute | solution.py:31
  132.0 4.1 %collective-permute-done.25.refs_8_.refs_18_ = bf16[512,256]{1,0:T(8,128)(2,1)S(1)} collective-permute-done((bf16[512,256]{1,0:T(8,128)(2,1)S(1)}, bf16[512,256]{1,0:T(8,128)(2,1)S(1)}, u32[]{:S(2)}, u32[]{:S(2)}) %collective-permute-start.25) | collective-permute-done | bytes 262176 | tf_op jit(solution)/shard_map/fifth_moves/ppermute | solution.py:31
  136.1 0.7 copy-done.24
  136.8 0.7 copy-done.25
  137.4 7.2 %fifth_moves.1 = (f32[256,1024]{1,0:T(8,128)}, f32[256,1024]{1,0:T(8,128)}) custom-call(bf16[1024,256]{1,0:T(8,128)(2,1)} %copy-done.3, bf16[1024,256]{1,0:T(8,128)(2,1)} %copy-done.1, bf16[1024,256]{1,0:T(8,128)(2,1)} %copy-done.10, bf16[512,256]{1,0:T(8,128)(2,1)} %copy-done.22, bf16[512,256]{1,0:T(8,128)(2,1)} %copy-done.23, bf16[1024,256]{1,0:T(8,128)(2,1)} %copy-done.4, ...), custom_call_target="tpu_custom_call" | custom-call | flops 2147483648 | bytes 8388608 | tf_op jit(solution)/shard_map/fifth_moves/pallas_call | solution.py:164
  144.7 1.0 slice.60
  146.3 11.1 %hidden.1 = (f32[512,896]{1,0:T(8,128)}, f32[512,896]{1,0:T(8,128)}) custom-call(bf16[1024,256]{1,0:T(8,128)(2,1)} %copy-done.2, bf16[1024,256]{1,0:T(8,128)(2,1)} %copy-done.6, bf16[1024,256]{1,0:T(8,128)(2,1)} %copy-done.7, bf16[512,256]{1,0:T(8,128)(2,1)} %copy-done.18, bf16[512,256]{1,0:T(8,128)(2,1)} %copy-done.19, ...), custom_call_target="tpu_custom_call" | custom-call | flops 3758096384 | bytes 8388608 | tf_op jit(solution)/shard_map/hidden/pallas_call | solution.py:164
  158.6 5.8 %collective-permute-done.29 = f32[32,256]{1,0:T(8,128)S(1)} collective-permute-done((f32[32,256]{1,0:T(8,128)S(1)}, f32[32,256]{1,0:T(8,128)S(1)}, u32[]{:S(2)}, u32[]{:S(2)}) %collective-permute-start.29) | collective-permute-done | bytes 32800 | tf_op jit(solution)/shard_map/hidden/ppermute | solution.py:31
  164.7 1.3 copy-done.5
  166.2 0.7 copy-done.30
  167.8 9.8 %collective-permute-start.30 = (f32[96,256]{1,0:T(8,128)S(1)}, f32[96,256]{1,0:T(8,128)S(1)}, u32[]{:S(2)}, u32[]{:S(2)}) collective-permute-start(f32[96,256]{1,0:T(8,128)S(1)} %select_maximum_fusion), channel_id=1, source_target_pairs={{0,16},{1,17},{2,18},{3,19},{4,20},{5,21},{6,22},{7,23},{8,24},{9,... | collective-permute-start | bytes 294920 | tf_op jit(solution)/shard_map/finish/ppermute | solution.py:31
  178.0 4.6 %collective-permute-done.30 = f32[96,256]{1,0:T(8,128)S(1)} collective-permute-done((f32[96,256]{1,0:T(8,128)S(1)}, f32[96,256]{1,0:T(8,128)S(1)}, u32[]{:S(2)}, u32[]{:S(2)}) %collective-permute-start.30) | collective-permute-done | bytes 98336 | tf_op jit(solution)/shard_map/finish/ppermute | solution.py:31
  183.5 10.6 %all_to_all.16 = f32[16,1,256]{2,1,0:T(1,128)S(1)} all-to-all(f32[16,1,256]{2,1,0:T(1,128)S(1)} %all_to_all.13), channel_id=1, replica_groups=mesh['dp'=16,'mp'=16] {'mp'}, dimensions={0} | all-to-all | bytes 32768 | tf_op jit(solution)/shard_map/finish/all_to_all | solution.py:279
  194.3 8.3 %all_to_all.17 = f32[16,1,32]{2,1,0:T(1,128)S(1)} all-to-all(f32[16,1,32]{2,1,0:T(1,128)S(1)} %broadcast_in_dim.2), channel_id=1, replica_groups=mesh['dp'=16,'mp'=16] {'mp'}, dimensions={0} | all-to-all | bytes 4096 | tf_op jit(solution)/shard_map/finish/all_to_all | solution.py:198
  (133 shorter events, 7.5 us)
Async XLA Ops:
  6.5 37.8 %copy-start = (bf16[128,256]{1,0:T(8,128)(2,1)S(1)}, bf16[128,256]{1,0:T(8,128)(2,1)}, u32[]{:S(2)}) copy-start(bf16[128,256]{1,0:T(8,128)(2,1)} %param.18) | copy-start | bytes 196612
  6.5 31.1 %copy-start.27 = (bf16[1,512,256]{2,1,0:T(8,128)(2,1)S(1)}, bf16[1,512,256]{2,1,0:T(8,128)(2,1)}, u32[]{:S(2)}) copy-start(bf16[1,512,256]{2,1,0:T(8,128)(2,1)} %param.10) | copy-start | bytes 786436
  6.5 31.1 %copy-start.26 = (bf16[1,512,256]{2,1,0:T(8,128)(2,1)S(1)}, bf16[1,512,256]{2,1,0:T(8,128)(2,1)}, u32[]{:S(2)}) copy-start(bf16[1,512,256]{2,1,0:T(8,128)(2,1)} %param.11) | copy-start | bytes 786436
  6.5 113.4 %all-gather.5.cloned.1.call-start = ((), (), s32[]{:S(2)}) async-start(), calls=%async_computation.2 | async-start | bytes 4587520 | tf_op jit(solution)/shard_map/first_moves/all_gather | solution.py:223
  6.5 25.0 %collective-permute-start.5 = (bf16[256,896]{1,0:T(8,128)(2,1)}, bf16[256,896]{1,0:T(8,128)(2,1)S(1)}, u32[]{:S(2)}, u32[]{:S(2)}) collective-permute-start(bf16[256,896]{1,0:T(8,128)(2,1)} %param.12), channel_id=1, source_target_pairs={{0,32},{1,16},{2,34},{3,18},{4,36},{5,20},{6,38},{7,22},{8,40},{9,... | collective-permute-start | bytes 1376264 | tf_op jit(solution)/shard_map/first_moves/ppermute | solution.py:31
  11.0 25.5 %collective-permute-start.23 = (bf16[256,896]{1,0:T(8,128)(2,1)}, bf16[256,896]{1,0:T(8,128)(2,1)S(1)}, u32[]{:S(2)}, u32[]{:S(2)}) collective-permute-start(bf16[256,896]{1,0:T(8,128)(2,1)} %param.12), channel_id=1, source_target_pairs={{0,0},{1,48},{2,2},{3,50},{4,4},{5,52},{6,6},{7,54},{8,8},{9,56},{... | collective-permute-start | bytes 1376264 | tf_op jit(solution)/shard_map/first_moves/ppermute | solution.py:31
  37.6 107.1 %all-gather.7.cloned.1.call-start = ((), (), s32[]{:S(2)}) async-start(), calls=%async_computation.3 | async-start | bytes 4915200 | tf_op jit(solution)/shard_map/third_moves/all_gather | solution.py:236
  37.7 10.8 %collective-permute-start = (bf16[1024,256]{1,0:T(8,128)(2,1)S(1)}, bf16[1024,256]{1,0:T(8,128)(2,1)}, u32[]{:S(2)}, u32[]{:S(2)}) collective-permute-start(bf16[1024,256]{1,0:T(8,128)(2,1)S(1)} %pad_maximum_fusion.2.refs_0_), channel_id=1, source_target_pairs={{0,2},{1,3},{2,0},{3,1},{4,6},{5,7},{6,4},{7,5},{8,10},{9,11},{10,... | collective-permute-start | bytes 1572872 | tf_op jit(solution)/shard_map/first_moves/ppermute | solution.py:31
  38.5 10.1 %collective-permute-start.1 = (bf16[1024,256]{1,0:T(8,128)(2,1)S(1)}, bf16[1024,256]{1,0:T(8,128)(2,1)}, u32[]{:S(2)}, u32[]{:S(2)}) collective-permute-start(bf16[1024,256]{1,0:T(8,128)(2,1)S(1)} %pad_maximum_fusion.2.refs_0_), channel_id=1, source_target_pairs={{2,16},{3,17},{6,20},{7,21},{10,24},{11,25},{14,28},{15,29},{16,2}... | collective-permute-start | bytes 1572872 | tf_op jit(solution)/shard_map/first_moves/ppermute | solution.py:31
  40.0 11.3 %collective-permute-start.2 = (bf16[1024,256]{1,0:T(8,128)(2,1)S(1)}, bf16[1024,256]{1,0:T(8,128)(2,1)S(1)}, u32[]{:S(2)}, u32[]{:S(2)}) collective-permute-start(bf16[1024,256]{1,0:T(8,128)(2,1)S(1)} %pad_maximum_fusion.2.refs_0_), channel_id=1, source_target_pairs={{0,4},{1,5},{2,6},{3,7},{4,8},{5,9},{6,10},{7,11},{8,12},{9,13},{1... | collective-permute-start | bytes 1572872 | tf_op jit(solution)/shard_map/first_moves/ppermute | solution.py:31
  41.2 10.4 %collective-permute-start.3 = (bf16[1024,256]{1,0:T(8,128)(2,1)S(1)}, bf16[1024,256]{1,0:T(8,128)(2,1)S(1)}, u32[]{:S(2)}, u32[]{:S(2)}) collective-permute-start(bf16[1024,256]{1,0:T(8,128)(2,1)S(1)} %pad_maximum_fusion.2.refs_0_), channel_id=1, source_target_pairs={{0,12},{1,13},{2,14},{3,15},{4,0},{5,1},{6,2},{7,3},{8,4},{9,5},{1... | collective-permute-start | bytes 1572872 | tf_op jit(solution)/shard_map/first_moves/ppermute | solution.py:31
  42.6 1.9 collective-permute-start.4
  51.3 44.4 %copy-start.6 = (bf16[1024,256]{1,0:T(8,128)(2,1)}, bf16[1024,256]{1,0:T(8,128)(2,1)S(1)}, u32[]{:S(2)}) copy-start(bf16[1024,256]{1,0:T(8,128)(2,1)S(1)} %collective-permute-done.2.refs_1_) | copy-start | bytes 1572868
  51.6 44.1 %copy-start.7 = (bf16[1024,256]{1,0:T(8,128)(2,1)}, bf16[1024,256]{1,0:T(8,128)(2,1)S(1)}, u32[]{:S(2)}) copy-start(bf16[1024,256]{1,0:T(8,128)(2,1)S(1)} %collective-permute-done.3.refs_2_) | copy-start | bytes 1572868
  51.6 26.1 %collective-permute-start.8 = (bf16[960,256]{1,0:T(8,128)(2,1)S(1)}, bf16[960,256]{1,0:T(8,128)(2,1)S(1)}, u32[]{:S(2)}, u32[]{:S(2)}) collective-permute-start(bf16[960,256]{1,0:T(8,128)(2,1)S(1)} %pad_maximum_fusion.3), channel_id=1, source_target_pairs={{0,32},{1,16},{2,34},{3,18},{4,36},{5,20},{6,38},{7,22},{8,40},{9,... | collective-permute-start | bytes 1474568 | tf_op jit(solution)/shard_map/second_moves/ppermute | solution.py:31
  56.2 38.1 %collective-permute-start.10 = (bf16[1024,256]{1,0:T(8,128)(2,1)}, bf16[1024,256]{1,0:T(8,128)(2,1)S(1)}, u32[]{:S(2)}, u32[]{:S(2)}) collective-permute-start(bf16[1024,256]{1,0:T(8,128)(2,1)} %collective-permute-done.refs_5_), channel_id=1, source_target_pairs={{0,4},{1,5},{2,6},{3,7},{4,8},{5,9},{6,10},{7,11},{8,12},{9,13},{1... | collective-permute-start | bytes 1572872 | tf_op jit(solution)/shard_map/second_moves/ppermute | solution.py:31
  57.4 36.9 %collective-permute-start.11 = (bf16[1024,256]{1,0:T(8,128)(2,1)}, bf16[1024,256]{1,0:T(8,128)(2,1)S(1)}, u32[]{:S(2)}, u32[]{:S(2)}) collective-permute-start(bf16[1024,256]{1,0:T(8,128)(2,1)} %collective-permute-done.refs_5_), channel_id=1, source_target_pairs={{0,12},{1,13},{2,14},{3,15},{4,0},{5,1},{6,2},{7,3},{8,4},{9,5},{1... | collective-permute-start | bytes 1572872 | tf_op jit(solution)/shard_map/second_moves/ppermute | solution.py:31
  58.9 35.5 %collective-permute-start.6 = (bf16[1024,256]{1,0:T(8,128)(2,1)}, bf16[1024,256]{1,0:T(8,128)(2,1)S(1)}, u32[]{:S(2)}, u32[]{:S(2)}) collective-permute-start(bf16[1024,256]{1,0:T(8,128)(2,1)} %collective-permute-done.refs_5_), channel_id=1, source_target_pairs={{2,16},{3,17},{6,20},{7,21},{10,24},{11,25},{14,28},{15,29},{16,2}... | collective-permute-start | bytes 1572872 | tf_op jit(solution)/shard_map/second_moves/ppermute | solution.py:31
  59.6 34.8 %collective-permute-start.7 = (bf16[1024,256]{1,0:T(8,128)(2,1)}, bf16[1024,256]{1,0:T(8,128)(2,1)S(1)}, u32[]{:S(2)}, u32[]{:S(2)}) collective-permute-start(bf16[1024,256]{1,0:T(8,128)(2,1)} %collective-permute-done.1), channel_id=1, source_target_pairs={{2,0},{3,1},{6,4},{7,5},{10,8},{11,9},{14,12},{15,13},{16,18},{17,... | collective-permute-start | bytes 1572872 | tf_op jit(solution)/shard_map/second_moves/ppermute | solution.py:31
  77.7 16.6 %collective-permute-start.9 = (bf16[960,256]{1,0:T(8,128)(2,1)S(1)}, bf16[960,256]{1,0:T(8,128)(2,1)S(1)}, u32[]{:S(2)}, u32[]{:S(2)}) collective-permute-start(bf16[960,256]{1,0:T(8,128)(2,1)S(1)} %pad_maximum_fusion.3), channel_id=1, source_target_pairs={{0,0},{1,48},{2,2},{3,50},{4,4},{5,52},{6,6},{7,54},{8,8},{9,56},{... | collective-permute-start | bytes 1474568 | tf_op jit(solution)/shard_map/second_moves/ppermute | solution.py:31
  95.6 7.1 %collective-permute-start.17 = (bf16[512,256]{1,0:T(8,128)(2,1)S(1)}, bf16[512,256]{1,0:T(8,128)(2,1)S(1)}, u32[]{:S(2)}, u32[]{:S(2)}) collective-permute-start(bf16[512,256]{1,0:T(8,128)(2,1)S(1)} %slice.53), channel_id=1, source_target_pairs={{0,4},{1,5},{2,6},{3,7},{4,8},{5,9},{6,10},{7,11},{8,12},{9,13},{1... | collective-permute-start | bytes 786440 | tf_op jit(solution)/shard_map/third_moves/ppermute | solution.py:31
  95.7 7.0 %collective-permute-start.18 = (bf16[512,256]{1,0:T(8,128)(2,1)S(1)}, bf16[512,256]{1,0:T(8,128)(2,1)S(1)}, u32[]{:S(2)}, u32[]{:S(2)}) collective-permute-start(bf16[512,256]{1,0:T(8,128)(2,1)S(1)} %slice.54), channel_id=1, source_target_pairs={{0,12},{1,13},{2,14},{3,15},{4,0},{5,1},{6,2},{7,3},{8,4},{9,5},{1... | collective-permute-start | bytes 786440 | tf_op jit(solution)/shard_map/third_moves/ppermute | solution.py:31
  98.5 18.7 %copy-start.3 = (bf16[1024,256]{1,0:T(8,128)(2,1)}, bf16[1024,256]{1,0:T(8,128)(2,1)S(1)}, u32[]{:S(2)}) copy-start(bf16[1024,256]{1,0:T(8,128)(2,1)S(1)} %broadcast_select_fusion.1.refs_0_.refs_10_) | copy-start | bytes 1572868
  98.5 13.6 %collective-permute-start.13 = (bf16[1024,256]{1,0:T(8,128)(2,1)S(1)}, bf16[1024,256]{1,0:T(8,128)(2,1)S(1)}, u32[]{:S(2)}, u32[]{:S(2)}) collective-permute-start(bf16[1024,256]{1,0:T(8,128)(2,1)S(1)} %broadcast_select_fusion.1.refs_0_.refs_10_), channel_id=1, source_target_pairs={{0,4},{1,5},{2,6},{3,7},{4,8},{5,9},{6,10},{7,11},{8,12},{9,13},{1... | collective-permute-start | bytes 1572872 | tf_op jit(solution)/shard_map/third_moves/ppermute | solution.py:31
  98.6 13.5 %collective-permute-start.14 = (bf16[1024,256]{1,0:T(8,128)(2,1)S(1)}, bf16[1024,256]{1,0:T(8,128)(2,1)S(1)}, u32[]{:S(2)}, u32[]{:S(2)}) collective-permute-start(bf16[1024,256]{1,0:T(8,128)(2,1)S(1)} %broadcast_select_fusion.1.refs_0_.refs_10_), channel_id=1, source_target_pairs={{0,12},{1,13},{2,14},{3,15},{4,0},{5,1},{6,2},{7,3},{8,4},{9,5},{1... | collective-permute-start | bytes 1572872 | tf_op jit(solution)/shard_map/third_moves/ppermute | solution.py:31
  101.3 10.9 %collective-permute-start.12 = (bf16[1024,256]{1,0:T(8,128)(2,1)S(1)}, bf16[1024,256]{1,0:T(8,128)(2,1)S(1)}, u32[]{:S(2)}, u32[]{:S(2)}) collective-permute-start(bf16[1024,256]{1,0:T(8,128)(2,1)S(1)} %collective-permute-done.6), channel_id=1, source_target_pairs={{2,0},{3,1},{6,4},{7,5},{10,8},{11,9},{14,12},{15,13},{16,18},{17,... | collective-permute-start | bytes 1572872 | tf_op jit(solution)/shard_map/third_moves/ppermute | solution.py:31
  102.7 17.2 %copy-start.18 = (bf16[512,256]{1,0:T(8,128)(2,1)}, bf16[512,256]{1,0:T(8,128)(2,1)S(1)}, u32[]{:S(2)}) copy-start(bf16[512,256]{1,0:T(8,128)(2,1)S(1)} %collective-permute-done.17.refs_3_) | copy-start | bytes 786436
  102.7 9.5 %collective-permute-start.15 = (bf16[512,256]{1,0:T(8,128)(2,1)S(1)}, bf16[512,256]{1,0:T(8,128)(2,1)S(1)}, u32[]{:S(2)}, u32[]{:S(2)}) collective-permute-start(bf16[512,256]{1,0:T(8,128)(2,1)S(1)} %slice.51), channel_id=1, source_target_pairs={{0,4},{1,5},{2,6},{3,7},{4,8},{5,9},{6,10},{7,11},{8,12},{9,13},{1... | collective-permute-start | bytes 786440 | tf_op jit(solution)/shard_map/third_moves/ppermute | solution.py:31
  102.8 9.4 %collective-permute-start.16 = (bf16[512,256]{1,0:T(8,128)(2,1)S(1)}, bf16[512,256]{1,0:T(8,128)(2,1)S(1)}, u32[]{:S(2)}, u32[]{:S(2)}) collective-permute-start(bf16[512,256]{1,0:T(8,128)(2,1)S(1)} %slice.52), channel_id=1, source_target_pairs={{0,12},{1,13},{2,14},{3,15},{4,0},{5,1},{6,2},{7,3},{8,4},{9,5},{1... | collective-permute-start | bytes 786440 | tf_op jit(solution)/shard_map/third_moves/ppermute | solution.py:31
  112.2 15.0 %copy-start.10 = (bf16[1024,256]{1,0:T(8,128)(2,1)}, bf16[1024,256]{1,0:T(8,128)(2,1)S(1)}, u32[]{:S(2)}) copy-start(bf16[1024,256]{1,0:T(8,128)(2,1)S(1)} %collective-permute-done.14.refs_2_.refs_12_) | copy-start | bytes 1572868
  113.0 14.1 %copy-start.4 = (bf16[1024,256]{1,0:T(8,128)(2,1)}, bf16[1024,256]{1,0:T(8,128)(2,1)S(1)}, u32[]{:S(2)}) copy-start(bf16[1024,256]{1,0:T(8,128)(2,1)S(1)} %broadcast_select_fusion.refs_5_.refs_15_) | copy-start | bytes 1572868
  113.0 16.0 %collective-permute-start.19 = (bf16[1024,256]{1,0:T(8,128)(2,1)S(1)}, bf16[1024,256]{1,0:T(8,128)(2,1)S(1)}, u32[]{:S(2)}, u32[]{:S(2)}) collective-permute-start(bf16[1024,256]{1,0:T(8,128)(2,1)S(1)} %broadcast_select_fusion.refs_5_.refs_15_), channel_id=1, source_target_pairs={{0,4},{1,5},{2,6},{3,7},{4,8},{5,9},{6,10},{7,11},{8,12},{9,13},{1... | collective-permute-start | bytes 1572872 | tf_op jit(solution)/shard_map/fourth_moves/ppermute | solution.py:31
  114.0 15.1 %collective-permute-start.20 = (bf16[1024,256]{1,0:T(8,128)(2,1)S(1)}, bf16[1024,256]{1,0:T(8,128)(2,1)S(1)}, u32[]{:S(2)}, u32[]{:S(2)}) collective-permute-start(bf16[1024,256]{1,0:T(8,128)(2,1)S(1)} %broadcast_select_fusion.refs_5_.refs_15_), channel_id=1, source_target_pairs={{0,12},{1,13},{2,14},{3,15},{4,0},{5,1},{6,2},{7,3},{8,4},{9,5},{1... | collective-permute-start | bytes 1572872 | tf_op jit(solution)/shard_map/fourth_moves/ppermute | solution.py:31
  116.5 12.5 %collective-permute-start.21 = (bf16[512,256]{1,0:T(8,128)(2,1)}, bf16[512,256]{1,0:T(8,128)(2,1)S(1)}, u32[]{:S(2)}, u32[]{:S(2)}) collective-permute-start(bf16[512,256]{1,0:T(8,128)(2,1)} %slice.55), channel_id=1, source_target_pairs={{0,4},{1,5},{2,6},{3,7},{4,8},{5,9},{6,10},{7,11},{8,12},{9,13},{1... | collective-permute-start | bytes 786440 | tf_op jit(solution)/shard_map/fourth_moves/ppermute | solution.py:31
  117.2 11.8 %collective-permute-start.22 = (bf16[512,256]{1,0:T(8,128)(2,1)}, bf16[512,256]{1,0:T(8,128)(2,1)S(1)}, u32[]{:S(2)}, u32[]{:S(2)}) collective-permute-start(bf16[512,256]{1,0:T(8,128)(2,1)} %slice.56), channel_id=1, source_target_pairs={{0,12},{1,13},{2,14},{3,15},{4,0},{5,1},{6,2},{7,3},{8,4},{9,5},{1... | collective-permute-start | bytes 786440 | tf_op jit(solution)/shard_map/fourth_moves/ppermute | solution.py:31
  129.1 6.9 %collective-permute-start.25 = (bf16[512,256]{1,0:T(8,128)(2,1)S(1)}, bf16[512,256]{1,0:T(8,128)(2,1)S(1)}, u32[]{:S(2)}, u32[]{:S(2)}) collective-permute-start(bf16[512,256]{1,0:T(8,128)(2,1)S(1)} %slice.58), channel_id=1, source_target_pairs={{0,4},{1,5},{2,6},{3,7},{4,8},{5,9},{6,10},{7,11},{8,12},{9,13},{1... | collective-permute-start | bytes 786440 | tf_op jit(solution)/shard_map/fifth_moves/ppermute | solution.py:31
  129.2 6.8 %collective-permute-start.26 = (bf16[512,256]{1,0:T(8,128)(2,1)S(1)}, bf16[512,256]{1,0:T(8,128)(2,1)S(1)}, u32[]{:S(2)}, u32[]{:S(2)}) collective-permute-start(bf16[512,256]{1,0:T(8,128)(2,1)S(1)} %slice.59), channel_id=1, source_target_pairs={{0,12},{1,13},{2,14},{3,15},{4,0},{5,1},{6,2},{7,3},{8,4},{9,5},{1... | collective-permute-start | bytes 786440 | tf_op jit(solution)/shard_map/fifth_moves/ppermute | solution.py:31
  146.3 11.2 %copy-start.14 = (f32[256,1024]{1,0:T(8,128)S(1)}, f32[256,1024]{1,0:T(8,128)}, u32[]{:S(2)}) copy-start(f32[256,1024]{1,0:T(8,128)} %get-tuple-element.59.refs_12_) | copy-start | bytes 3145732
  146.3 11.7 %copy-start.34 = (f32[256,1024]{1,0:T(8,128)S(1)}, f32[256,1024]{1,0:T(8,128)}, u32[]{:S(2)}) copy-start(f32[256,1024]{1,0:T(8,128)} %get-tuple-element.72) | copy-start | bytes 3145732
  146.3 11.8 %copy-start.28 = (f32[32,256]{1,0:T(8,128)S(1)}, f32[32,256]{1,0:T(8,128)}, u32[]{:S(2)}) copy-start(f32[32,256]{1,0:T(8,128)} %convert_reduce_fusion.refs_21_) | copy-start | bytes 98308
  146.3 18.1 %copy-start.13 = (f32[256,1024]{1,0:T(8,128)S(1)}, f32[256,1024]{1,0:T(8,128)}, u32[]{:S(2)}) copy-start(f32[256,1024]{1,0:T(8,128)} %get-tuple-element.58) | copy-start | bytes 3145732
  157.5 7.3 %collective-permute-start.27 = (f32[512,896]{1,0:T(8,128)}, f32[512,896]{1,0:T(8,128)S(1)}, u32[]{:S(2)}, u32[]{:S(2)}) collective-permute-start(f32[512,896]{1,0:T(8,128)} %get-tuple-element.69), channel_id=1, source_target_pairs={{0,1},{1,0},{2,3},{3,2},{4,5},{5,4},{6,7},{7,6},{8,9},{9,8},{10,11... | collective-permute-start | bytes 5505032 | tf_op jit(solution)/shard_map/hidden/ppermute | solution.py:31
  157.6 6.8 %collective-permute-start.24 = (f32[256,1024]{1,0:T(8,128)S(1)}, f32[256,1024]{1,0:T(8,128)S(1)}, u32[]{:S(2)}, u32[]{:S(2)}) collective-permute-start(f32[256,1024]{1,0:T(8,128)S(1)} %copy-done.14), channel_id=1, source_target_pairs={{0,1},{1,0},{2,3},{3,2},{4,5},{5,4},{6,7},{7,6},{8,9},{9,8},{10,11... | collective-permute-start | bytes 3145736 | tf_op jit(solution)/shard_map/fifth_moves/ppermute | solution.py:31
  158.1 6.5 %collective-permute-start.28 = (f32[256,1024]{1,0:T(8,128)S(1)}, f32[256,1024]{1,0:T(8,128)S(1)}, u32[]{:S(2)}, u32[]{:S(2)}) collective-permute-start(f32[256,1024]{1,0:T(8,128)S(1)} %copy-done.34), channel_id=1, source_target_pairs={{0,1},{1,0},{2,3},{3,2},{4,5},{5,4},{6,7},{7,6},{8,9},{9,8},{10,11... | collective-permute-start | bytes 3145736 | tf_op jit(solution)/shard_map/fifth_moves/ppermute | solution.py:31
  158.2 6.2 %collective-permute-start.29 = (f32[32,256]{1,0:T(8,128)S(1)}, f32[32,256]{1,0:T(8,128)S(1)}, u32[]{:S(2)}, u32[]{:S(2)}) collective-permute-start(f32[32,256]{1,0:T(8,128)S(1)} %copy-done.28), channel_id=1, source_target_pairs={{0,1},{1,0},{2,3},{3,2},{4,5},{5,4},{6,7},{7,6},{8,9},{9,8},{10,11... | collective-permute-start | bytes 98312 | tf_op jit(solution)/shard_map/hidden/ppermute | solution.py:31
  167.7 15.2 %copy-start.31 = (f32[64,64]{1,0:T(8,128)S(1)}, f32[64,64]{1,0:T(8,128)}, u32[]{:S(2)}) copy-start(f32[64,64]{1,0:T(8,128)} %param.16) | copy-start | bytes 49156
  167.7 15.4 %copy-start.32 = (f32[64,64]{1,0:T(8,128)S(1)}, f32[64,64]{1,0:T(8,128)}, u32[]{:S(2)}) copy-start(f32[64,64]{1,0:T(8,128)} %param.17) | copy-start | bytes 49156
  167.8 14.8 %collective-permute-start.30 = (f32[96,256]{1,0:T(8,128)S(1)}, f32[96,256]{1,0:T(8,128)S(1)}, u32[]{:S(2)}, u32[]{:S(2)}) collective-permute-start(f32[96,256]{1,0:T(8,128)S(1)} %select_maximum_fusion), channel_id=1, source_target_pairs={{0,16},{1,17},{2,18},{3,19},{4,20},{5,21},{6,22},{7,23},{8,24},{9,... | collective-permute-start | bytes 294920 | tf_op jit(solution)/shard_map/finish/ppermute | solution.py:31
  (20 other events, 97.0 us)
Sparse Core Ops, SparseCore 0:
  37.7 46.8 all-gather.4
  95.7 47.9 all-gather.6

commit v4 on v3

--- a/solution.py
+++ b/solution.py
@@ -131,7 +131,7 @@
         for part, target in enumerate((keep, other)):
             @pl.when(i == part)
             def _():
-                target[...] = product
+                target[...] = product.astype(target.dtype)
 
 
 def hidden_kernel(*refs):
@@ -157,13 +157,13 @@
         for part, target in enumerate((keep, other)):
             @pl.when(i % 2 == part)
             def _():
-                target[place, :] = product
+                target[place, :] = product.astype(target.dtype)
 
 
 def call(kernel, args, shape, scratch, flops):
     return pl.pallas_call(
         kernel,
-        out_shape=[jax.ShapeDtypeStruct(shape, F32)] * 2,
+        out_shape=[jax.ShapeDtypeStruct(shape, F32), jax.ShapeDtypeStruct(shape, jnp.bfloat16)],
         in_specs=[pl.BlockSpec(memory_space=pltpu.MemorySpace.HBM)] * len(args),
         out_specs=[pl.BlockSpec(memory_space=pltpu.VMEM)] * 2,
         scratch_shapes=scratch,
@@ -250,14 +250,14 @@
     with jax.named_scope("fifth_moves"):
         fb3, fb4 = ring_far(fb1, fb2, "x")
         late = [far_a, fa1, fa2, fa3, fa4, far_b, fb1, fb2, fb3, fb4]
-        gate1 = gate_matmul(True, late, gates, in_proj, gate0[1])
-        downs, other = hold((downs, gate1[1]))
-        gate1 = [gate1[0], other]
-        gate_both = [keep + send(other, swap) for keep, other in (gate0, gate1)]
+        first = send(gate0[1], swap)
+        gate1 = gate_matmul(True, late, gates, in_proj, first)
     with jax.named_scope("hidden"):
+        hidden, other = hidden_matmul(early, late, downs, gate1[1])
+        gate_both = [gate0[0] + first.astype(F32), gate1[0] + send(gate1[1], swap).astype(F32)]
+        hidden = hidden + send(other, swap).astype(F32)
+        downs, other = hold((downs, other))
         sums = jnp.sum(downs[:, :, 896:].astype(F32).reshape(16, LANGS, 256), axis=0)
-        hidden, other = hidden_matmul(early, late, downs, sums)
-        hidden = hidden + send(other, swap)
         sums = sums + send(sums, swap)
 
     def finish(gate, hidden_grad):

time: 210 us -> 206 us (0.981)
  waiting for transfers between devices: 80.4 us -> 76.9 us
    ppermute x31, waiting for transfers between devices: 80.4 us -> 76.8 us  [send(): return lax.ppermute(v, AXES, perm_of(move))]
where the time goes in v4:
time: 206 us
  waiting for transfers between devices  76.9 us (37%)
  starting transfers between devices  57 us (28%)
  Pallas kernels  24.8 us (12%)
  blocking collectives  18.8 us (9%)
  between operations  14.1 us (7%)
  local copies, waits for them, and re-layouts  7.72 us (4%)
  other arithmetic  4.3 us (2%)
  matrix products  2.12 us (1%)
    ppermute x31, waiting for transfers between devices, send(): return lax.ppermute(v, AXES, perm_of(move))  76.8 us
    ppermute x31, starting transfers between devices, send(): return lax.ppermute(v, AXES, perm_of(move))  57 us
    pallas_call x3, Pallas kernels, call(): pl.pallas_call(kernel, out_shape=[jax.ShapeDtypeStruct(shape, F32), jax.S...  24.8 us
    all_to_all x1, blocking collectives, shards(): bands = lax.all_to_all(part.reshape(16, 256), 'mp', 0, 0, tiled=True)  10.5 us
    all_to_all x1, blocking collectives, everyone(): lax.all_to_all(jnp.broadcast_to(v[None], (16,) + v.shape), axis, 0, 0, ti...  8.32 us
  transfers between devices with their start and end apart: 33, of which 12 were waited for; matrix products, arithmetic and copies ran while one was open for 3% of the time, Pallas kernels for 7%

profile of v4, /device:TPU:1, one launch (start us, length us, event | category | flops | bytes accessed | tf_op | source)
XLA Modules:
  0.0 205.7 jit_solution(16587414162913827289)
XLA Ops:
  6.5 4.5 %collective-permute-start.5 = (bf16[256,896]{1,0:T(8,128)(2,1)}, bf16[256,896]{1,0:T(8,128)(2,1)S(1)}, u32[]{:S(2)}, u32[]{:S(2)}) collective-permute-start(bf16[256,896]{1,0:T(8,128)(2,1)} %param.12), channel_id=1, source_target_pairs={{0,32},{1,16},{2,34},{3,18},{4,36},{5,20},{6,38},{7,22},{8,40},{9,... | collective-permute-start | bytes 1376264 | tf_op jit(solution)/shard_map/first_moves/ppermute | solution.py:31
  11.0 5.1 %collective-permute-start.23 = (bf16[256,896]{1,0:T(8,128)(2,1)}, bf16[256,896]{1,0:T(8,128)(2,1)S(1)}, u32[]{:S(2)}, u32[]{:S(2)}) collective-permute-start(bf16[256,896]{1,0:T(8,128)(2,1)} %param.12), channel_id=1, source_target_pairs={{0,0},{1,48},{2,2},{3,50},{4,4},{5,52},{6,6},{7,54},{8,8},{9,56},{... | collective-permute-start | bytes 1376264 | tf_op jit(solution)/shard_map/first_moves/ppermute | solution.py:31
  16.1 15.4 %collective-permute-done.5 = bf16[256,896]{1,0:T(8,128)(2,1)S(1)} collective-permute-done((bf16[256,896]{1,0:T(8,128)(2,1)}, bf16[256,896]{1,0:T(8,128)(2,1)S(1)}, u32[]{:S(2)}, u32[]{:S(2)}) %collective-permute-start.5) | collective-permute-done | bytes 458784 | tf_op jit(solution)/shard_map/first_moves/ppermute | solution.py:31
  31.5 4.9 %collective-permute-done.23 = bf16[256,896]{1,0:T(8,128)(2,1)S(1)} collective-permute-done((bf16[256,896]{1,0:T(8,128)(2,1)}, bf16[256,896]{1,0:T(8,128)(2,1)S(1)}, u32[]{:S(2)}, u32[]{:S(2)}) %collective-permute-start.23) | collective-permute-done | bytes 458784 | tf_op jit(solution)/shard_map/first_moves/ppermute | solution.py:31
  36.5 1.1 pad_maximum_fusion.1
  37.7 0.8 collective-permute-start
  38.5 1.5 collective-permute-start.1
  40.0 1.2 collective-permute-start.2
  41.2 1.5 collective-permute-start.3
  43.2 1.2 pad.8.refs_11_
  45.3 3.3 %collective-permute-done.refs_5_ = bf16[1024,256]{1,0:T(8,128)(2,1)} collective-permute-done((bf16[1024,256]{1,0:T(8,128)(2,1)S(1)}, bf16[1024,256]{1,0:T(8,128)(2,1)}, u32[]{:S(2)}, u32[]{:S(2)}) %collective-permute-start) | collective-permute-done | bytes 524320 | tf_op jit(solution)/shard_map/first_moves/ppermute | solution.py:31
  48.6 2.7 %collective-permute-done.2.refs_1_ = bf16[1024,256]{1,0:T(8,128)(2,1)S(1)} collective-permute-done((bf16[1024,256]{1,0:T(8,128)(2,1)S(1)}, bf16[1024,256]{1,0:T(8,128)(2,1)S(1)}, u32[]{:S(2)}, u32[]{:S(2)}) %collective-permute-start.2) | collective-permute-done | bytes 524320 | tf_op jit(solution)/shard_map/first_moves/ppermute | solution.py:31
  51.6 4.6 %collective-permute-start.8 = (bf16[960,256]{1,0:T(8,128)(2,1)S(1)}, bf16[960,256]{1,0:T(8,128)(2,1)S(1)}, u32[]{:S(2)}, u32[]{:S(2)}) collective-permute-start(bf16[960,256]{1,0:T(8,128)(2,1)S(1)} %pad_maximum_fusion.3), channel_id=1, source_target_pairs={{0,32},{1,16},{2,34},{3,18},{4,36},{5,20},{6,38},{7,22},{8,40},{9,... | collective-permute-start | bytes 1474568 | tf_op jit(solution)/shard_map/second_moves/ppermute | solution.py:31
  56.2 1.2 collective-permute-start.10
  57.4 1.5 collective-permute-start.11
  58.9 0.7 collective-permute-start.6
  59.6 1.3 collective-permute-start.7
  60.9 16.9 %collective-permute-done.8 = bf16[960,256]{1,0:T(8,128)(2,1)S(1)} collective-permute-done((bf16[960,256]{1,0:T(8,128)(2,1)S(1)}, bf16[960,256]{1,0:T(8,128)(2,1)S(1)}, u32[]{:S(2)}, u32[]{:S(2)}) %collective-permute-start.8) | collective-permute-done | bytes 491552 | tf_op jit(solution)/shard_map/second_moves/ppermute | solution.py:31
  77.7 2.9 %collective-permute-start.9 = (bf16[960,256]{1,0:T(8,128)(2,1)S(1)}, bf16[960,256]{1,0:T(8,128)(2,1)S(1)}, u32[]{:S(2)}, u32[]{:S(2)}) collective-permute-start(bf16[960,256]{1,0:T(8,128)(2,1)S(1)} %pad_maximum_fusion.3), channel_id=1, source_target_pairs={{0,0},{1,48},{2,2},{3,50},{4,4},{5,52},{6,6},{7,54},{8,8},{9,56},{... | collective-permute-start | bytes 1474568 | tf_op jit(solution)/shard_map/second_moves/ppermute | solution.py:31
  80.6 13.7 %collective-permute-done.9 = bf16[960,256]{1,0:T(8,128)(2,1)S(1)} collective-permute-done((bf16[960,256]{1,0:T(8,128)(2,1)S(1)}, bf16[960,256]{1,0:T(8,128)(2,1)S(1)}, u32[]{:S(2)}, u32[]{:S(2)}) %collective-permute-start.9) | collective-permute-done | bytes 491552 | tf_op jit(solution)/shard_map/second_moves/ppermute | solution.py:31
  94.4 1.2 pad_maximum_fusion
  95.8 2.7 %collective-permute-start.18 = (bf16[512,256]{1,0:T(8,128)(2,1)S(1)}, bf16[512,256]{1,0:T(8,128)(2,1)S(1)}, u32[]{:S(2)}, u32[]{:S(2)}) collective-permute-start(bf16[512,256]{1,0:T(8,128)(2,1)S(1)} %slice.54), channel_id=1, source_target_pairs={{0,12},{1,13},{2,14},{3,15},{4,0},{5,1},{6,2},{7,3},{8,4},{9,5},{1... | collective-permute-start | bytes 786440 | tf_op jit(solution)/shard_map/third_moves/ppermute | solution.py:31
  98.7 2.7 %collective-permute-start.14 = (bf16[1024,256]{1,0:T(8,128)(2,1)S(1)}, bf16[1024,256]{1,0:T(8,128)(2,1)S(1)}, u32[]{:S(2)}, u32[]{:S(2)}) collective-permute-start(bf16[1024,256]{1,0:T(8,128)(2,1)S(1)} %broadcast_select_fusion.1.refs_0_.refs_10_), channel_id=1, source_target_pairs={{0,12},{1,13},{2,14},{3,15},{4,0},{5,1},{6,2},{7,3},{8,4},{9,5},{1... | collective-permute-start | bytes 1572872 | tf_op jit(solution)/shard_map/third_moves/ppermute | solution.py:31
  101.3 1.3 collective-permute-start.12
  102.8 2.6 %collective-permute-start.16 = (bf16[512,256]{1,0:T(8,128)(2,1)S(1)}, bf16[512,256]{1,0:T(8,128)(2,1)S(1)}, u32[]{:S(2)}, u32[]{:S(2)}) collective-permute-start(bf16[512,256]{1,0:T(8,128)(2,1)S(1)} %slice.52), channel_id=1, source_target_pairs={{0,12},{1,13},{2,14},{3,15},{4,0},{5,1},{6,2},{7,3},{8,4},{9,5},{1... | collective-permute-start | bytes 786440 | tf_op jit(solution)/shard_map/third_moves/ppermute | solution.py:31
  105.5 6.7 %collective-permute-done.15.refs_8_ = bf16[512,256]{1,0:T(8,128)(2,1)S(1)} collective-permute-done((bf16[512,256]{1,0:T(8,128)(2,1)S(1)}, bf16[512,256]{1,0:T(8,128)(2,1)S(1)}, u32[]{:S(2)}, u32[]{:S(2)}) %collective-permute-start.15) | collective-permute-done | bytes 262176 | tf_op jit(solution)/shard_map/third_moves/ppermute | solution.py:31
  112.2 0.7 copy-done.21
  113.0 0.9 collective-permute-start.19
  114.0 1.8 collective-permute-start.20
  115.8 0.7 slice.55
  116.5 0.8 slice.56
  117.3 2.7 %collective-permute-start.22 = (bf16[512,256]{1,0:T(8,128)(2,1)}, bf16[512,256]{1,0:T(8,128)(2,1)S(1)}, u32[]{:S(2)}, u32[]{:S(2)}) collective-permute-start(bf16[512,256]{1,0:T(8,128)(2,1)} %slice.56), channel_id=1, source_target_pairs={{0,12},{1,13},{2,14},{3,15},{4,0},{5,1},{6,2},{7,3},{8,4},{9,5},{1... | collective-permute-start | bytes 786440 | tf_op jit(solution)/shard_map/fourth_moves/ppermute | solution.py:31
  120.0 7.0 %fourth_moves.1 = (f32[256,1024]{1,0:T(8,128)}, bf16[256,1024]{1,0:T(8,128)(2,1)}) custom-call(bf16[1024,256]{1,0:T(8,128)(2,1)} %copy-done.4, bf16[1024,256]{1,0:T(8,128)(2,1)} %copy-done.8, bf16[1024,256]{1,0:T(8,128)(2,1)} %copy-done.9, bf16[512,256]{1,0:T(8,128)(2,1)} %copy-done.19, bf16[512,256]{1,0:T(8,128)(2,1)} %copy-done.20, ...), custom_call_target="tpu_custom_call" | custom-call | flops 2147483648 | bytes 8388608 | tf_op jit(solution)/shard_map/fourth_moves/pallas_call | solution.py:164
  127.0 0.9 collective-permute-done.21.refs_3_.refs_13_
  128.3 2.7 %collective-permute-start.26 = (bf16[512,256]{1,0:T(8,128)(2,1)S(1)}, bf16[512,256]{1,0:T(8,128)(2,1)S(1)}, u32[]{:S(2)}, u32[]{:S(2)}) collective-permute-start(bf16[512,256]{1,0:T(8,128)(2,1)S(1)} %slice.59), channel_id=1, source_target_pairs={{0,12},{1,13},{2,14},{3,15},{4,0},{5,1},{6,2},{7,3},{8,4},{9,5},{1... | collective-permute-start | bytes 786440 | tf_op jit(solution)/shard_map/fifth_moves/ppermute | solution.py:31
  131.1 6.0 %collective-permute-done.25.refs_8_.refs_18_ = bf16[512,256]{1,0:T(8,128)(2,1)S(1)} collective-permute-done((bf16[512,256]{1,0:T(8,128)(2,1)S(1)}, bf16[512,256]{1,0:T(8,128)(2,1)S(1)}, u32[]{:S(2)}, u32[]{:S(2)}) %collective-permute-start.25) | collective-permute-done | bytes 262176 | tf_op jit(solution)/shard_map/fifth_moves/ppermute | solution.py:31
  137.1 0.7 copy-done.25
  137.8 0.8 copy-done.2
  138.7 6.9 %fifth_moves.1 = (f32[256,1024]{1,0:T(8,128)}, bf16[256,1024]{1,0:T(8,128)(2,1)}) custom-call(bf16[1024,256]{1,0:T(8,128)(2,1)} %copy-done.5, bf16[1024,256]{1,0:T(8,128)(2,1)} %copy-done.1, bf16[1024,256]{1,0:T(8,128)(2,1)} %copy-done.12, bf16[512,256]{1,0:T(8,128)(2,1)} %copy-done.23, bf16[512,256]{1,0:T(8,128)(2,1)} %copy-done.24, ...), custom_call_target="tpu_custom_call" | custom-call | flops 2147483648 | bytes 8388608 | tf_op jit(solution)/shard_map/fifth_moves/pallas_call | solution.py:164
  145.7 10.8 %hidden.1 = (f32[512,896]{1,0:T(8,128)}, bf16[512,896]{1,0:T(8,128)(2,1)}) custom-call(bf16[1024,256]{1,0:T(8,128)(2,1)} %copy-done.4, bf16[1024,256]{1,0:T(8,128)(2,1)} %copy-done.8, bf16[1024,256]{1,0:T(8,128)(2,1)} %copy-done.9, bf16[512,256]{1,0:T(8,128)(2,1)} %copy-done.19, bf16[512,256]{1,0:T(8,128)(2,1)} %copy-done.20, ...), custom_call_target="tpu_custom_call" | custom-call | flops 3758096384 | bytes 8388608 | tf_op jit(solution)/shard_map/hidden/pallas_call | solution.py:164
  156.5 1.2 collective-permute-start.27
  157.9 1.0 slice.65
  159.5 1.1 collective-permute-done.29
  161.2 0.7 copy-done.30
  162.7 10.5 %collective-permute-start.30 = (f32[96,256]{1,0:T(8,128)S(1)}, f32[96,256]{1,0:T(8,128)S(1)}, u32[]{:S(2)}, u32[]{:S(2)}) collective-permute-start(f32[96,256]{1,0:T(8,128)S(1)} %select_maximum_fusion), channel_id=1, source_target_pairs={{0,16},{1,17},{2,18},{3,19},{4,20},{5,21},{6,22},{7,23},{8,24},{9,... | collective-permute-start | bytes 294920 | tf_op jit(solution)/shard_map/finish/ppermute | solution.py:31
  173.6 4.8 %collective-permute-done.30 = f32[96,256]{1,0:T(8,128)S(1)} collective-permute-done((f32[96,256]{1,0:T(8,128)S(1)}, f32[96,256]{1,0:T(8,128)S(1)}, u32[]{:S(2)}, u32[]{:S(2)}) %collective-permute-start.30) | collective-permute-done | bytes 98336 | tf_op jit(solution)/shard_map/finish/ppermute | solution.py:31
  179.4 10.5 %all_to_all.16 = f32[16,1,256]{2,1,0:T(1,128)S(1)} all-to-all(f32[16,1,256]{2,1,0:T(1,128)S(1)} %all_to_all.13), channel_id=1, replica_groups=mesh['dp'=16,'mp'=16] {'mp'}, dimensions={0} | all-to-all | bytes 32768 | tf_op jit(solution)/shard_map/finish/all_to_all | solution.py:279
  190.0 8.3 %all_to_all.17 = f32[16,1,32]{2,1,0:T(1,128)S(1)} all-to-all(f32[16,1,32]{2,1,0:T(1,128)S(1)} %broadcast_in_dim.2), channel_id=1, replica_groups=mesh['dp'=16,'mp'=16] {'mp'}, dimensions={0} | all-to-all | bytes 4096 | tf_op jit(solution)/shard_map/finish/all_to_all | solution.py:198
  (133 shorter events, 6.9 us)
Async XLA Ops:
  6.5 37.9 %copy-start = (bf16[128,256]{1,0:T(8,128)(2,1)S(1)}, bf16[128,256]{1,0:T(8,128)(2,1)}, u32[]{:S(2)}) copy-start(bf16[128,256]{1,0:T(8,128)(2,1)} %param.18) | copy-start | bytes 196612
  6.5 31.1 %copy-start.28 = (bf16[1,512,256]{2,1,0:T(8,128)(2,1)S(1)}, bf16[1,512,256]{2,1,0:T(8,128)(2,1)}, u32[]{:S(2)}) copy-start(bf16[1,512,256]{2,1,0:T(8,128)(2,1)} %param.10) | copy-start | bytes 786436
  6.5 31.1 %copy-start.27 = (bf16[1,512,256]{2,1,0:T(8,128)(2,1)S(1)}, bf16[1,512,256]{2,1,0:T(8,128)(2,1)}, u32[]{:S(2)}) copy-start(bf16[1,512,256]{2,1,0:T(8,128)(2,1)} %param.11) | copy-start | bytes 786436
  6.5 113.4 %all-gather.5.cloned.1.call-start = ((), (), s32[]{:S(2)}) async-start(), calls=%async_computation.2 | async-start | bytes 4587520 | tf_op jit(solution)/shard_map/first_moves/all_gather | solution.py:223
  6.5 25.0 %collective-permute-start.5 = (bf16[256,896]{1,0:T(8,128)(2,1)}, bf16[256,896]{1,0:T(8,128)(2,1)S(1)}, u32[]{:S(2)}, u32[]{:S(2)}) collective-permute-start(bf16[256,896]{1,0:T(8,128)(2,1)} %param.12), channel_id=1, source_target_pairs={{0,32},{1,16},{2,34},{3,18},{4,36},{5,20},{6,38},{7,22},{8,40},{9,... | collective-permute-start | bytes 1376264 | tf_op jit(solution)/shard_map/first_moves/ppermute | solution.py:31
  11.0 25.5 %collective-permute-start.23 = (bf16[256,896]{1,0:T(8,128)(2,1)}, bf16[256,896]{1,0:T(8,128)(2,1)S(1)}, u32[]{:S(2)}, u32[]{:S(2)}) collective-permute-start(bf16[256,896]{1,0:T(8,128)(2,1)} %param.12), channel_id=1, source_target_pairs={{0,0},{1,48},{2,2},{3,50},{4,4},{5,52},{6,6},{7,54},{8,8},{9,56},{... | collective-permute-start | bytes 1376264 | tf_op jit(solution)/shard_map/first_moves/ppermute | solution.py:31
  37.6 108.0 %all-gather.7.cloned.1.call-start = ((), (), s32[]{:S(2)}) async-start(), calls=%async_computation.3 | async-start | bytes 4915200 | tf_op jit(solution)/shard_map/third_moves/all_gather | solution.py:236
  37.7 10.8 %collective-permute-start = (bf16[1024,256]{1,0:T(8,128)(2,1)S(1)}, bf16[1024,256]{1,0:T(8,128)(2,1)}, u32[]{:S(2)}, u32[]{:S(2)}) collective-permute-start(bf16[1024,256]{1,0:T(8,128)(2,1)S(1)} %pad_maximum_fusion.2.refs_0_), channel_id=1, source_target_pairs={{0,2},{1,3},{2,0},{3,1},{4,6},{5,7},{6,4},{7,5},{8,10},{9,11},{10,... | collective-permute-start | bytes 1572872 | tf_op jit(solution)/shard_map/first_moves/ppermute | solution.py:31
  38.5 10.1 %collective-permute-start.1 = (bf16[1024,256]{1,0:T(8,128)(2,1)S(1)}, bf16[1024,256]{1,0:T(8,128)(2,1)}, u32[]{:S(2)}, u32[]{:S(2)}) collective-permute-start(bf16[1024,256]{1,0:T(8,128)(2,1)S(1)} %pad_maximum_fusion.2.refs_0_), channel_id=1, source_target_pairs={{2,16},{3,17},{6,20},{7,21},{10,24},{11,25},{14,28},{15,29},{16,2}... | collective-permute-start | bytes 1572872 | tf_op jit(solution)/shard_map/first_moves/ppermute | solution.py:31
  40.0 11.3 %collective-permute-start.2 = (bf16[1024,256]{1,0:T(8,128)(2,1)S(1)}, bf16[1024,256]{1,0:T(8,128)(2,1)S(1)}, u32[]{:S(2)}, u32[]{:S(2)}) collective-permute-start(bf16[1024,256]{1,0:T(8,128)(2,1)S(1)} %pad_maximum_fusion.2.refs_0_), channel_id=1, source_target_pairs={{0,4},{1,5},{2,6},{3,7},{4,8},{5,9},{6,10},{7,11},{8,12},{9,13},{1... | collective-permute-start | bytes 1572872 | tf_op jit(solution)/shard_map/first_moves/ppermute | solution.py:31
  41.2 10.4 %collective-permute-start.3 = (bf16[1024,256]{1,0:T(8,128)(2,1)S(1)}, bf16[1024,256]{1,0:T(8,128)(2,1)S(1)}, u32[]{:S(2)}, u32[]{:S(2)}) collective-permute-start(bf16[1024,256]{1,0:T(8,128)(2,1)S(1)} %pad_maximum_fusion.2.refs_0_), channel_id=1, source_target_pairs={{0,12},{1,13},{2,14},{3,15},{4,0},{5,1},{6,2},{7,3},{8,4},{9,5},{1... | collective-permute-start | bytes 1572872 | tf_op jit(solution)/shard_map/first_moves/ppermute | solution.py:31
  42.6 1.9 collective-permute-start.4
  51.3 44.4 %copy-start.8 = (bf16[1024,256]{1,0:T(8,128)(2,1)}, bf16[1024,256]{1,0:T(8,128)(2,1)S(1)}, u32[]{:S(2)}) copy-start(bf16[1024,256]{1,0:T(8,128)(2,1)S(1)} %collective-permute-done.2.refs_1_) | copy-start | bytes 1572868
  51.6 44.2 %copy-start.9 = (bf16[1024,256]{1,0:T(8,128)(2,1)}, bf16[1024,256]{1,0:T(8,128)(2,1)S(1)}, u32[]{:S(2)}) copy-start(bf16[1024,256]{1,0:T(8,128)(2,1)S(1)} %collective-permute-done.3.refs_2_) | copy-start | bytes 1572868
  51.6 26.1 %collective-permute-start.8 = (bf16[960,256]{1,0:T(8,128)(2,1)S(1)}, bf16[960,256]{1,0:T(8,128)(2,1)S(1)}, u32[]{:S(2)}, u32[]{:S(2)}) collective-permute-start(bf16[960,256]{1,0:T(8,128)(2,1)S(1)} %pad_maximum_fusion.3), channel_id=1, source_target_pairs={{0,32},{1,16},{2,34},{3,18},{4,36},{5,20},{6,38},{7,22},{8,40},{9,... | collective-permute-start | bytes 1474568 | tf_op jit(solution)/shard_map/second_moves/ppermute | solution.py:31
  56.2 38.1 %collective-permute-start.10 = (bf16[1024,256]{1,0:T(8,128)(2,1)}, bf16[1024,256]{1,0:T(8,128)(2,1)S(1)}, u32[]{:S(2)}, u32[]{:S(2)}) collective-permute-start(bf16[1024,256]{1,0:T(8,128)(2,1)} %collective-permute-done.refs_5_), channel_id=1, source_target_pairs={{0,4},{1,5},{2,6},{3,7},{4,8},{5,9},{6,10},{7,11},{8,12},{9,13},{1... | collective-permute-start | bytes 1572872 | tf_op jit(solution)/shard_map/second_moves/ppermute | solution.py:31
  57.4 36.9 %collective-permute-start.11 = (bf16[1024,256]{1,0:T(8,128)(2,1)}, bf16[1024,256]{1,0:T(8,128)(2,1)S(1)}, u32[]{:S(2)}, u32[]{:S(2)}) collective-permute-start(bf16[1024,256]{1,0:T(8,128)(2,1)} %collective-permute-done.refs_5_), channel_id=1, source_target_pairs={{0,12},{1,13},{2,14},{3,15},{4,0},{5,1},{6,2},{7,3},{8,4},{9,5},{1... | collective-permute-start | bytes 1572872 | tf_op jit(solution)/shard_map/second_moves/ppermute | solution.py:31
  58.9 35.5 %collective-permute-start.6 = (bf16[1024,256]{1,0:T(8,128)(2,1)}, bf16[1024,256]{1,0:T(8,128)(2,1)S(1)}, u32[]{:S(2)}, u32[]{:S(2)}) collective-permute-start(bf16[1024,256]{1,0:T(8,128)(2,1)} %collective-permute-done.refs_5_), channel_id=1, source_target_pairs={{2,16},{3,17},{6,20},{7,21},{10,24},{11,25},{14,28},{15,29},{16,2}... | collective-permute-start | bytes 1572872 | tf_op jit(solution)/shard_map/second_moves/ppermute | solution.py:31
  59.6 34.8 %collective-permute-start.7 = (bf16[1024,256]{1,0:T(8,128)(2,1)}, bf16[1024,256]{1,0:T(8,128)(2,1)S(1)}, u32[]{:S(2)}, u32[]{:S(2)}) collective-permute-start(bf16[1024,256]{1,0:T(8,128)(2,1)} %collective-permute-done.1), channel_id=1, source_target_pairs={{2,0},{3,1},{6,4},{7,5},{10,8},{11,9},{14,12},{15,13},{16,18},{17,... | collective-permute-start | bytes 1572872 | tf_op jit(solution)/shard_map/second_moves/ppermute | solution.py:31
  77.7 16.6 %collective-permute-start.9 = (bf16[960,256]{1,0:T(8,128)(2,1)S(1)}, bf16[960,256]{1,0:T(8,128)(2,1)S(1)}, u32[]{:S(2)}, u32[]{:S(2)}) collective-permute-start(bf16[960,256]{1,0:T(8,128)(2,1)S(1)} %pad_maximum_fusion.3), channel_id=1, source_target_pairs={{0,0},{1,48},{2,2},{3,50},{4,4},{5,52},{6,6},{7,54},{8,8},{9,56},{... | collective-permute-start | bytes 1474568 | tf_op jit(solution)/shard_map/second_moves/ppermute | solution.py:31
  95.6 7.1 %collective-permute-start.17 = (bf16[512,256]{1,0:T(8,128)(2,1)S(1)}, bf16[512,256]{1,0:T(8,128)(2,1)S(1)}, u32[]{:S(2)}, u32[]{:S(2)}) collective-permute-start(bf16[512,256]{1,0:T(8,128)(2,1)S(1)} %slice.53), channel_id=1, source_target_pairs={{0,4},{1,5},{2,6},{3,7},{4,8},{5,9},{6,10},{7,11},{8,12},{9,13},{1... | collective-permute-start | bytes 786440 | tf_op jit(solution)/shard_map/third_moves/ppermute | solution.py:31
  95.8 7.0 %collective-permute-start.18 = (bf16[512,256]{1,0:T(8,128)(2,1)S(1)}, bf16[512,256]{1,0:T(8,128)(2,1)S(1)}, u32[]{:S(2)}, u32[]{:S(2)}) collective-permute-start(bf16[512,256]{1,0:T(8,128)(2,1)S(1)} %slice.54), channel_id=1, source_target_pairs={{0,12},{1,13},{2,14},{3,15},{4,0},{5,1},{6,2},{7,3},{8,4},{9,5},{1... | collective-permute-start | bytes 786440 | tf_op jit(solution)/shard_map/third_moves/ppermute | solution.py:31
  98.6 18.7 %copy-start.5 = (bf16[1024,256]{1,0:T(8,128)(2,1)}, bf16[1024,256]{1,0:T(8,128)(2,1)S(1)}, u32[]{:S(2)}) copy-start(bf16[1024,256]{1,0:T(8,128)(2,1)S(1)} %broadcast_select_fusion.1.refs_0_.refs_10_) | copy-start | bytes 1572868
  98.6 13.6 %collective-permute-start.13 = (bf16[1024,256]{1,0:T(8,128)(2,1)S(1)}, bf16[1024,256]{1,0:T(8,128)(2,1)S(1)}, u32[]{:S(2)}, u32[]{:S(2)}) collective-permute-start(bf16[1024,256]{1,0:T(8,128)(2,1)S(1)} %broadcast_select_fusion.1.refs_0_.refs_10_), channel_id=1, source_target_pairs={{0,4},{1,5},{2,6},{3,7},{4,8},{5,9},{6,10},{7,11},{8,12},{9,13},{1... | collective-permute-start | bytes 1572872 | tf_op jit(solution)/shard_map/third_moves/ppermute | solution.py:31
  98.7 13.5 %collective-permute-start.14 = (bf16[1024,256]{1,0:T(8,128)(2,1)S(1)}, bf16[1024,256]{1,0:T(8,128)(2,1)S(1)}, u32[]{:S(2)}, u32[]{:S(2)}) collective-permute-start(bf16[1024,256]{1,0:T(8,128)(2,1)S(1)} %broadcast_select_fusion.1.refs_0_.refs_10_), channel_id=1, source_target_pairs={{0,12},{1,13},{2,14},{3,15},{4,0},{5,1},{6,2},{7,3},{8,4},{9,5},{1... | collective-permute-start | bytes 1572872 | tf_op jit(solution)/shard_map/third_moves/ppermute | solution.py:31
  101.3 10.9 %collective-permute-start.12 = (bf16[1024,256]{1,0:T(8,128)(2,1)S(1)}, bf16[1024,256]{1,0:T(8,128)(2,1)S(1)}, u32[]{:S(2)}, u32[]{:S(2)}) collective-permute-start(bf16[1024,256]{1,0:T(8,128)(2,1)S(1)} %collective-permute-done.6), channel_id=1, source_target_pairs={{2,0},{3,1},{6,4},{7,5},{10,8},{11,9},{14,12},{15,13},{16,18},{17,... | collective-permute-start | bytes 1572872 | tf_op jit(solution)/shard_map/third_moves/ppermute | solution.py:31
  102.7 17.3 %copy-start.19 = (bf16[512,256]{1,0:T(8,128)(2,1)}, bf16[512,256]{1,0:T(8,128)(2,1)S(1)}, u32[]{:S(2)}) copy-start(bf16[512,256]{1,0:T(8,128)(2,1)S(1)} %collective-permute-done.17.refs_3_) | copy-start | bytes 786436
  102.7 9.5 %collective-permute-start.15 = (bf16[512,256]{1,0:T(8,128)(2,1)S(1)}, bf16[512,256]{1,0:T(8,128)(2,1)S(1)}, u32[]{:S(2)}, u32[]{:S(2)}) collective-permute-start(bf16[512,256]{1,0:T(8,128)(2,1)S(1)} %slice.51), channel_id=1, source_target_pairs={{0,4},{1,5},{2,6},{3,7},{4,8},{5,9},{6,10},{7,11},{8,12},{9,13},{1... | collective-permute-start | bytes 786440 | tf_op jit(solution)/shard_map/third_moves/ppermute | solution.py:31
  102.8 10.2 %copy-start.20 = (bf16[512,256]{1,0:T(8,128)(2,1)}, bf16[512,256]{1,0:T(8,128)(2,1)S(1)}, u32[]{:S(2)}) copy-start(bf16[512,256]{1,0:T(8,128)(2,1)S(1)} %collective-permute-done.18.refs_4_) | copy-start | bytes 786436
  102.8 9.4 %collective-permute-start.16 = (bf16[512,256]{1,0:T(8,128)(2,1)S(1)}, bf16[512,256]{1,0:T(8,128)(2,1)S(1)}, u32[]{:S(2)}, u32[]{:S(2)}) collective-permute-start(bf16[512,256]{1,0:T(8,128)(2,1)S(1)} %slice.52), channel_id=1, source_target_pairs={{0,12},{1,13},{2,14},{3,15},{4,0},{5,1},{6,2},{7,3},{8,4},{9,5},{1... | collective-permute-start | bytes 786440 | tf_op jit(solution)/shard_map/third_moves/ppermute | solution.py:31
  112.2 14.8 %copy-start.12 = (bf16[1024,256]{1,0:T(8,128)(2,1)}, bf16[1024,256]{1,0:T(8,128)(2,1)S(1)}, u32[]{:S(2)}) copy-start(bf16[1024,256]{1,0:T(8,128)(2,1)S(1)} %collective-permute-done.14.refs_2_.refs_12_) | copy-start | bytes 1572868
  113.0 14.0 %copy-start.6 = (bf16[1024,256]{1,0:T(8,128)(2,1)}, bf16[1024,256]{1,0:T(8,128)(2,1)S(1)}, u32[]{:S(2)}) copy-start(bf16[1024,256]{1,0:T(8,128)(2,1)S(1)} %broadcast_select_fusion.refs_5_.refs_15_) | copy-start | bytes 1572868
  113.0 14.9 %collective-permute-start.19 = (bf16[1024,256]{1,0:T(8,128)(2,1)S(1)}, bf16[1024,256]{1,0:T(8,128)(2,1)S(1)}, u32[]{:S(2)}, u32[]{:S(2)}) collective-permute-start(bf16[1024,256]{1,0:T(8,128)(2,1)S(1)} %broadcast_select_fusion.refs_5_.refs_15_), channel_id=1, source_target_pairs={{0,4},{1,5},{2,6},{3,7},{4,8},{5,9},{6,10},{7,11},{8,12},{9,13},{1... | collective-permute-start | bytes 1572872 | tf_op jit(solution)/shard_map/fourth_moves/ppermute | solution.py:31
  114.0 14.0 %collective-permute-start.20 = (bf16[1024,256]{1,0:T(8,128)(2,1)S(1)}, bf16[1024,256]{1,0:T(8,128)(2,1)S(1)}, u32[]{:S(2)}, u32[]{:S(2)}) collective-permute-start(bf16[1024,256]{1,0:T(8,128)(2,1)S(1)} %broadcast_select_fusion.refs_5_.refs_15_), channel_id=1, source_target_pairs={{0,12},{1,13},{2,14},{3,15},{4,0},{5,1},{6,2},{7,3},{8,4},{9,5},{1... | collective-permute-start | bytes 1572872 | tf_op jit(solution)/shard_map/fourth_moves/ppermute | solution.py:31
  116.5 11.4 %collective-permute-start.21 = (bf16[512,256]{1,0:T(8,128)(2,1)}, bf16[512,256]{1,0:T(8,128)(2,1)S(1)}, u32[]{:S(2)}, u32[]{:S(2)}) collective-permute-start(bf16[512,256]{1,0:T(8,128)(2,1)} %slice.55), channel_id=1, source_target_pairs={{0,4},{1,5},{2,6},{3,7},{4,8},{5,9},{6,10},{7,11},{8,12},{9,13},{1... | collective-permute-start | bytes 786440 | tf_op jit(solution)/shard_map/fourth_moves/ppermute | solution.py:31
  117.3 10.7 %collective-permute-start.22 = (bf16[512,256]{1,0:T(8,128)(2,1)}, bf16[512,256]{1,0:T(8,128)(2,1)S(1)}, u32[]{:S(2)}, u32[]{:S(2)}) collective-permute-start(bf16[512,256]{1,0:T(8,128)(2,1)} %slice.56), channel_id=1, source_target_pairs={{0,12},{1,13},{2,14},{3,15},{4,0},{5,1},{6,2},{7,3},{8,4},{9,5},{1... | collective-permute-start | bytes 786440 | tf_op jit(solution)/shard_map/fourth_moves/ppermute | solution.py:31
  128.0 9.1 %collective-permute-start.24 = (bf16[256,1024]{1,0:T(8,128)(2,1)}, bf16[256,1024]{1,0:T(8,128)(2,1)S(1)}, u32[]{:S(2)}, u32[]{:S(2)}) collective-permute-start(bf16[256,1024]{1,0:T(8,128)(2,1)} %get-tuple-element.58), channel_id=1, source_target_pairs={{0,1},{1,0},{2,3},{3,2},{4,5},{5,4},{6,7},{7,6},{8,9},{9,8},{10,11... | collective-permute-start | bytes 1572872 | tf_op jit(solution)/shard_map/fifth_moves/ppermute | solution.py:31
  128.1 8.9 %collective-permute-start.25 = (bf16[512,256]{1,0:T(8,128)(2,1)S(1)}, bf16[512,256]{1,0:T(8,128)(2,1)S(1)}, u32[]{:S(2)}, u32[]{:S(2)}) collective-permute-start(bf16[512,256]{1,0:T(8,128)(2,1)S(1)} %slice.58), channel_id=1, source_target_pairs={{0,4},{1,5},{2,6},{3,7},{4,8},{5,9},{6,10},{7,11},{8,12},{9,13},{1... | collective-permute-start | bytes 786440 | tf_op jit(solution)/shard_map/fifth_moves/ppermute | solution.py:31
  128.3 8.7 %collective-permute-start.26 = (bf16[512,256]{1,0:T(8,128)(2,1)S(1)}, bf16[512,256]{1,0:T(8,128)(2,1)S(1)}, u32[]{:S(2)}, u32[]{:S(2)}) collective-permute-start(bf16[512,256]{1,0:T(8,128)(2,1)S(1)} %slice.59), channel_id=1, source_target_pairs={{0,12},{1,13},{2,14},{3,15},{4,0},{5,1},{6,2},{7,3},{8,4},{9,5},{1... | collective-permute-start | bytes 786440 | tf_op jit(solution)/shard_map/fifth_moves/ppermute | solution.py:31
  145.6 12.1 %copy-start.34 = (bf16[256,1024]{1,0:T(8,128)(2,1)S(1)}, bf16[256,1024]{1,0:T(8,128)(2,1)}, u32[]{:S(2)}) copy-start(bf16[256,1024]{1,0:T(8,128)(2,1)} %get-tuple-element.65.refs_21_) | copy-start | bytes 1572868
  145.6 13.7 %copy-start.3 = (bf16[256,1024]{1,0:T(8,128)(2,1)S(1)}, bf16[256,1024]{1,0:T(8,128)(2,1)}, u32[]{:S(2)}) copy-start(bf16[256,1024]{1,0:T(8,128)(2,1)} %copy-done.2) | copy-start | bytes 1572868
  145.6 13.7 %copy-start.15 = (f32[256,1024]{1,0:T(8,128)S(1)}, f32[256,1024]{1,0:T(8,128)}, u32[]{:S(2)}) copy-start(f32[256,1024]{1,0:T(8,128)} %get-tuple-element.57) | copy-start | bytes 3145732
  156.5 4.3 %collective-permute-start.27 = (bf16[512,896]{1,0:T(8,128)(2,1)}, bf16[512,896]{1,0:T(8,128)(2,1)S(1)}, u32[]{:S(2)}, u32[]{:S(2)}) collective-permute-start(bf16[512,896]{1,0:T(8,128)(2,1)} %get-tuple-element.67), channel_id=1, source_target_pairs={{0,1},{1,0},{2,3},{3,2},{4,5},{5,4},{6,7},{7,6},{8,9},{9,8},{10,11... | collective-permute-start | bytes 2752520 | tf_op jit(solution)/shard_map/hidden/ppermute | solution.py:31
  157.7 2.9 %collective-permute-start.28 = (bf16[256,1024]{1,0:T(8,128)(2,1)S(1)}, bf16[256,1024]{1,0:T(8,128)(2,1)S(1)}, u32[]{:S(2)}, u32[]{:S(2)}) collective-permute-start(bf16[256,1024]{1,0:T(8,128)(2,1)S(1)} %copy-done.34), channel_id=1, source_target_pairs={{0,1},{1,0},{2,3},{3,2},{4,5},{5,4},{6,7},{7,6},{8,9},{9,8},{10,11... | collective-permute-start | bytes 1572872 | tf_op jit(solution)/shard_map/hidden/ppermute | solution.py:31
  158.9 1.8 collective-permute-start.29
  162.7 16.1 %copy-start.31 = (f32[64,64]{1,0:T(8,128)S(1)}, f32[64,64]{1,0:T(8,128)}, u32[]{:S(2)}) copy-start(f32[64,64]{1,0:T(8,128)} %param.16) | copy-start | bytes 49156
  162.7 16.3 %copy-start.32 = (f32[64,64]{1,0:T(8,128)S(1)}, f32[64,64]{1,0:T(8,128)}, u32[]{:S(2)}) copy-start(f32[64,64]{1,0:T(8,128)} %param.17) | copy-start | bytes 49156
  162.7 15.7 %collective-permute-start.30 = (f32[96,256]{1,0:T(8,128)S(1)}, f32[96,256]{1,0:T(8,128)S(1)}, u32[]{:S(2)}, u32[]{:S(2)}) collective-permute-start(f32[96,256]{1,0:T(8,128)S(1)} %select_maximum_fusion), channel_id=1, source_target_pairs={{0,16},{1,17},{2,18},{3,19},{4,20},{5,21},{6,22},{7,23},{8,24},{9,... | collective-permute-start | bytes 294920 | tf_op jit(solution)/shard_map/finish/ppermute | solution.py:31
  (20 other events, 93.4 us)
Sparse Core Ops, SparseCore 0:
  37.7 46.8 all-gather.4
  95.7 47.9 all-gather.6

commit v5 on v4

--- a/solution.py
+++ b/solution.py
@@ -163,7 +163,7 @@
 def call(kernel, args, shape, scratch, flops):
     return pl.pallas_call(
         kernel,
-        out_shape=[jax.ShapeDtypeStruct(shape, F32), jax.ShapeDtypeStruct(shape, jnp.bfloat16)],
+        out_shape=[jax.ShapeDtypeStruct(shape, F32)] * 2,
         in_specs=[pl.BlockSpec(memory_space=pltpu.MemorySpace.HBM)] * len(args),
         out_specs=[pl.BlockSpec(memory_space=pltpu.VMEM)] * 2,
         scratch_shapes=scratch,
@@ -220,8 +220,9 @@
         near = send(both, lambda x, y, z, c: (x, y, z ^ 1, c))
         inner_a = send(both, inward)
         own1, own2 = ring_near(both, "x")
+        out_mine = jnp.where(c == zhl, out_proj, send(out_proj, swap))
+        ga, gb, own1, own2, out_mine, in_proj, down_weight = hold((ga, gb, own1, own2, out_mine, in_proj, down_weight))
         gates = lax.all_gather(jnp.stack([ga, gb]), "dp", axis_index_groups=rings)
-        out_mine = jnp.where(c == zhl, out_proj, send(out_proj, swap))
         near, inner_a, own1, own2, down_weight, out_mine, in_proj, ga = hold(
             (near, inner_a, own1, own2, down_weight, out_mine, in_proj, ga)
         )
@@ -254,8 +255,8 @@
         gate1 = gate_matmul(True, late, gates, in_proj, first)
     with jax.named_scope("hidden"):
         hidden, other = hidden_matmul(early, late, downs, gate1[1])
-        gate_both = [gate0[0] + first.astype(F32), gate1[0] + send(gate1[1], swap).astype(F32)]
-        hidden = hidden + send(other, swap).astype(F32)
+        gate_both = [gate0[0] + first, gate1[0] + send(gate1[1], swap)]
+        hidden = hidden + send(other, swap)
         downs, other = hold((downs, other))
         sums = jnp.sum(downs[:, :, 896:].astype(F32).reshape(16, LANGS, 256), axis=0)
         sums = sums + send(sums, swap)

time: 206 us -> 220 us (1.068)
  starting transfers between devices: 57 us -> 61.8 us
  other arithmetic: 4.3 us -> 8.43 us
  waiting for transfers between devices: 76.9 us -> 79.5 us
    ppermute x31, starting transfers between devices: 57 us -> 61.7 us  [send(): return lax.ppermute(v, AXES, perm_of(move))]
    ppermute x31, waiting for transfers between devices: 76.8 us -> 79.4 us  [send(): return lax.ppermute(v, AXES, perm_of(move))]
    unnamed x71 -> x63, local copies, waits for them, and re-layouts: 3.88 us -> 5 us
  transfers between devices with their start and end apart: 33 -> 33, of which waited for: 12 -> 13; matrix products, arithmetic and copies ran while one was open for 3% -> 5% of each run, Pallas kernels for 7% -> 6%
where the time goes in v5:
time: 220 us
  waiting for transfers between devices  79.5 us (36%)
  starting transfers between devices  61.8 us (28%)
  Pallas kernels  25.4 us (12%)
  blocking collectives  18.9 us (9%)
  between operations  14.1 us (6%)
  local copies, waits for them, and re-layouts  8.89 us (4%)
  other arithmetic  8.43 us (4%)
  matrix products  2.8 us (1%)
    ppermute x31, waiting for transfers between devices, send(): return lax.ppermute(v, AXES, perm_of(move))  79.4 us
    ppermute x31, starting transfers between devices, send(): return lax.ppermute(v, AXES, perm_of(move))  61.7 us
    pallas_call x3, Pallas kernels, call(): pl.pallas_call(kernel, out_shape=[jax.ShapeDtypeStruct(shape, F32)] * 2,...  25.4 us
    all_to_all x1, blocking collectives, shards(): bands = lax.all_to_all(part.reshape(16, 256), 'mp', 0, 0, tiled=True)  10.5 us
    all_to_all x1, blocking collectives, everyone(): lax.all_to_all(jnp.broadcast_to(v[None], (16,) + v.shape), axis, 0, 0, ti...  8.32 us
    unnamed x63, local copies, waits for them, and re-layouts  5 us
  transfers between devices with their start and end apart: 33, of which 13 were waited for; matrix products, arithmetic and copies ran while one was open for 5% of the time, Pallas kernels for 6%

profile of v5, /device:TPU:1, one launch (start us, length us, event | category | flops | bytes accessed | tf_op | source)
XLA Modules:
  0.0 219.7 jit_solution(10405917923471315877)
XLA Ops:
  6.5 1.1 pad_maximum_fusion.2.refs_0_
  7.6 2.1 collective-permute-start.4
  9.8 1.4 collective-permute-start.5
  11.1 4.2 %collective-permute-start.2 = (bf16[256,896]{1,0:T(8,128)(2,1)}, bf16[256,896]{1,0:T(8,128)(2,1)S(1)}, u32[]{:S(2)}, u32[]{:S(2)}) collective-permute-start(bf16[256,896]{1,0:T(8,128)(2,1)} %param.12), channel_id=1, source_target_pairs={{0,32},{1,16},{2,34},{3,18},{4,36},{5,20},{6,38},{7,22},{8,40},{9,... | collective-permute-start | bytes 1376264 | tf_op jit(solution)/shard_map/first_moves/ppermute | solution.py:31
  15.3 4.9 %collective-permute-start.3 = (bf16[256,896]{1,0:T(8,128)(2,1)}, bf16[256,896]{1,0:T(8,128)(2,1)}, u32[]{:S(2)}, u32[]{:S(2)}) collective-permute-start(bf16[256,896]{1,0:T(8,128)(2,1)} %param.12), channel_id=1, source_target_pairs={{0,0},{1,48},{2,2},{3,50},{4,4},{5,52},{6,6},{7,54},{8,8},{9,56},{... | collective-permute-start | bytes 1376264 | tf_op jit(solution)/shard_map/first_moves/ppermute | solution.py:31
  20.3 4.4 %collective-permute-start.6 = (bf16[896,64]{0,1:T(8,128)(2,1)}, bf16[896,64]{0,1:T(8,128)(2,1)S(1)}, u32[]{:S(2)}, u32[]{:S(2)}) collective-permute-start(bf16[896,64]{0,1:T(8,128)(2,1)} %param.15), channel_id=1, source_target_pairs={{0,1},{1,0},{2,3},{3,2},{4,5},{5,4},{6,7},{7,6},{8,9},{9,8},{10,11... | collective-permute-start | bytes 344072 | tf_op jit(solution)/shard_map/first_moves/ppermute | solution.py:31
  24.7 0.8 reduce-precision_convert_fusion
  25.5 1.5 copy.16
  27.1 1.3 pad.8.refs_11_
  28.3 0.8 pad_maximum_fusion.3
  29.8 4.9 %collective-permute-done.2 = bf16[256,896]{1,0:T(8,128)(2,1)S(1)} collective-permute-done((bf16[256,896]{1,0:T(8,128)(2,1)}, bf16[256,896]{1,0:T(8,128)(2,1)S(1)}, u32[]{:S(2)}, u32[]{:S(2)}) %collective-permute-start.2) | collective-permute-done | bytes 458784 | tf_op jit(solution)/shard_map/first_moves/ppermute | solution.py:31
  34.8 6.0 %collective-permute-done.3 = bf16[256,896]{1,0:T(8,128)(2,1)} collective-permute-done((bf16[256,896]{1,0:T(8,128)(2,1)}, bf16[256,896]{1,0:T(8,128)(2,1)}, u32[]{:S(2)}, u32[]{:S(2)}) %collective-permute-start.3) | collective-permute-done | bytes 458784 | tf_op jit(solution)/shard_map/first_moves/ppermute | solution.py:31
  40.7 2.4 %pad_maximum_fusion.1 = bf16[2,256,896]{2,1,0:T(8,128)(2,1)} fusion(bf16[1,256,896]{2,1,0:T(8,128)(2,1)} %bitcast.3, bf16[1,256,896]{2,1,0:T(8,128)(2,1)S(1)} %bitcast.27), kind=kLoop, calls=%fused_computation.7 | loop fusion | flops 458752 | bytes 1835008 | tf_op jit(solution)/shard_map/first_moves/stack | solution.py:225
  44.0 9.7 %collective-permute-done.refs_5_ = bf16[1024,256]{1,0:T(8,128)(2,1)S(1)} collective-permute-done((bf16[1024,256]{1,0:T(8,128)(2,1)S(1)}, bf16[1024,256]{1,0:T(8,128)(2,1)S(1)}, u32[]{:S(2)}, u32[]{:S(2)}) %collective-permute-start) | collective-permute-done | bytes 524320 | tf_op jit(solution)/shard_map/first_moves/ppermute | solution.py:31
  53.7 9.9 %collective-permute-start.10 = (bf16[960,256]{1,0:T(8,128)(2,1)}, bf16[960,256]{1,0:T(8,128)(2,1)S(1)}, u32[]{:S(2)}, u32[]{:S(2)}) collective-permute-start(bf16[960,256]{1,0:T(8,128)(2,1)} %pad_maximum_fusion.3), channel_id=1, source_target_pairs={{0,0},{1,48},{2,2},{3,50},{4,4},{5,52},{6,6},{7,54},{8,8},{9,56},{... | collective-permute-start | bytes 1474568 | tf_op jit(solution)/shard_map/second_moves/ppermute | solution.py:31
  63.8 2.7 %collective-permute-start.12 = (bf16[1024,256]{1,0:T(8,128)(2,1)S(1)}, bf16[1024,256]{1,0:T(8,128)(2,1)S(1)}, u32[]{:S(2)}, u32[]{:S(2)}) collective-permute-start(bf16[1024,256]{1,0:T(8,128)(2,1)S(1)} %collective-permute-done.refs_5_), channel_id=1, source_target_pairs={{0,12},{1,13},{2,14},{3,15},{4,0},{5,1},{6,2},{7,3},{8,4},{9,5},{1... | collective-permute-start | bytes 1572872 | tf_op jit(solution)/shard_map/second_moves/ppermute | solution.py:31
  67.1 1.3 collective-permute-start.8
  68.4 15.8 %collective-permute-done.10 = bf16[960,256]{1,0:T(8,128)(2,1)S(1)} collective-permute-done((bf16[960,256]{1,0:T(8,128)(2,1)}, bf16[960,256]{1,0:T(8,128)(2,1)S(1)}, u32[]{:S(2)}, u32[]{:S(2)}) %collective-permute-start.10) | collective-permute-done | bytes 491552 | tf_op jit(solution)/shard_map/second_moves/ppermute | solution.py:31
  84.3 15.5 %collective-permute-done.9 = bf16[960,256]{1,0:T(8,128)(2,1)S(1)} collective-permute-done((bf16[960,256]{1,0:T(8,128)(2,1)}, bf16[960,256]{1,0:T(8,128)(2,1)S(1)}, u32[]{:S(2)}, u32[]{:S(2)}) %collective-permute-start.9) | collective-permute-done | bytes 491552 | tf_op jit(solution)/shard_map/second_moves/ppermute | solution.py:31
  99.8 0.9 copy-done.19
  100.7 1.1 pad_maximum_fusion
  101.9 2.7 %collective-permute-start.19 = (bf16[512,256]{1,0:T(8,128)(2,1)S(1)}, bf16[512,256]{1,0:T(8,128)(2,1)S(1)}, u32[]{:S(2)}, u32[]{:S(2)}) collective-permute-start(bf16[512,256]{1,0:T(8,128)(2,1)S(1)} %slice.54), channel_id=1, source_target_pairs={{0,12},{1,13},{2,14},{3,15},{4,0},{5,1},{6,2},{7,3},{8,4},{9,5},{1... | collective-permute-start | bytes 786440 | tf_op jit(solution)/shard_map/third_moves/ppermute | solution.py:31
  104.7 1.1 broadcast_select_fusion.1.refs_0_.refs_10_
  105.9 2.7 %collective-permute-start.15 = (bf16[1024,256]{1,0:T(8,128)(2,1)S(1)}, bf16[1024,256]{1,0:T(8,128)(2,1)S(1)}, u32[]{:S(2)}, u32[]{:S(2)}) collective-permute-start(bf16[1024,256]{1,0:T(8,128)(2,1)S(1)} %broadcast_select_fusion.1.refs_0_.refs_10_), channel_id=1, source_target_pairs={{0,12},{1,13},{2,14},{3,15},{4,0},{5,1},{6,2},{7,3},{8,4},{9,5},{1... | collective-permute-start | bytes 1572872 | tf_op jit(solution)/shard_map/third_moves/ppermute | solution.py:31
  108.5 1.3 collective-permute-start.13
  109.9 1.6 collective-permute-done.18.refs_3_
  111.5 2.8 %collective-permute-start.17 = (bf16[512,256]{1,0:T(8,128)(2,1)S(1)}, bf16[512,256]{1,0:T(8,128)(2,1)S(1)}, u32[]{:S(2)}, u32[]{:S(2)}) collective-permute-start(bf16[512,256]{1,0:T(8,128)(2,1)S(1)} %slice.52), channel_id=1, source_target_pairs={{0,12},{1,13},{2,14},{3,15},{4,0},{5,1},{6,2},{7,3},{8,4},{9,5},{1... | collective-permute-start | bytes 786440 | tf_op jit(solution)/shard_map/third_moves/ppermute | solution.py:31
  114.3 6.4 %collective-permute-done.16.refs_8_ = bf16[512,256]{1,0:T(8,128)(2,1)S(1)} collective-permute-done((bf16[512,256]{1,0:T(8,128)(2,1)S(1)}, bf16[512,256]{1,0:T(8,128)(2,1)S(1)}, u32[]{:S(2)}, u32[]{:S(2)}) %collective-permute-start.16) | collective-permute-done | bytes 262176 | tf_op jit(solution)/shard_map/third_moves/ppermute | solution.py:31
  120.7 0.8 collective-permute-done.13
  121.6 2.7 %collective-permute-start.21 = (bf16[1024,256]{1,0:T(8,128)(2,1)S(1)}, bf16[1024,256]{1,0:T(8,128)(2,1)S(1)}, u32[]{:S(2)}, u32[]{:S(2)}) collective-permute-start(bf16[1024,256]{1,0:T(8,128)(2,1)S(1)} %broadcast_select_fusion.refs_5_.refs_15_), channel_id=1, source_target_pairs={{0,12},{1,13},{2,14},{3,15},{4,0},{5,1},{6,2},{7,3},{8,4},{9,5},{1... | collective-permute-start | bytes 1572872 | tf_op jit(solution)/shard_map/fourth_moves/ppermute | solution.py:31
  124.3 0.7 slice.55
  125.0 0.7 slice.56
  125.8 2.7 %collective-permute-start.23 = (bf16[512,256]{1,0:T(8,128)(2,1)}, bf16[512,256]{1,0:T(8,128)(2,1)}, u32[]{:S(2)}, u32[]{:S(2)}) collective-permute-start(bf16[512,256]{1,0:T(8,128)(2,1)} %slice.56), channel_id=1, source_target_pairs={{0,12},{1,13},{2,14},{3,15},{4,0},{5,1},{6,2},{7,3},{8,4},{9,5},{1... | collective-permute-start | bytes 786440 | tf_op jit(solution)/shard_map/fourth_moves/ppermute | solution.py:31
  128.5 7.2 %fourth_moves.1 = (f32[256,1024]{1,0:T(8,128)}, f32[256,1024]{1,0:T(8,128)}) custom-call(bf16[1024,256]{1,0:T(8,128)(2,1)} %copy-done.4, bf16[1024,256]{1,0:T(8,128)(2,1)} %copy-done.8, bf16[1024,256]{1,0:T(8,128)(2,1)} %copy-done.9, bf16[512,256]{1,0:T(8,128)(2,1)} %copy-done.21, bf16[512,256]{1,0:T(8,128)(2,1)} %copy-done.22, ...), custom_call_target="tpu_custom_call" | custom-call | flops 2147483648 | bytes 8388608 | tf_op jit(solution)/shard_map/fourth_moves/pallas_call | solution.py:164
  135.7 4.5 %collective-permute-done.22.refs_3_.refs_13_ = bf16[512,256]{1,0:T(8,128)(2,1)} collective-permute-done((bf16[512,256]{1,0:T(8,128)(2,1)}, bf16[512,256]{1,0:T(8,128)(2,1)}, u32[]{:S(2)}, u32[]{:S(2)}) %collective-permute-start.22) | collective-permute-done | bytes 262176 | tf_op jit(solution)/shard_map/fourth_moves/ppermute | solution.py:31
  140.5 3.0 %collective-permute-start.26 = (bf16[512,256]{1,0:T(8,128)(2,1)S(1)}, bf16[512,256]{1,0:T(8,128)(2,1)S(1)}, u32[]{:S(2)}, u32[]{:S(2)}) collective-permute-start(bf16[512,256]{1,0:T(8,128)(2,1)S(1)} %slice.59), channel_id=1, source_target_pairs={{0,12},{1,13},{2,14},{3,15},{4,0},{5,1},{6,2},{7,3},{8,4},{9,5},{1... | collective-permute-start | bytes 786440 | tf_op jit(solution)/shard_map/fifth_moves/ppermute | solution.py:31
  143.5 6.1 %collective-permute-done.25.refs_8_.refs_18_ = bf16[512,256]{1,0:T(8,128)(2,1)S(1)} collective-permute-done((bf16[512,256]{1,0:T(8,128)(2,1)S(1)}, bf16[512,256]{1,0:T(8,128)(2,1)S(1)}, u32[]{:S(2)}, u32[]{:S(2)}) %collective-permute-start.25) | collective-permute-done | bytes 262176 | tf_op jit(solution)/shard_map/fifth_moves/ppermute | solution.py:31
  150.4 1.1 copy-done.1
  151.5 7.1 %fifth_moves.1 = (f32[256,1024]{1,0:T(8,128)}, f32[256,1024]{1,0:T(8,128)}) custom-call(bf16[1024,256]{1,0:T(8,128)(2,1)} %copy-done.5, bf16[1024,256]{1,0:T(8,128)(2,1)} %copy-done.3, bf16[1024,256]{1,0:T(8,128)(2,1)} %copy-done.12, bf16[512,256]{1,0:T(8,128)(2,1)} %collective-permute-done.22.refs_3_.refs_13_, ...), custom_call_target="tpu_custom_call" | custom-call | flops 2147483648 | bytes 8388608 | tf_op jit(solution)/shard_map/fifth_moves/pallas_call | solution.py:164
  158.6 11.1 %hidden.1 = (f32[512,896]{1,0:T(8,128)}, f32[512,896]{1,0:T(8,128)}) custom-call(bf16[1024,256]{1,0:T(8,128)(2,1)} %copy-done.4, bf16[1024,256]{1,0:T(8,128)(2,1)} %copy-done.8, bf16[1024,256]{1,0:T(8,128)(2,1)} %copy-done.9, bf16[512,256]{1,0:T(8,128)(2,1)} %copy-done.21, bf16[512,256]{1,0:T(8,128)(2,1)} %copy-done.22, bf16[1024,256]{1,0:T(8,128)(2,1)} %copy-done.17, ...), custom_call_target="tpu_custom_call" | custom-call | flops 3758096384 | bytes 8388608 | tf_op jit(solution)/shard_map/hidden/pallas_call | solution.py:164
  169.7 1.1 collective-permute-start.27
  170.9 1.0 slice.65
  172.6 1.7 collective-permute-done.29
  174.3 1.7 collective-permute-done.28
  177.9 9.3 %collective-permute-start.30 = (f32[96,256]{1,0:T(8,128)S(1)}, f32[96,256]{1,0:T(8,128)S(1)}, u32[]{:S(2)}, u32[]{:S(2)}) collective-permute-start(f32[96,256]{1,0:T(8,128)S(1)} %select_maximum_fusion), channel_id=1, source_target_pairs={{0,16},{1,17},{2,18},{3,19},{4,20},{5,21},{6,22},{7,23},{8,24},{9,... | collective-permute-start | bytes 294920 | tf_op jit(solution)/shard_map/finish/ppermute | solution.py:31
  187.5 4.8 %collective-permute-done.30 = f32[96,256]{1,0:T(8,128)S(1)} collective-permute-done((f32[96,256]{1,0:T(8,128)S(1)}, f32[96,256]{1,0:T(8,128)S(1)}, u32[]{:S(2)}, u32[]{:S(2)}) %collective-permute-start.30) | collective-permute-done | bytes 98336 | tf_op jit(solution)/shard_map/finish/ppermute | solution.py:31
  193.3 10.5 %all_to_all.16 = f32[16,1,256]{2,1,0:T(1,128)S(1)} all-to-all(f32[16,1,256]{2,1,0:T(1,128)S(1)} %all_to_all.13), channel_id=1, replica_groups=mesh['dp'=16,'mp'=16] {'mp'}, dimensions={0} | all-to-all | bytes 32768 | tf_op jit(solution)/shard_map/finish/all_to_all | solution.py:280
  204.0 8.3 %all_to_all.17 = f32[16,1,32]{2,1,0:T(1,128)S(1)} all-to-all(f32[16,1,32]{2,1,0:T(1,128)S(1)} %broadcast_in_dim.2), channel_id=1, replica_groups=mesh['dp'=16,'mp'=16] {'mp'}, dimensions={0} | all-to-all | bytes 4096 | tf_op jit(solution)/shard_map/finish/all_to_all | solution.py:198
  (125 shorter events, 8.5 us)
Async XLA Ops:
  6.5 18.2 %copy-start = (bf16[128,256]{1,0:T(8,128)(2,1)S(1)}, bf16[128,256]{1,0:T(8,128)(2,1)}, u32[]{:S(2)}) copy-start(bf16[128,256]{1,0:T(8,128)(2,1)} %param.18) | copy-start | bytes 196612
  6.5 121.9 %all-gather.5.cloned.1.call-start = ((), (), s32[]{:S(2)}) async-start(), calls=%async_computation.2 | async-start | bytes 4587520 | tf_op jit(solution)/shard_map/first_moves/all_gather | solution.py:225
  7.6 35.7 %copy-start.4 = (bf16[1024,256]{1,0:T(8,128)(2,1)}, bf16[1024,256]{1,0:T(8,128)(2,1)S(1)}, u32[]{:S(2)}) copy-start(bf16[1024,256]{1,0:T(8,128)(2,1)S(1)} %pad_maximum_fusion.2.refs_0_) | copy-start | bytes 1572868
  7.6 33.1 %collective-permute-start.4 = (bf16[1024,256]{1,0:T(8,128)(2,1)S(1)}, bf16[1024,256]{1,0:T(8,128)(2,1)S(1)}, u32[]{:S(2)}, u32[]{:S(2)}) collective-permute-start(bf16[1024,256]{1,0:T(8,128)(2,1)S(1)} %pad_maximum_fusion.2.refs_0_), channel_id=1, source_target_pairs={{0,4},{1,5},{2,6},{3,7},{4,8},{5,9},{6,10},{7,11},{8,12},{9,13},{1... | collective-permute-start | bytes 1572872 | tf_op jit(solution)/shard_map/first_moves/ppermute | solution.py:31
  9.8 31.0 %collective-permute-start.5 = (bf16[1024,256]{1,0:T(8,128)(2,1)S(1)}, bf16[1024,256]{1,0:T(8,128)(2,1)S(1)}, u32[]{:S(2)}, u32[]{:S(2)}) collective-permute-start(bf16[1024,256]{1,0:T(8,128)(2,1)S(1)} %pad_maximum_fusion.2.refs_0_), channel_id=1, source_target_pairs={{0,12},{1,13},{2,14},{3,15},{4,0},{5,1},{6,2},{7,3},{8,4},{9,5},{1... | collective-permute-start | bytes 1572872 | tf_op jit(solution)/shard_map/first_moves/ppermute | solution.py:31
  11.1 23.6 %collective-permute-start.2 = (bf16[256,896]{1,0:T(8,128)(2,1)}, bf16[256,896]{1,0:T(8,128)(2,1)S(1)}, u32[]{:S(2)}, u32[]{:S(2)}) collective-permute-start(bf16[256,896]{1,0:T(8,128)(2,1)} %param.12), channel_id=1, source_target_pairs={{0,32},{1,16},{2,34},{3,18},{4,36},{5,20},{6,38},{7,22},{8,40},{9,... | collective-permute-start | bytes 1376264 | tf_op jit(solution)/shard_map/first_moves/ppermute | solution.py:31
  15.3 25.4 %collective-permute-start.3 = (bf16[256,896]{1,0:T(8,128)(2,1)}, bf16[256,896]{1,0:T(8,128)(2,1)}, u32[]{:S(2)}, u32[]{:S(2)}) collective-permute-start(bf16[256,896]{1,0:T(8,128)(2,1)} %param.12), channel_id=1, source_target_pairs={{0,0},{1,48},{2,2},{3,50},{4,4},{5,52},{6,6},{7,54},{8,8},{9,56},{... | collective-permute-start | bytes 1376264 | tf_op jit(solution)/shard_map/first_moves/ppermute | solution.py:31
  20.3 8.9 %collective-permute-start.6 = (bf16[896,64]{0,1:T(8,128)(2,1)}, bf16[896,64]{0,1:T(8,128)(2,1)S(1)}, u32[]{:S(2)}, u32[]{:S(2)}) collective-permute-start(bf16[896,64]{0,1:T(8,128)(2,1)} %param.15), channel_id=1, source_target_pairs={{0,1},{1,0},{2,3},{3,2},{4,5},{5,4},{6,7},{7,6},{8,9},{9,8},{10,11... | collective-permute-start | bytes 344072 | tf_op jit(solution)/shard_map/first_moves/ppermute | solution.py:31
  40.7 61.0 %copy-start.8 = (bf16[1024,256]{1,0:T(8,128)(2,1)}, bf16[1024,256]{1,0:T(8,128)(2,1)S(1)}, u32[]{:S(2)}) copy-start(bf16[1024,256]{1,0:T(8,128)(2,1)S(1)} %collective-permute-done.4.refs_1_) | copy-start | bytes 1572868
  40.7 61.2 %copy-start.9 = (bf16[1024,256]{1,0:T(8,128)(2,1)}, bf16[1024,256]{1,0:T(8,128)(2,1)S(1)}, u32[]{:S(2)}) copy-start(bf16[1024,256]{1,0:T(8,128)(2,1)S(1)} %collective-permute-done.5.refs_2_) | copy-start | bytes 1572868
  43.1 115.4 %all-gather.7.cloned.1.call-start = ((), (), s32[]{:S(2)}) async-start(), calls=%async_computation.3 | async-start | bytes 4915200 | tf_op jit(solution)/shard_map/third_moves/all_gather | solution.py:237
  43.2 10.5 %collective-permute-start = (bf16[1024,256]{1,0:T(8,128)(2,1)S(1)}, bf16[1024,256]{1,0:T(8,128)(2,1)S(1)}, u32[]{:S(2)}, u32[]{:S(2)}) collective-permute-start(bf16[1024,256]{1,0:T(8,128)(2,1)S(1)} %pad_maximum_fusion.2.refs_0_), channel_id=1, source_target_pairs={{0,2},{1,3},{2,0},{3,1},{4,6},{5,7},{6,4},{7,5},{8,10},{9,11},{10,... | collective-permute-start | bytes 1572872 | tf_op jit(solution)/shard_map/first_moves/ppermute | solution.py:31
  43.3 10.4 %collective-permute-start.1 = (bf16[1024,256]{1,0:T(8,128)(2,1)S(1)}, bf16[1024,256]{1,0:T(8,128)(2,1)S(1)}, u32[]{:S(2)}, u32[]{:S(2)}) collective-permute-start(bf16[1024,256]{1,0:T(8,128)(2,1)S(1)} %pad_maximum_fusion.2.refs_0_), channel_id=1, source_target_pairs={{2,16},{3,17},{6,20},{7,21},{10,24},{11,25},{14,28},{15,29},{16,2}... | collective-permute-start | bytes 1572872 | tf_op jit(solution)/shard_map/first_moves/ppermute | solution.py:31
  53.7 48.2 %copy-start.17 = (bf16[1024,256]{1,0:T(8,128)(2,1)}, bf16[1024,256]{1,0:T(8,128)(2,1)S(1)}, u32[]{:S(2)}) copy-start(bf16[1024,256]{1,0:T(8,128)(2,1)S(1)} %collective-permute-done.refs_5_) | copy-start | bytes 1572868
  53.7 46.0 %copy-start.18 = (bf16[1024,256]{1,0:T(8,128)(2,1)}, bf16[1024,256]{1,0:T(8,128)(2,1)S(1)}, u32[]{:S(2)}) copy-start(bf16[1024,256]{1,0:T(8,128)(2,1)S(1)} %collective-permute-done.1) | copy-start | bytes 1572868
  53.7 30.5 %collective-permute-start.10 = (bf16[960,256]{1,0:T(8,128)(2,1)}, bf16[960,256]{1,0:T(8,128)(2,1)S(1)}, u32[]{:S(2)}, u32[]{:S(2)}) collective-permute-start(bf16[960,256]{1,0:T(8,128)(2,1)} %pad_maximum_fusion.3), channel_id=1, source_target_pairs={{0,0},{1,48},{2,2},{3,50},{4,4},{5,52},{6,6},{7,54},{8,8},{9,56},{... | collective-permute-start | bytes 1474568 | tf_op jit(solution)/shard_map/second_moves/ppermute | solution.py:31
  63.7 36.1 %collective-permute-start.11 = (bf16[1024,256]{1,0:T(8,128)(2,1)S(1)}, bf16[1024,256]{1,0:T(8,128)(2,1)S(1)}, u32[]{:S(2)}, u32[]{:S(2)}) collective-permute-start(bf16[1024,256]{1,0:T(8,128)(2,1)S(1)} %collective-permute-done.refs_5_), channel_id=1, source_target_pairs={{0,4},{1,5},{2,6},{3,7},{4,8},{5,9},{6,10},{7,11},{8,12},{9,13},{1... | collective-permute-start | bytes 1572872 | tf_op jit(solution)/shard_map/second_moves/ppermute | solution.py:31
  63.8 36.0 %collective-permute-start.12 = (bf16[1024,256]{1,0:T(8,128)(2,1)S(1)}, bf16[1024,256]{1,0:T(8,128)(2,1)S(1)}, u32[]{:S(2)}, u32[]{:S(2)}) collective-permute-start(bf16[1024,256]{1,0:T(8,128)(2,1)S(1)} %collective-permute-done.refs_5_), channel_id=1, source_target_pairs={{0,12},{1,13},{2,14},{3,15},{4,0},{5,1},{6,2},{7,3},{8,4},{9,5},{1... | collective-permute-start | bytes 1572872 | tf_op jit(solution)/shard_map/second_moves/ppermute | solution.py:31
  66.4 33.3 %collective-permute-start.7 = (bf16[1024,256]{1,0:T(8,128)(2,1)S(1)}, bf16[1024,256]{1,0:T(8,128)(2,1)S(1)}, u32[]{:S(2)}, u32[]{:S(2)}) collective-permute-start(bf16[1024,256]{1,0:T(8,128)(2,1)S(1)} %collective-permute-done.refs_5_), channel_id=1, source_target_pairs={{2,16},{3,17},{6,20},{7,21},{10,24},{11,25},{14,28},{15,29},{16,2}... | collective-permute-start | bytes 1572872 | tf_op jit(solution)/shard_map/second_moves/ppermute | solution.py:31
  67.1 32.7 %collective-permute-start.8 = (bf16[1024,256]{1,0:T(8,128)(2,1)S(1)}, bf16[1024,256]{1,0:T(8,128)(2,1)S(1)}, u32[]{:S(2)}, u32[]{:S(2)}) collective-permute-start(bf16[1024,256]{1,0:T(8,128)(2,1)S(1)} %collective-permute-done.1), channel_id=1, source_target_pairs={{2,0},{3,1},{6,4},{7,5},{10,8},{11,9},{14,12},{15,13},{16,18},{17,... | collective-permute-start | bytes 1572872 | tf_op jit(solution)/shard_map/second_moves/ppermute | solution.py:31
  84.3 15.5 %collective-permute-start.9 = (bf16[960,256]{1,0:T(8,128)(2,1)}, bf16[960,256]{1,0:T(8,128)(2,1)S(1)}, u32[]{:S(2)}, u32[]{:S(2)}) collective-permute-start(bf16[960,256]{1,0:T(8,128)(2,1)} %pad_maximum_fusion.3), channel_id=1, source_target_pairs={{0,32},{1,16},{2,34},{3,18},{4,36},{5,20},{6,38},{7,22},{8,40},{9,... | collective-permute-start | bytes 1474568 | tf_op jit(solution)/shard_map/second_moves/ppermute | solution.py:31
  99.7 10.1 %copy-start.11 = (bf16[1024,256]{1,0:T(8,128)(2,1)}, bf16[1024,256]{1,0:T(8,128)(2,1)S(1)}, u32[]{:S(2)}) copy-start(bf16[1024,256]{1,0:T(8,128)(2,1)S(1)} %collective-permute-done.12.refs_7_) | copy-start | bytes 1572868
  101.8 9.7 %collective-permute-start.18 = (bf16[512,256]{1,0:T(8,128)(2,1)S(1)}, bf16[512,256]{1,0:T(8,128)(2,1)S(1)}, u32[]{:S(2)}, u32[]{:S(2)}) collective-permute-start(bf16[512,256]{1,0:T(8,128)(2,1)S(1)} %slice.53), channel_id=1, source_target_pairs={{0,4},{1,5},{2,6},{3,7},{4,8},{5,9},{6,10},{7,11},{8,12},{9,13},{1... | collective-permute-start | bytes 786440 | tf_op jit(solution)/shard_map/third_moves/ppermute | solution.py:31
  101.9 9.5 %collective-permute-start.19 = (bf16[512,256]{1,0:T(8,128)(2,1)S(1)}, bf16[512,256]{1,0:T(8,128)(2,1)S(1)}, u32[]{:S(2)}, u32[]{:S(2)}) collective-permute-start(bf16[512,256]{1,0:T(8,128)(2,1)S(1)} %slice.54), channel_id=1, source_target_pairs={{0,12},{1,13},{2,14},{3,15},{4,0},{5,1},{6,2},{7,3},{8,4},{9,5},{1... | collective-permute-start | bytes 786440 | tf_op jit(solution)/shard_map/third_moves/ppermute | solution.py:31
  105.8 20.0 %copy-start.5 = (bf16[1024,256]{1,0:T(8,128)(2,1)}, bf16[1024,256]{1,0:T(8,128)(2,1)S(1)}, u32[]{:S(2)}) copy-start(bf16[1024,256]{1,0:T(8,128)(2,1)S(1)} %broadcast_select_fusion.1.refs_0_.refs_10_) | copy-start | bytes 1572868
  105.8 14.9 %collective-permute-start.14 = (bf16[1024,256]{1,0:T(8,128)(2,1)S(1)}, bf16[1024,256]{1,0:T(8,128)(2,1)S(1)}, u32[]{:S(2)}, u32[]{:S(2)}) collective-permute-start(bf16[1024,256]{1,0:T(8,128)(2,1)S(1)} %broadcast_select_fusion.1.refs_0_.refs_10_), channel_id=1, source_target_pairs={{0,4},{1,5},{2,6},{3,7},{4,8},{5,9},{6,10},{7,11},{8,12},{9,13},{1... | collective-permute-start | bytes 1572872 | tf_op jit(solution)/shard_map/third_moves/ppermute | solution.py:31
  105.9 14.8 %collective-permute-start.15 = (bf16[1024,256]{1,0:T(8,128)(2,1)S(1)}, bf16[1024,256]{1,0:T(8,128)(2,1)S(1)}, u32[]{:S(2)}, u32[]{:S(2)}) collective-permute-start(bf16[1024,256]{1,0:T(8,128)(2,1)S(1)} %broadcast_select_fusion.1.refs_0_.refs_10_), channel_id=1, source_target_pairs={{0,12},{1,13},{2,14},{3,15},{4,0},{5,1},{6,2},{7,3},{8,4},{9,5},{1... | collective-permute-start | bytes 1572872 | tf_op jit(solution)/shard_map/third_moves/ppermute | solution.py:31
  108.5 12.9 %collective-permute-start.13 = (bf16[1024,256]{1,0:T(8,128)(2,1)S(1)}, bf16[1024,256]{1,0:T(8,128)(2,1)S(1)}, u32[]{:S(2)}, u32[]{:S(2)}) collective-permute-start(bf16[1024,256]{1,0:T(8,128)(2,1)S(1)} %collective-permute-done.7), channel_id=1, source_target_pairs={{2,0},{3,1},{6,4},{7,5},{10,8},{11,9},{14,12},{15,13},{16,18},{17,... | collective-permute-start | bytes 1572872 | tf_op jit(solution)/shard_map/third_moves/ppermute | solution.py:31
  111.5 17.0 %copy-start.21 = (bf16[512,256]{1,0:T(8,128)(2,1)}, bf16[512,256]{1,0:T(8,128)(2,1)S(1)}, u32[]{:S(2)}) copy-start(bf16[512,256]{1,0:T(8,128)(2,1)S(1)} %collective-permute-done.18.refs_3_) | copy-start | bytes 786436
  111.5 9.2 %collective-permute-start.16 = (bf16[512,256]{1,0:T(8,128)(2,1)S(1)}, bf16[512,256]{1,0:T(8,128)(2,1)S(1)}, u32[]{:S(2)}, u32[]{:S(2)}) collective-permute-start(bf16[512,256]{1,0:T(8,128)(2,1)S(1)} %slice.51), channel_id=1, source_target_pairs={{0,4},{1,5},{2,6},{3,7},{4,8},{5,9},{6,10},{7,11},{8,12},{9,13},{1... | collective-permute-start | bytes 786440 | tf_op jit(solution)/shard_map/third_moves/ppermute | solution.py:31
  111.5 9.1 %collective-permute-start.17 = (bf16[512,256]{1,0:T(8,128)(2,1)S(1)}, bf16[512,256]{1,0:T(8,128)(2,1)S(1)}, u32[]{:S(2)}, u32[]{:S(2)}) collective-permute-start(bf16[512,256]{1,0:T(8,128)(2,1)S(1)} %slice.52), channel_id=1, source_target_pairs={{0,12},{1,13},{2,14},{3,15},{4,0},{5,1},{6,2},{7,3},{8,4},{9,5},{1... | collective-permute-start | bytes 786440 | tf_op jit(solution)/shard_map/third_moves/ppermute | solution.py:31
  120.7 15.0 %copy-start.12 = (bf16[1024,256]{1,0:T(8,128)(2,1)}, bf16[1024,256]{1,0:T(8,128)(2,1)S(1)}, u32[]{:S(2)}) copy-start(bf16[1024,256]{1,0:T(8,128)(2,1)S(1)} %collective-permute-done.15.refs_2_.refs_12_) | copy-start | bytes 1572868
  121.5 14.1 %copy-start.6 = (bf16[1024,256]{1,0:T(8,128)(2,1)}, bf16[1024,256]{1,0:T(8,128)(2,1)S(1)}, u32[]{:S(2)}) copy-start(bf16[1024,256]{1,0:T(8,128)(2,1)S(1)} %broadcast_select_fusion.refs_5_.refs_15_) | copy-start | bytes 1572868
  121.6 18.6 %collective-permute-start.20 = (bf16[1024,256]{1,0:T(8,128)(2,1)S(1)}, bf16[1024,256]{1,0:T(8,128)(2,1)S(1)}, u32[]{:S(2)}, u32[]{:S(2)}) collective-permute-start(bf16[1024,256]{1,0:T(8,128)(2,1)S(1)} %broadcast_select_fusion.refs_5_.refs_15_), channel_id=1, source_target_pairs={{0,4},{1,5},{2,6},{3,7},{4,8},{5,9},{6,10},{7,11},{8,12},{9,13},{1... | collective-permute-start | bytes 1572872 | tf_op jit(solution)/shard_map/fourth_moves/ppermute | solution.py:31
  121.6 18.6 %collective-permute-start.21 = (bf16[1024,256]{1,0:T(8,128)(2,1)S(1)}, bf16[1024,256]{1,0:T(8,128)(2,1)S(1)}, u32[]{:S(2)}, u32[]{:S(2)}) collective-permute-start(bf16[1024,256]{1,0:T(8,128)(2,1)S(1)} %broadcast_select_fusion.refs_5_.refs_15_), channel_id=1, source_target_pairs={{0,12},{1,13},{2,14},{3,15},{4,0},{5,1},{6,2},{7,3},{8,4},{9,5},{1... | collective-permute-start | bytes 1572872 | tf_op jit(solution)/shard_map/fourth_moves/ppermute | solution.py:31
  125.0 15.2 %collective-permute-start.22 = (bf16[512,256]{1,0:T(8,128)(2,1)}, bf16[512,256]{1,0:T(8,128)(2,1)}, u32[]{:S(2)}, u32[]{:S(2)}) collective-permute-start(bf16[512,256]{1,0:T(8,128)(2,1)} %slice.55), channel_id=1, source_target_pairs={{0,4},{1,5},{2,6},{3,7},{4,8},{5,9},{6,10},{7,11},{8,12},{9,13},{1... | collective-permute-start | bytes 786440 | tf_op jit(solution)/shard_map/fourth_moves/ppermute | solution.py:31
  125.8 14.4 %collective-permute-start.23 = (bf16[512,256]{1,0:T(8,128)(2,1)}, bf16[512,256]{1,0:T(8,128)(2,1)}, u32[]{:S(2)}, u32[]{:S(2)}) collective-permute-start(bf16[512,256]{1,0:T(8,128)(2,1)} %slice.56), channel_id=1, source_target_pairs={{0,12},{1,13},{2,14},{3,15},{4,0},{5,1},{6,2},{7,3},{8,4},{9,5},{1... | collective-permute-start | bytes 786440 | tf_op jit(solution)/shard_map/fourth_moves/ppermute | solution.py:31
  140.2 9.4 %collective-permute-start.24 = (f32[256,1024]{1,0:T(8,128)}, f32[256,1024]{1,0:T(8,128)S(1)}, u32[]{:S(2)}, u32[]{:S(2)}) collective-permute-start(f32[256,1024]{1,0:T(8,128)} %get-tuple-element.72), channel_id=1, source_target_pairs={{0,1},{1,0},{2,3},{3,2},{4,5},{5,4},{6,7},{7,6},{8,9},{9,8},{10,11... | collective-permute-start | bytes 3145736 | tf_op jit(solution)/shard_map/fifth_moves/ppermute | solution.py:31
  140.4 9.3 %collective-permute-start.25 = (bf16[512,256]{1,0:T(8,128)(2,1)S(1)}, bf16[512,256]{1,0:T(8,128)(2,1)S(1)}, u32[]{:S(2)}, u32[]{:S(2)}) collective-permute-start(bf16[512,256]{1,0:T(8,128)(2,1)S(1)} %slice.58), channel_id=1, source_target_pairs={{0,4},{1,5},{2,6},{3,7},{4,8},{5,9},{6,10},{7,11},{8,12},{9,13},{1... | collective-permute-start | bytes 786440 | tf_op jit(solution)/shard_map/fifth_moves/ppermute | solution.py:31
  140.5 9.1 %collective-permute-start.26 = (bf16[512,256]{1,0:T(8,128)(2,1)S(1)}, bf16[512,256]{1,0:T(8,128)(2,1)S(1)}, u32[]{:S(2)}, u32[]{:S(2)}) collective-permute-start(bf16[512,256]{1,0:T(8,128)(2,1)S(1)} %slice.59), channel_id=1, source_target_pairs={{0,12},{1,13},{2,14},{3,15},{4,0},{5,1},{6,2},{7,3},{8,4},{9,5},{1... | collective-permute-start | bytes 786440 | tf_op jit(solution)/shard_map/fifth_moves/ppermute | solution.py:31
  158.6 13.8 %copy-start.2 = (f32[256,1024]{1,0:T(8,128)S(1)}, f32[256,1024]{1,0:T(8,128)}, u32[]{:S(2)}) copy-start(f32[256,1024]{1,0:T(8,128)} %copy-done.1) | copy-start | bytes 3145732
  158.6 13.8 %copy-start.15 = (f32[256,1024]{1,0:T(8,128)S(1)}, f32[256,1024]{1,0:T(8,128)}, u32[]{:S(2)}) copy-start(f32[256,1024]{1,0:T(8,128)} %get-tuple-element.71) | copy-start | bytes 3145732
  169.7 6.4 %collective-permute-start.27 = (f32[512,896]{1,0:T(8,128)}, f32[512,896]{1,0:T(8,128)S(1)}, u32[]{:S(2)}, u32[]{:S(2)}) collective-permute-start(f32[512,896]{1,0:T(8,128)} %get-tuple-element.81), channel_id=1, source_target_pairs={{0,1},{1,0},{2,3},{3,2},{4,5},{5,4},{6,7},{7,6},{8,9},{9,8},{10,11... | collective-permute-start | bytes 5505032 | tf_op jit(solution)/shard_map/hidden/ppermute | solution.py:31
  170.8 5.2 %collective-permute-start.28 = (f32[256,1024]{1,0:T(8,128)}, f32[256,1024]{1,0:T(8,128)S(1)}, u32[]{:S(2)}, u32[]{:S(2)}) collective-permute-start(f32[256,1024]{1,0:T(8,128)} %get-tuple-element.79.refs_21_), channel_id=1, source_target_pairs={{0,1},{1,0},{2,3},{3,2},{4,5},{5,4},{6,7},{7,6},{8,9},{9,8},{10,11... | collective-permute-start | bytes 3145736 | tf_op jit(solution)/shard_map/hidden/ppermute | solution.py:31
  171.9 2.4 %collective-permute-start.29 = (f32[32,256]{1,0:T(8,128)S(1)}, f32[32,256]{1,0:T(8,128)S(1)}, u32[]{:S(2)}, u32[]{:S(2)}) collective-permute-start(f32[32,256]{1,0:T(8,128)S(1)} %convert_reduce_fusion), channel_id=1, source_target_pairs={{0,1},{1,0},{2,3},{3,2},{4,5},{5,4},{6,7},{7,6},{8,9},{9,8},{10,11... | collective-permute-start | bytes 98312 | tf_op jit(solution)/shard_map/hidden/ppermute | solution.py:31
  177.8 14.9 %copy-start.29 = (f32[64,64]{1,0:T(8,128)S(1)}, f32[64,64]{1,0:T(8,128)}, u32[]{:S(2)}) copy-start(f32[64,64]{1,0:T(8,128)} %param.16) | copy-start | bytes 49156
  177.8 15.1 %copy-start.30 = (f32[64,64]{1,0:T(8,128)S(1)}, f32[64,64]{1,0:T(8,128)}, u32[]{:S(2)}) copy-start(f32[64,64]{1,0:T(8,128)} %param.17) | copy-start | bytes 49156
  177.9 14.5 %collective-permute-start.30 = (f32[96,256]{1,0:T(8,128)S(1)}, f32[96,256]{1,0:T(8,128)S(1)}, u32[]{:S(2)}, u32[]{:S(2)}) collective-permute-start(f32[96,256]{1,0:T(8,128)S(1)} %select_maximum_fusion), channel_id=1, source_target_pairs={{0,16},{1,17},{2,18},{3,19},{4,20},{5,21},{6,22},{7,23},{8,24},{9,... | collective-permute-start | bytes 294920 | tf_op jit(solution)/shard_map/finish/ppermute | solution.py:31
  (16 other events, 77.7 us)
Sparse Core Ops, SparseCore 0:
  43.3 45.5 all-gather.4
  101.8 47.4 all-gather.6

commit v6 on v5

--- a/solution.py
+++ b/solution.py
@@ -220,9 +220,8 @@
         near = send(both, lambda x, y, z, c: (x, y, z ^ 1, c))
         inner_a = send(both, inward)
         own1, own2 = ring_near(both, "x")
+        gates = lax.all_gather(jnp.stack([ga, gb]), "dp", axis_index_groups=rings)
         out_mine = jnp.where(c == zhl, out_proj, send(out_proj, swap))
-        ga, gb, own1, own2, out_mine, in_proj, down_weight = hold((ga, gb, own1, own2, out_mine, in_proj, down_weight))
-        gates = lax.all_gather(jnp.stack([ga, gb]), "dp", axis_index_groups=rings)
         near, inner_a, own1, own2, down_weight, out_mine, in_proj, ga = hold(
             (near, inner_a, own1, own2, down_weight, out_mine, in_proj, ga)
         )

time: 220 us -> 208 us (0.945)
  starting transfers between devices: 61.8 us -> 56.4 us
  other arithmetic: 8.43 us -> 4.33 us
    ppermute x31, starting transfers between devices: 61.7 us -> 56.3 us  [send(): return lax.ppermute(v, AXES, perm_of(move))]
    unnamed x63 -> x67, local copies, waits for them, and re-layouts: 5 us -> 3.08 us
  transfers between devices with their start and end apart: 33 -> 33, of which waited for: 13 -> 12; matrix products, arithmetic and copies ran while one was open for 5% -> 3% of each run, Pallas kernels for 6% -> 7%
where the time goes in v6:
time: 208 us
  waiting for transfers between devices  79.3 us (38%)
  starting transfers between devices  56.4 us (27%)
  Pallas kernels  25.6 us (12%)
  blocking collectives  19.2 us (9%)
  between operations  14.1 us (7%)
  local copies, waits for them, and re-layouts  6.87 us (3%)
  other arithmetic  4.33 us (2%)
  matrix products  2.13 us (1%)
    ppermute x31, waiting for transfers between devices, send(): return lax.ppermute(v, AXES, perm_of(move))  79.2 us
    ppermute x31, starting transfers between devices, send(): return lax.ppermute(v, AXES, perm_of(move))  56.3 us
    pallas_call x3, Pallas kernels, call(): pl.pallas_call(kernel, out_shape=[jax.ShapeDtypeStruct(shape, F32)] * 2,...  25.6 us
    all_to_all x1, blocking collectives, shards(): bands = lax.all_to_all(part.reshape(16, 256), 'mp', 0, 0, tiled=True)  10.9 us
    all_to_all x1, blocking collectives, everyone(): lax.all_to_all(jnp.broadcast_to(v[None], (16,) + v.shape), axis, 0, 0, ti...  8.32 us
  transfers between devices with their start and end apart: 33, of which 12 were waited for; matrix products, arithmetic and copies ran while one was open for 3% of the time, Pallas kernels for 7%

profile of v6, /device:TPU:1, one launch (start us, length us, event | category | flops | bytes accessed | tf_op | source)
XLA Modules:
  0.0 207.9 jit_solution(18233071937094840805)
XLA Ops:
  6.5 4.5 %collective-permute-start.5 = (bf16[256,896]{1,0:T(8,128)(2,1)}, bf16[256,896]{1,0:T(8,128)(2,1)S(1)}, u32[]{:S(2)}, u32[]{:S(2)}) collective-permute-start(bf16[256,896]{1,0:T(8,128)(2,1)} %param.12), channel_id=1, source_target_pairs={{0,32},{1,16},{2,34},{3,18},{4,36},{5,20},{6,38},{7,22},{8,40},{9,... | collective-permute-start | bytes 1376264 | tf_op jit(solution)/shard_map/first_moves/ppermute | solution.py:31
  11.0 5.1 %collective-permute-start.23 = (bf16[256,896]{1,0:T(8,128)(2,1)}, bf16[256,896]{1,0:T(8,128)(2,1)S(1)}, u32[]{:S(2)}, u32[]{:S(2)}) collective-permute-start(bf16[256,896]{1,0:T(8,128)(2,1)} %param.12), channel_id=1, source_target_pairs={{0,0},{1,48},{2,2},{3,50},{4,4},{5,52},{6,6},{7,54},{8,8},{9,56},{... | collective-permute-start | bytes 1376264 | tf_op jit(solution)/shard_map/first_moves/ppermute | solution.py:31
  16.1 15.4 %collective-permute-done.5 = bf16[256,896]{1,0:T(8,128)(2,1)S(1)} collective-permute-done((bf16[256,896]{1,0:T(8,128)(2,1)}, bf16[256,896]{1,0:T(8,128)(2,1)S(1)}, u32[]{:S(2)}, u32[]{:S(2)}) %collective-permute-start.5) | collective-permute-done | bytes 458784 | tf_op jit(solution)/shard_map/first_moves/ppermute | solution.py:31
  31.5 4.9 %collective-permute-done.23 = bf16[256,896]{1,0:T(8,128)(2,1)S(1)} collective-permute-done((bf16[256,896]{1,0:T(8,128)(2,1)}, bf16[256,896]{1,0:T(8,128)(2,1)S(1)}, u32[]{:S(2)}, u32[]{:S(2)}) %collective-permute-start.23) | collective-permute-done | bytes 458784 | tf_op jit(solution)/shard_map/first_moves/ppermute | solution.py:31
  36.5 1.1 pad_maximum_fusion.1
  37.7 0.8 collective-permute-start
  38.5 1.5 collective-permute-start.1
  40.0 1.2 collective-permute-start.2
  41.2 1.5 collective-permute-start.3
  43.2 1.2 pad.8.refs_11_
  44.6 0.7 broadcast_select_fusion.2
  45.3 3.3 %collective-permute-done.refs_5_ = bf16[1024,256]{1,0:T(8,128)(2,1)} collective-permute-done((bf16[1024,256]{1,0:T(8,128)(2,1)S(1)}, bf16[1024,256]{1,0:T(8,128)(2,1)}, u32[]{:S(2)}, u32[]{:S(2)}) %collective-permute-start) | collective-permute-done | bytes 524320 | tf_op jit(solution)/shard_map/first_moves/ppermute | solution.py:31
  48.6 2.7 %collective-permute-done.2.refs_1_ = bf16[1024,256]{1,0:T(8,128)(2,1)S(1)} collective-permute-done((bf16[1024,256]{1,0:T(8,128)(2,1)S(1)}, bf16[1024,256]{1,0:T(8,128)(2,1)S(1)}, u32[]{:S(2)}, u32[]{:S(2)}) %collective-permute-start.2) | collective-permute-done | bytes 524320 | tf_op jit(solution)/shard_map/first_moves/ppermute | solution.py:31
  51.6 4.6 %collective-permute-start.8 = (bf16[960,256]{1,0:T(8,128)(2,1)S(1)}, bf16[960,256]{1,0:T(8,128)(2,1)S(1)}, u32[]{:S(2)}, u32[]{:S(2)}) collective-permute-start(bf16[960,256]{1,0:T(8,128)(2,1)S(1)} %pad_maximum_fusion.3), channel_id=1, source_target_pairs={{0,32},{1,16},{2,34},{3,18},{4,36},{5,20},{6,38},{7,22},{8,40},{9,... | collective-permute-start | bytes 1474568 | tf_op jit(solution)/shard_map/second_moves/ppermute | solution.py:31
  56.2 1.2 collective-permute-start.10
  57.4 1.5 collective-permute-start.11
  58.9 0.7 collective-permute-start.6
  59.6 1.3 collective-permute-start.7
  60.9 16.9 %collective-permute-done.8 = bf16[960,256]{1,0:T(8,128)(2,1)S(1)} collective-permute-done((bf16[960,256]{1,0:T(8,128)(2,1)S(1)}, bf16[960,256]{1,0:T(8,128)(2,1)S(1)}, u32[]{:S(2)}, u32[]{:S(2)}) %collective-permute-start.8) | collective-permute-done | bytes 491552 | tf_op jit(solution)/shard_map/second_moves/ppermute | solution.py:31
  77.7 2.9 %collective-permute-start.9 = (bf16[960,256]{1,0:T(8,128)(2,1)S(1)}, bf16[960,256]{1,0:T(8,128)(2,1)S(1)}, u32[]{:S(2)}, u32[]{:S(2)}) collective-permute-start(bf16[960,256]{1,0:T(8,128)(2,1)S(1)} %pad_maximum_fusion.3), channel_id=1, source_target_pairs={{0,0},{1,48},{2,2},{3,50},{4,4},{5,52},{6,6},{7,54},{8,8},{9,56},{... | collective-permute-start | bytes 1474568 | tf_op jit(solution)/shard_map/second_moves/ppermute | solution.py:31
  80.6 13.7 %collective-permute-done.9 = bf16[960,256]{1,0:T(8,128)(2,1)S(1)} collective-permute-done((bf16[960,256]{1,0:T(8,128)(2,1)S(1)}, bf16[960,256]{1,0:T(8,128)(2,1)S(1)}, u32[]{:S(2)}, u32[]{:S(2)}) %collective-permute-start.9) | collective-permute-done | bytes 491552 | tf_op jit(solution)/shard_map/second_moves/ppermute | solution.py:31
  94.4 1.2 pad_maximum_fusion
  95.7 2.7 %collective-permute-start.18 = (bf16[512,256]{1,0:T(8,128)(2,1)S(1)}, bf16[512,256]{1,0:T(8,128)(2,1)S(1)}, u32[]{:S(2)}, u32[]{:S(2)}) collective-permute-start(bf16[512,256]{1,0:T(8,128)(2,1)S(1)} %slice.54), channel_id=1, source_target_pairs={{0,12},{1,13},{2,14},{3,15},{4,0},{5,1},{6,2},{7,3},{8,4},{9,5},{1... | collective-permute-start | bytes 786440 | tf_op jit(solution)/shard_map/third_moves/ppermute | solution.py:31
  98.6 2.7 %collective-permute-start.14 = (bf16[1024,256]{1,0:T(8,128)(2,1)S(1)}, bf16[1024,256]{1,0:T(8,128)(2,1)S(1)}, u32[]{:S(2)}, u32[]{:S(2)}) collective-permute-start(bf16[1024,256]{1,0:T(8,128)(2,1)S(1)} %broadcast_select_fusion.1.refs_0_.refs_10_), channel_id=1, source_target_pairs={{0,12},{1,13},{2,14},{3,15},{4,0},{5,1},{6,2},{7,3},{8,4},{9,5},{1... | collective-permute-start | bytes 1572872 | tf_op jit(solution)/shard_map/third_moves/ppermute | solution.py:31
  101.3 1.3 collective-permute-start.12
  102.8 2.6 %collective-permute-start.16 = (bf16[512,256]{1,0:T(8,128)(2,1)S(1)}, bf16[512,256]{1,0:T(8,128)(2,1)S(1)}, u32[]{:S(2)}, u32[]{:S(2)}) collective-permute-start(bf16[512,256]{1,0:T(8,128)(2,1)S(1)} %slice.52), channel_id=1, source_target_pairs={{0,12},{1,13},{2,14},{3,15},{4,0},{5,1},{6,2},{7,3},{8,4},{9,5},{1... | collective-permute-start | bytes 786440 | tf_op jit(solution)/shard_map/third_moves/ppermute | solution.py:31
  105.4 6.7 %collective-permute-done.15.refs_8_ = bf16[512,256]{1,0:T(8,128)(2,1)S(1)} collective-permute-done((bf16[512,256]{1,0:T(8,128)(2,1)S(1)}, bf16[512,256]{1,0:T(8,128)(2,1)S(1)}, u32[]{:S(2)}, u32[]{:S(2)}) %collective-permute-start.15) | collective-permute-done | bytes 262176 | tf_op jit(solution)/shard_map/third_moves/ppermute | solution.py:31
  112.3 1.7 collective-permute-start.19
  113.9 1.1 collective-permute-start.20
  115.0 0.7 slice.55
  116.1 0.7 slice.56
  116.9 2.3 %collective-permute-start.22 = (bf16[512,256]{1,0:T(8,128)(2,1)}, bf16[512,256]{1,0:T(8,128)(2,1)}, u32[]{:S(2)}, u32[]{:S(2)}) collective-permute-start(bf16[512,256]{1,0:T(8,128)(2,1)} %slice.56), channel_id=1, source_target_pairs={{0,12},{1,13},{2,14},{3,15},{4,0},{5,1},{6,2},{7,3},{8,4},{9,5},{1... | collective-permute-start | bytes 786440 | tf_op jit(solution)/shard_map/fourth_moves/ppermute | solution.py:31
  119.2 7.2 %fourth_moves.1 = (f32[256,1024]{1,0:T(8,128)}, f32[256,1024]{1,0:T(8,128)}) custom-call(bf16[1024,256]{1,0:T(8,128)(2,1)} %copy-done.4, bf16[1024,256]{1,0:T(8,128)(2,1)} %copy-done.8, bf16[1024,256]{1,0:T(8,128)(2,1)} %copy-done.9, bf16[512,256]{1,0:T(8,128)(2,1)} %copy-done.19, bf16[512,256]{1,0:T(8,128)(2,1)} %copy-done.20, ...), custom_call_target="tpu_custom_call" | custom-call | flops 2147483648 | bytes 8388608 | tf_op jit(solution)/shard_map/fourth_moves/pallas_call | solution.py:164
  126.5 1.5 collective-permute-done.21.refs_3_.refs_13_
  128.3 2.7 %collective-permute-start.26 = (bf16[512,256]{1,0:T(8,128)(2,1)S(1)}, bf16[512,256]{1,0:T(8,128)(2,1)S(1)}, u32[]{:S(2)}, u32[]{:S(2)}) collective-permute-start(bf16[512,256]{1,0:T(8,128)(2,1)S(1)} %slice.59), channel_id=1, source_target_pairs={{0,12},{1,13},{2,14},{3,15},{4,0},{5,1},{6,2},{7,3},{8,4},{9,5},{1... | collective-permute-start | bytes 786440 | tf_op jit(solution)/shard_map/fifth_moves/ppermute | solution.py:31
  131.0 6.0 %collective-permute-done.25.refs_8_.refs_18_ = bf16[512,256]{1,0:T(8,128)(2,1)S(1)} collective-permute-done((bf16[512,256]{1,0:T(8,128)(2,1)S(1)}, bf16[512,256]{1,0:T(8,128)(2,1)S(1)}, u32[]{:S(2)}, u32[]{:S(2)}) %collective-permute-start.25) | collective-permute-done | bytes 262176 | tf_op jit(solution)/shard_map/fifth_moves/ppermute | solution.py:31
  137.1 0.7 copy-done.23
  137.8 1.0 copy-done.1
  138.8 7.2 %fifth_moves.1 = (f32[256,1024]{1,0:T(8,128)}, f32[256,1024]{1,0:T(8,128)}) custom-call(bf16[1024,256]{1,0:T(8,128)(2,1)} %copy-done.5, bf16[1024,256]{1,0:T(8,128)(2,1)} %copy-done.3, bf16[1024,256]{1,0:T(8,128)(2,1)} %copy-done.12, bf16[512,256]{1,0:T(8,128)(2,1)} %collective-permute-done.21.refs_3_.refs_13_, ...), custom_call_target="tpu_custom_call" | custom-call | flops 2147483648 | bytes 8388608 | tf_op jit(solution)/shard_map/fifth_moves/pallas_call | solution.py:164
  146.1 11.1 %hidden.1 = (f32[512,896]{1,0:T(8,128)}, f32[512,896]{1,0:T(8,128)}) custom-call(bf16[1024,256]{1,0:T(8,128)(2,1)} %copy-done.4, bf16[1024,256]{1,0:T(8,128)(2,1)} %copy-done.8, bf16[1024,256]{1,0:T(8,128)(2,1)} %copy-done.9, bf16[512,256]{1,0:T(8,128)(2,1)} %copy-done.19, bf16[512,256]{1,0:T(8,128)(2,1)} %copy-done.20, ...), custom_call_target="tpu_custom_call" | custom-call | flops 3758096384 | bytes 8388608 | tf_op jit(solution)/shard_map/hidden/pallas_call | solution.py:164
  157.2 1.2 collective-permute-start.27
  158.6 1.0 slice.65
  160.2 3.2 %collective-permute-done.29 = f32[32,256]{1,0:T(8,128)S(1)} collective-permute-done((f32[32,256]{1,0:T(8,128)S(1)}, f32[32,256]{1,0:T(8,128)S(1)}, u32[]{:S(2)}, u32[]{:S(2)}) %collective-permute-start.29) | collective-permute-done | bytes 32800 | tf_op jit(solution)/shard_map/hidden/ppermute | solution.py:31
  163.8 0.7 copy-done.28
  165.3 9.9 %collective-permute-start.30 = (f32[96,256]{1,0:T(8,128)S(1)}, f32[96,256]{1,0:T(8,128)S(1)}, u32[]{:S(2)}, u32[]{:S(2)}) collective-permute-start(f32[96,256]{1,0:T(8,128)S(1)} %select_maximum_fusion), channel_id=1, source_target_pairs={{0,16},{1,17},{2,18},{3,19},{4,20},{5,21},{6,22},{7,23},{8,24},{9,... | collective-permute-start | bytes 294920 | tf_op jit(solution)/shard_map/finish/ppermute | solution.py:31
  175.6 4.6 %collective-permute-done.30 = f32[96,256]{1,0:T(8,128)S(1)} collective-permute-done((f32[96,256]{1,0:T(8,128)S(1)}, f32[96,256]{1,0:T(8,128)S(1)}, u32[]{:S(2)}, u32[]{:S(2)}) %collective-permute-start.30) | collective-permute-done | bytes 98336 | tf_op jit(solution)/shard_map/finish/ppermute | solution.py:31
  181.1 10.9 %all_to_all.16 = f32[16,1,256]{2,1,0:T(1,128)S(1)} all-to-all(f32[16,1,256]{2,1,0:T(1,128)S(1)} %all_to_all.13), channel_id=1, replica_groups=mesh['dp'=16,'mp'=16] {'mp'}, dimensions={0} | all-to-all | bytes 32768 | tf_op jit(solution)/shard_map/finish/all_to_all | solution.py:279
  192.2 8.3 %all_to_all.17 = f32[16,1,32]{2,1,0:T(1,128)S(1)} all-to-all(f32[16,1,32]{2,1,0:T(1,128)S(1)} %broadcast_in_dim.2), channel_id=1, replica_groups=mesh['dp'=16,'mp'=16] {'mp'}, dimensions={0} | all-to-all | bytes 4096 | tf_op jit(solution)/shard_map/finish/all_to_all | solution.py:198
  (129 shorter events, 6.4 us)
Async XLA Ops:
  6.5 37.8 %copy-start = (bf16[128,256]{1,0:T(8,128)(2,1)S(1)}, bf16[128,256]{1,0:T(8,128)(2,1)}, u32[]{:S(2)}) copy-start(bf16[128,256]{1,0:T(8,128)(2,1)} %param.18) | copy-start | bytes 196612
  6.5 31.1 %copy-start.26 = (bf16[1,512,256]{2,1,0:T(8,128)(2,1)S(1)}, bf16[1,512,256]{2,1,0:T(8,128)(2,1)}, u32[]{:S(2)}) copy-start(bf16[1,512,256]{2,1,0:T(8,128)(2,1)} %param.10) | copy-start | bytes 786436
  6.5 31.1 %copy-start.25 = (bf16[1,512,256]{2,1,0:T(8,128)(2,1)S(1)}, bf16[1,512,256]{2,1,0:T(8,128)(2,1)}, u32[]{:S(2)}) copy-start(bf16[1,512,256]{2,1,0:T(8,128)(2,1)} %param.11) | copy-start | bytes 786436
  6.5 112.6 %all-gather.5.cloned.1.call-start = ((), (), s32[]{:S(2)}) async-start(), calls=%async_computation.2 | async-start | bytes 4587520 | tf_op jit(solution)/shard_map/first_moves/all_gather | solution.py:223
  6.5 25.0 %collective-permute-start.5 = (bf16[256,896]{1,0:T(8,128)(2,1)}, bf16[256,896]{1,0:T(8,128)(2,1)S(1)}, u32[]{:S(2)}, u32[]{:S(2)}) collective-permute-start(bf16[256,896]{1,0:T(8,128)(2,1)} %param.12), channel_id=1, source_target_pairs={{0,32},{1,16},{2,34},{3,18},{4,36},{5,20},{6,38},{7,22},{8,40},{9,... | collective-permute-start | bytes 1376264 | tf_op jit(solution)/shard_map/first_moves/ppermute | solution.py:31
  11.0 25.5 %collective-permute-start.23 = (bf16[256,896]{1,0:T(8,128)(2,1)}, bf16[256,896]{1,0:T(8,128)(2,1)S(1)}, u32[]{:S(2)}, u32[]{:S(2)}) collective-permute-start(bf16[256,896]{1,0:T(8,128)(2,1)} %param.12), channel_id=1, source_target_pairs={{0,0},{1,48},{2,2},{3,50},{4,4},{5,52},{6,6},{7,54},{8,8},{9,56},{... | collective-permute-start | bytes 1376264 | tf_op jit(solution)/shard_map/first_moves/ppermute | solution.py:31
  37.6 108.5 %all-gather.7.cloned.1.call-start = ((), (), s32[]{:S(2)}) async-start(), calls=%async_computation.3 | async-start | bytes 4915200 | tf_op jit(solution)/shard_map/third_moves/all_gather | solution.py:236
  37.7 10.8 %collective-permute-start = (bf16[1024,256]{1,0:T(8,128)(2,1)S(1)}, bf16[1024,256]{1,0:T(8,128)(2,1)}, u32[]{:S(2)}, u32[]{:S(2)}) collective-permute-start(bf16[1024,256]{1,0:T(8,128)(2,1)S(1)} %pad_maximum_fusion.2.refs_0_), channel_id=1, source_target_pairs={{0,2},{1,3},{2,0},{3,1},{4,6},{5,7},{6,4},{7,5},{8,10},{9,11},{10,... | collective-permute-start | bytes 1572872 | tf_op jit(solution)/shard_map/first_moves/ppermute | solution.py:31
  38.5 10.1 %collective-permute-start.1 = (bf16[1024,256]{1,0:T(8,128)(2,1)S(1)}, bf16[1024,256]{1,0:T(8,128)(2,1)}, u32[]{:S(2)}, u32[]{:S(2)}) collective-permute-start(bf16[1024,256]{1,0:T(8,128)(2,1)S(1)} %pad_maximum_fusion.2.refs_0_), channel_id=1, source_target_pairs={{2,16},{3,17},{6,20},{7,21},{10,24},{11,25},{14,28},{15,29},{16,2}... | collective-permute-start | bytes 1572872 | tf_op jit(solution)/shard_map/first_moves/ppermute | solution.py:31
  40.0 11.3 %collective-permute-start.2 = (bf16[1024,256]{1,0:T(8,128)(2,1)S(1)}, bf16[1024,256]{1,0:T(8,128)(2,1)S(1)}, u32[]{:S(2)}, u32[]{:S(2)}) collective-permute-start(bf16[1024,256]{1,0:T(8,128)(2,1)S(1)} %pad_maximum_fusion.2.refs_0_), channel_id=1, source_target_pairs={{0,4},{1,5},{2,6},{3,7},{4,8},{5,9},{6,10},{7,11},{8,12},{9,13},{1... | collective-permute-start | bytes 1572872 | tf_op jit(solution)/shard_map/first_moves/ppermute | solution.py:31
  41.2 10.4 %collective-permute-start.3 = (bf16[1024,256]{1,0:T(8,128)(2,1)S(1)}, bf16[1024,256]{1,0:T(8,128)(2,1)S(1)}, u32[]{:S(2)}, u32[]{:S(2)}) collective-permute-start(bf16[1024,256]{1,0:T(8,128)(2,1)S(1)} %pad_maximum_fusion.2.refs_0_), channel_id=1, source_target_pairs={{0,12},{1,13},{2,14},{3,15},{4,0},{5,1},{6,2},{7,3},{8,4},{9,5},{1... | collective-permute-start | bytes 1572872 | tf_op jit(solution)/shard_map/first_moves/ppermute | solution.py:31
  42.6 1.9 collective-permute-start.4
  51.3 44.4 %copy-start.8 = (bf16[1024,256]{1,0:T(8,128)(2,1)}, bf16[1024,256]{1,0:T(8,128)(2,1)S(1)}, u32[]{:S(2)}) copy-start(bf16[1024,256]{1,0:T(8,128)(2,1)S(1)} %collective-permute-done.2.refs_1_) | copy-start | bytes 1572868
  51.6 44.2 %copy-start.9 = (bf16[1024,256]{1,0:T(8,128)(2,1)}, bf16[1024,256]{1,0:T(8,128)(2,1)S(1)}, u32[]{:S(2)}) copy-start(bf16[1024,256]{1,0:T(8,128)(2,1)S(1)} %collective-permute-done.3.refs_2_) | copy-start | bytes 1572868
  51.6 26.1 %collective-permute-start.8 = (bf16[960,256]{1,0:T(8,128)(2,1)S(1)}, bf16[960,256]{1,0:T(8,128)(2,1)S(1)}, u32[]{:S(2)}, u32[]{:S(2)}) collective-permute-start(bf16[960,256]{1,0:T(8,128)(2,1)S(1)} %pad_maximum_fusion.3), channel_id=1, source_target_pairs={{0,32},{1,16},{2,34},{3,18},{4,36},{5,20},{6,38},{7,22},{8,40},{9,... | collective-permute-start | bytes 1474568 | tf_op jit(solution)/shard_map/second_moves/ppermute | solution.py:31
  56.2 38.1 %collective-permute-start.10 = (bf16[1024,256]{1,0:T(8,128)(2,1)}, bf16[1024,256]{1,0:T(8,128)(2,1)S(1)}, u32[]{:S(2)}, u32[]{:S(2)}) collective-permute-start(bf16[1024,256]{1,0:T(8,128)(2,1)} %collective-permute-done.refs_5_), channel_id=1, source_target_pairs={{0,4},{1,5},{2,6},{3,7},{4,8},{5,9},{6,10},{7,11},{8,12},{9,13},{1... | collective-permute-start | bytes 1572872 | tf_op jit(solution)/shard_map/second_moves/ppermute | solution.py:31
  57.4 36.9 %collective-permute-start.11 = (bf16[1024,256]{1,0:T(8,128)(2,1)}, bf16[1024,256]{1,0:T(8,128)(2,1)S(1)}, u32[]{:S(2)}, u32[]{:S(2)}) collective-permute-start(bf16[1024,256]{1,0:T(8,128)(2,1)} %collective-permute-done.refs_5_), channel_id=1, source_target_pairs={{0,12},{1,13},{2,14},{3,15},{4,0},{5,1},{6,2},{7,3},{8,4},{9,5},{1... | collective-permute-start | bytes 1572872 | tf_op jit(solution)/shard_map/second_moves/ppermute | solution.py:31
  58.9 35.5 %collective-permute-start.6 = (bf16[1024,256]{1,0:T(8,128)(2,1)}, bf16[1024,256]{1,0:T(8,128)(2,1)S(1)}, u32[]{:S(2)}, u32[]{:S(2)}) collective-permute-start(bf16[1024,256]{1,0:T(8,128)(2,1)} %collective-permute-done.refs_5_), channel_id=1, source_target_pairs={{2,16},{3,17},{6,20},{7,21},{10,24},{11,25},{14,28},{15,29},{16,2}... | collective-permute-start | bytes 1572872 | tf_op jit(solution)/shard_map/second_moves/ppermute | solution.py:31
  59.6 34.8 %collective-permute-start.7 = (bf16[1024,256]{1,0:T(8,128)(2,1)}, bf16[1024,256]{1,0:T(8,128)(2,1)S(1)}, u32[]{:S(2)}, u32[]{:S(2)}) collective-permute-start(bf16[1024,256]{1,0:T(8,128)(2,1)} %collective-permute-done.1), channel_id=1, source_target_pairs={{2,0},{3,1},{6,4},{7,5},{10,8},{11,9},{14,12},{15,13},{16,18},{17,... | collective-permute-start | bytes 1572872 | tf_op jit(solution)/shard_map/second_moves/ppermute | solution.py:31
  77.7 16.6 %collective-permute-start.9 = (bf16[960,256]{1,0:T(8,128)(2,1)S(1)}, bf16[960,256]{1,0:T(8,128)(2,1)S(1)}, u32[]{:S(2)}, u32[]{:S(2)}) collective-permute-start(bf16[960,256]{1,0:T(8,128)(2,1)S(1)} %pad_maximum_fusion.3), channel_id=1, source_target_pairs={{0,0},{1,48},{2,2},{3,50},{4,4},{5,52},{6,6},{7,54},{8,8},{9,56},{... | collective-permute-start | bytes 1474568 | tf_op jit(solution)/shard_map/second_moves/ppermute | solution.py:31
  95.6 7.1 %collective-permute-start.17 = (bf16[512,256]{1,0:T(8,128)(2,1)S(1)}, bf16[512,256]{1,0:T(8,128)(2,1)S(1)}, u32[]{:S(2)}, u32[]{:S(2)}) collective-permute-start(bf16[512,256]{1,0:T(8,128)(2,1)S(1)} %slice.53), channel_id=1, source_target_pairs={{0,4},{1,5},{2,6},{3,7},{4,8},{5,9},{6,10},{7,11},{8,12},{9,13},{1... | collective-permute-start | bytes 786440 | tf_op jit(solution)/shard_map/third_moves/ppermute | solution.py:31
  95.7 7.0 %collective-permute-start.18 = (bf16[512,256]{1,0:T(8,128)(2,1)S(1)}, bf16[512,256]{1,0:T(8,128)(2,1)S(1)}, u32[]{:S(2)}, u32[]{:S(2)}) collective-permute-start(bf16[512,256]{1,0:T(8,128)(2,1)S(1)} %slice.54), channel_id=1, source_target_pairs={{0,12},{1,13},{2,14},{3,15},{4,0},{5,1},{6,2},{7,3},{8,4},{9,5},{1... | collective-permute-start | bytes 786440 | tf_op jit(solution)/shard_map/third_moves/ppermute | solution.py:31
  98.5 18.3 %copy-start.5 = (bf16[1024,256]{1,0:T(8,128)(2,1)}, bf16[1024,256]{1,0:T(8,128)(2,1)S(1)}, u32[]{:S(2)}) copy-start(bf16[1024,256]{1,0:T(8,128)(2,1)S(1)} %broadcast_select_fusion.1.refs_0_.refs_10_) | copy-start | bytes 1572868
  98.5 13.6 %collective-permute-start.13 = (bf16[1024,256]{1,0:T(8,128)(2,1)S(1)}, bf16[1024,256]{1,0:T(8,128)(2,1)S(1)}, u32[]{:S(2)}, u32[]{:S(2)}) collective-permute-start(bf16[1024,256]{1,0:T(8,128)(2,1)S(1)} %broadcast_select_fusion.1.refs_0_.refs_10_), channel_id=1, source_target_pairs={{0,4},{1,5},{2,6},{3,7},{4,8},{5,9},{6,10},{7,11},{8,12},{9,13},{1... | collective-permute-start | bytes 1572872 | tf_op jit(solution)/shard_map/third_moves/ppermute | solution.py:31
  98.6 13.5 %collective-permute-start.14 = (bf16[1024,256]{1,0:T(8,128)(2,1)S(1)}, bf16[1024,256]{1,0:T(8,128)(2,1)S(1)}, u32[]{:S(2)}, u32[]{:S(2)}) collective-permute-start(bf16[1024,256]{1,0:T(8,128)(2,1)S(1)} %broadcast_select_fusion.1.refs_0_.refs_10_), channel_id=1, source_target_pairs={{0,12},{1,13},{2,14},{3,15},{4,0},{5,1},{6,2},{7,3},{8,4},{9,5},{1... | collective-permute-start | bytes 1572872 | tf_op jit(solution)/shard_map/third_moves/ppermute | solution.py:31
  101.3 10.9 %collective-permute-start.12 = (bf16[1024,256]{1,0:T(8,128)(2,1)S(1)}, bf16[1024,256]{1,0:T(8,128)(2,1)S(1)}, u32[]{:S(2)}, u32[]{:S(2)}) collective-permute-start(bf16[1024,256]{1,0:T(8,128)(2,1)S(1)} %collective-permute-done.6), channel_id=1, source_target_pairs={{2,0},{3,1},{6,4},{7,5},{10,8},{11,9},{14,12},{15,13},{16,18},{17,... | collective-permute-start | bytes 1572872 | tf_op jit(solution)/shard_map/third_moves/ppermute | solution.py:31
  102.7 16.5 %copy-start.19 = (bf16[512,256]{1,0:T(8,128)(2,1)}, bf16[512,256]{1,0:T(8,128)(2,1)S(1)}, u32[]{:S(2)}) copy-start(bf16[512,256]{1,0:T(8,128)(2,1)S(1)} %collective-permute-done.17.refs_3_) | copy-start | bytes 786436
  102.7 9.5 %collective-permute-start.15 = (bf16[512,256]{1,0:T(8,128)(2,1)S(1)}, bf16[512,256]{1,0:T(8,128)(2,1)S(1)}, u32[]{:S(2)}, u32[]{:S(2)}) collective-permute-start(bf16[512,256]{1,0:T(8,128)(2,1)S(1)} %slice.51), channel_id=1, source_target_pairs={{0,4},{1,5},{2,6},{3,7},{4,8},{5,9},{6,10},{7,11},{8,12},{9,13},{1... | collective-permute-start | bytes 786440 | tf_op jit(solution)/shard_map/third_moves/ppermute | solution.py:31
  102.8 9.5 %copy-start.20 = (bf16[512,256]{1,0:T(8,128)(2,1)}, bf16[512,256]{1,0:T(8,128)(2,1)S(1)}, u32[]{:S(2)}) copy-start(bf16[512,256]{1,0:T(8,128)(2,1)S(1)} %collective-permute-done.18.refs_4_) | copy-start | bytes 786436
  102.8 9.4 %collective-permute-start.16 = (bf16[512,256]{1,0:T(8,128)(2,1)S(1)}, bf16[512,256]{1,0:T(8,128)(2,1)S(1)}, u32[]{:S(2)}, u32[]{:S(2)}) collective-permute-start(bf16[512,256]{1,0:T(8,128)(2,1)S(1)} %slice.52), channel_id=1, source_target_pairs={{0,12},{1,13},{2,14},{3,15},{4,0},{5,1},{6,2},{7,3},{8,4},{9,5},{1... | collective-permute-start | bytes 786440 | tf_op jit(solution)/shard_map/third_moves/ppermute | solution.py:31
  112.2 14.3 %copy-start.12 = (bf16[1024,256]{1,0:T(8,128)(2,1)}, bf16[1024,256]{1,0:T(8,128)(2,1)S(1)}, u32[]{:S(2)}) copy-start(bf16[1024,256]{1,0:T(8,128)(2,1)S(1)} %collective-permute-done.14.refs_2_.refs_12_) | copy-start | bytes 1572868
  112.3 14.2 %copy-start.6 = (bf16[1024,256]{1,0:T(8,128)(2,1)}, bf16[1024,256]{1,0:T(8,128)(2,1)S(1)}, u32[]{:S(2)}) copy-start(bf16[1024,256]{1,0:T(8,128)(2,1)S(1)} %broadcast_select_fusion.refs_5_.refs_15_) | copy-start | bytes 1572868
  112.3 15.6 %collective-permute-start.19 = (bf16[1024,256]{1,0:T(8,128)(2,1)S(1)}, bf16[1024,256]{1,0:T(8,128)(2,1)S(1)}, u32[]{:S(2)}, u32[]{:S(2)}) collective-permute-start(bf16[1024,256]{1,0:T(8,128)(2,1)S(1)} %broadcast_select_fusion.refs_5_.refs_15_), channel_id=1, source_target_pairs={{0,4},{1,5},{2,6},{3,7},{4,8},{5,9},{6,10},{7,11},{8,12},{9,13},{1... | collective-permute-start | bytes 1572872 | tf_op jit(solution)/shard_map/fourth_moves/ppermute | solution.py:31
  113.9 14.0 %collective-permute-start.20 = (bf16[1024,256]{1,0:T(8,128)(2,1)S(1)}, bf16[1024,256]{1,0:T(8,128)(2,1)S(1)}, u32[]{:S(2)}, u32[]{:S(2)}) collective-permute-start(bf16[1024,256]{1,0:T(8,128)(2,1)S(1)} %broadcast_select_fusion.refs_5_.refs_15_), channel_id=1, source_target_pairs={{0,12},{1,13},{2,14},{3,15},{4,0},{5,1},{6,2},{7,3},{8,4},{9,5},{1... | collective-permute-start | bytes 1572872 | tf_op jit(solution)/shard_map/fourth_moves/ppermute | solution.py:31
  115.8 12.2 %collective-permute-start.21 = (bf16[512,256]{1,0:T(8,128)(2,1)}, bf16[512,256]{1,0:T(8,128)(2,1)}, u32[]{:S(2)}, u32[]{:S(2)}) collective-permute-start(bf16[512,256]{1,0:T(8,128)(2,1)} %slice.55), channel_id=1, source_target_pairs={{0,4},{1,5},{2,6},{3,7},{4,8},{5,9},{6,10},{7,11},{8,12},{9,13},{1... | collective-permute-start | bytes 786440 | tf_op jit(solution)/shard_map/fourth_moves/ppermute | solution.py:31
  116.9 11.1 %collective-permute-start.22 = (bf16[512,256]{1,0:T(8,128)(2,1)}, bf16[512,256]{1,0:T(8,128)(2,1)}, u32[]{:S(2)}, u32[]{:S(2)}) collective-permute-start(bf16[512,256]{1,0:T(8,128)(2,1)} %slice.56), channel_id=1, source_target_pairs={{0,12},{1,13},{2,14},{3,15},{4,0},{5,1},{6,2},{7,3},{8,4},{9,5},{1... | collective-permute-start | bytes 786440 | tf_op jit(solution)/shard_map/fourth_moves/ppermute | solution.py:31
  128.0 9.1 %collective-permute-start.24 = (f32[256,1024]{1,0:T(8,128)}, f32[256,1024]{1,0:T(8,128)S(1)}, u32[]{:S(2)}, u32[]{:S(2)}) collective-permute-start(f32[256,1024]{1,0:T(8,128)} %get-tuple-element.58), channel_id=1, source_target_pairs={{0,1},{1,0},{2,3},{3,2},{4,5},{5,4},{6,7},{7,6},{8,9},{9,8},{10,11... | collective-permute-start | bytes 3145736 | tf_op jit(solution)/shard_map/fifth_moves/ppermute | solution.py:31
  128.1 9.0 %collective-permute-start.25 = (bf16[512,256]{1,0:T(8,128)(2,1)S(1)}, bf16[512,256]{1,0:T(8,128)(2,1)S(1)}, u32[]{:S(2)}, u32[]{:S(2)}) collective-permute-start(bf16[512,256]{1,0:T(8,128)(2,1)S(1)} %slice.58), channel_id=1, source_target_pairs={{0,4},{1,5},{2,6},{3,7},{4,8},{5,9},{6,10},{7,11},{8,12},{9,13},{1... | collective-permute-start | bytes 786440 | tf_op jit(solution)/shard_map/fifth_moves/ppermute | solution.py:31
  128.3 8.7 %collective-permute-start.26 = (bf16[512,256]{1,0:T(8,128)(2,1)S(1)}, bf16[512,256]{1,0:T(8,128)(2,1)S(1)}, u32[]{:S(2)}, u32[]{:S(2)}) collective-permute-start(bf16[512,256]{1,0:T(8,128)(2,1)S(1)} %slice.59), channel_id=1, source_target_pairs={{0,12},{1,13},{2,14},{3,15},{4,0},{5,1},{6,2},{7,3},{8,4},{9,5},{1... | collective-permute-start | bytes 786440 | tf_op jit(solution)/shard_map/fifth_moves/ppermute | solution.py:31
  146.1 12.4 %copy-start.32 = (f32[256,1024]{1,0:T(8,128)S(1)}, f32[256,1024]{1,0:T(8,128)}, u32[]{:S(2)}) copy-start(f32[256,1024]{1,0:T(8,128)} %get-tuple-element.65.refs_21_) | copy-start | bytes 3145732
  146.1 14.0 %copy-start.2 = (f32[256,1024]{1,0:T(8,128)S(1)}, f32[256,1024]{1,0:T(8,128)}, u32[]{:S(2)}) copy-start(f32[256,1024]{1,0:T(8,128)} %copy-done.1) | copy-start | bytes 3145732
  146.1 14.0 %copy-start.15 = (f32[256,1024]{1,0:T(8,128)S(1)}, f32[256,1024]{1,0:T(8,128)}, u32[]{:S(2)}) copy-start(f32[256,1024]{1,0:T(8,128)} %get-tuple-element.57) | copy-start | bytes 3145732
  157.2 6.4 %collective-permute-start.27 = (f32[512,896]{1,0:T(8,128)}, f32[512,896]{1,0:T(8,128)S(1)}, u32[]{:S(2)}, u32[]{:S(2)}) collective-permute-start(f32[512,896]{1,0:T(8,128)} %get-tuple-element.67), channel_id=1, source_target_pairs={{0,1},{1,0},{2,3},{3,2},{4,5},{5,4},{6,7},{7,6},{8,9},{9,8},{10,11... | collective-permute-start | bytes 5505032 | tf_op jit(solution)/shard_map/hidden/ppermute | solution.py:31
  158.4 5.0 %collective-permute-start.28 = (f32[256,1024]{1,0:T(8,128)S(1)}, f32[256,1024]{1,0:T(8,128)S(1)}, u32[]{:S(2)}, u32[]{:S(2)}) collective-permute-start(f32[256,1024]{1,0:T(8,128)S(1)} %copy-done.32), channel_id=1, source_target_pairs={{0,1},{1,0},{2,3},{3,2},{4,5},{5,4},{6,7},{7,6},{8,9},{9,8},{10,11... | collective-permute-start | bytes 3145736 | tf_op jit(solution)/shard_map/hidden/ppermute | solution.py:31
  159.6 3.8 %collective-permute-start.29 = (f32[32,256]{1,0:T(8,128)S(1)}, f32[32,256]{1,0:T(8,128)S(1)}, u32[]{:S(2)}, u32[]{:S(2)}) collective-permute-start(f32[32,256]{1,0:T(8,128)S(1)} %convert_reduce_fusion), channel_id=1, source_target_pairs={{0,1},{1,0},{2,3},{3,2},{4,5},{5,4},{6,7},{7,6},{8,9},{9,8},{10,11... | collective-permute-start | bytes 98312 | tf_op jit(solution)/shard_map/hidden/ppermute | solution.py:31
  165.3 15.2 %copy-start.29 = (f32[64,64]{1,0:T(8,128)S(1)}, f32[64,64]{1,0:T(8,128)}, u32[]{:S(2)}) copy-start(f32[64,64]{1,0:T(8,128)} %param.16) | copy-start | bytes 49156
  165.3 15.5 %copy-start.30 = (f32[64,64]{1,0:T(8,128)S(1)}, f32[64,64]{1,0:T(8,128)}, u32[]{:S(2)}) copy-start(f32[64,64]{1,0:T(8,128)} %param.17) | copy-start | bytes 49156
  165.3 14.8 %collective-permute-start.30 = (f32[96,256]{1,0:T(8,128)S(1)}, f32[96,256]{1,0:T(8,128)S(1)}, u32[]{:S(2)}, u32[]{:S(2)}) collective-permute-start(f32[96,256]{1,0:T(8,128)S(1)} %select_maximum_fusion), channel_id=1, source_target_pairs={{0,16},{1,17},{2,18},{3,19},{4,20},{5,21},{6,22},{7,23},{8,24},{9,... | collective-permute-start | bytes 294920 | tf_op jit(solution)/shard_map/finish/ppermute | solution.py:31
  (18 other events, 88.6 us)
Sparse Core Ops, SparseCore 0:
  37.7 46.8 all-gather.4
  95.7 47.9 all-gather.6
